TPU v7x, 256 devices: a whole 4x4x8 slice. The times are simulated.
256 devices in a mesh: gx: 8 (over y, core), gy: 4 (over z_lo), gz: 8 (over x, z_hi).
Axes of the slice: x: 4, y: 4, z: 8 (z_hi: 2, z_lo: 4; z = z_hi * 4 + z_lo), core: 2. Of those that a mesh axis runs over, the one named last changes fastest.
Arguments:
- stiffness: float32 [64, 48, 1024], P('gx', 'gy', 'gz'), may hold values from 0.5 to 5
- density: float32 [64, 48, 1024], P('gx', 'gy', 'gz'), may hold values from 1 to 4
- load: float32 [3, 64, 48, 1024], P(None, 'gx', 'gy', 'gz'), may hold values from -6 to 6
- alive: int32 [4, 64, 48, 1024], P(None, 'gx', 'gy', 'gz'), may hold values 0 or 1
- surf_coords: float32 [4096, 3, 128], P(('gx', 'gy', 'gz')), may hold values from 0 to 1
- surf_nodes: int32 [4096, 128], P(('gx', 'gy', 'gz')), may hold values from 0 to 12287
- routes: int32 [4, 4096], P(None, ('gx', 'gy', 'gz')), may hold values from 0 to 7, as said below
- pairs: int32 [4, 256, 64, 2], P(None, ('gx', 'gy', 'gz')), may hold values from 0 to 31, as said below
Outputs:
- element_velocity: float32 [3, 64, 48, 1024], P(None, 'gx', 'gy', 'gz')
- element_stress: float32 [6, 64, 48, 1024], P(None, 'gx', 'gy', 'gz')
Inputs may be any that keep to these rules, and one draw needn't show every extreme that they name: `routes`: in every step a device sends at most 4 of its blocks to one box, and all devices of a gz column send exactly 4 blocks to one common box of that column. `pairs`: every slot named is live at that box and step whenever the box holds a block at all.
All inputs are finite; a program needn't handle non-finite values. No bound on the sum of `alive` on one device may be relied on, other than what follows from the above.
Results may differ from a plain program's by a relative error of at most 0.0003.
Values sent between devices are 32-bit elements; how exact they have to be, the bound alone decides.
No kernel may reach another device: no remote copies, remote signals or barrier semaphores. Data moves between devices by JAX's collectives and lax.ppermute only.
A program may use at most 64 MiB of HBM per device.

v0:
```python
import functools
import math
import jax
import jax.numpy as jnp
from jax import lax
from jax.experimental import pallas as pl
from jax.experimental.pallas import tpu as pltpu
from jax.sharding import PartitionSpec as P

F32 = jnp.float32
BF16 = jnp.bfloat16
SCALE = math.sqrt(math.log2(math.e) / 0.08)
TIME_STEP = 0.2
PARAMS = pltpu.CompilerParams(vmem_limit_bytes=48 * 2**20)


def split2(x):
    hi = x.astype(BF16)
    return hi, (x - hi.astype(F32)).astype(BF16)


def iota(shape, dim):
    return lax.broadcasted_iota(jnp.int32, shape, dim)


def plan_kernel(me_ref, all_ref, list_ref, *, around):
    me = me_ref[0]
    lane = iota((1, 128), 1)
    block_of = iota((128, 128), 0).astype(F32)
    eye = iota((128, 128), 0) == iota((128, 128), 1)
    upper = (iota((128, 128), 0) < iota((128, 128), 1)).astype(BF16)
    place = iota((512, 128), 0).astype(F32)
    for step in range(4):
        keys = all_ref[0, 48 + step : 49 + step, :]
        for src in range(1, 8):
            keys = keys + all_ref[src, 48 + step : 49 + step, :]
        key_col = jnp.sum(jnp.where(eye, keys, 0.0), axis=1, keepdims=True)
        base = jnp.zeros((1, 1), F32)
        total = jnp.zeros((8, 512), F32)
        for row in range(4):
            even = all_ref[2 * row, 52 + step : 53 + step, :]
            odd = all_ref[2 * row + 1, 52 + step : 53 + step, :]
            low = lane < 64
            first = jnp.where(low, even, pltpu.roll(odd, 64, 1))
            second = jnp.where(low, pltpu.roll(even, 64, 1), odd)
            box = jnp.where(low, 64.0 * row, 64.0 * row + 32.0)
            hit_first = key_col == first + box
            hit_second = key_col == second + box
            p_block = jnp.sum(jnp.where(hit_first, block_of, 0.0), axis=0, keepdims=True)
            r_block = jnp.sum(jnp.where(hit_second, block_of, 0.0), axis=0, keepdims=True)
            live = jnp.sum(jnp.where(hit_first, 1.0, 0.0), axis=0, keepdims=True) * jnp.sum(
                jnp.where(hit_second, 1.0, 0.0), axis=0, keepdims=True
            )
            p_local = p_block - (16 * me - 16).astype(F32)
            mine = (p_local >= 16.0) & (p_local < 32.0) & (live > 0.0)
            sel = jnp.where(mine, 1.0, 0.0)
            before = jnp.dot(
                jnp.broadcast_to(sel, (8, 128)).astype(BF16), upper, preferred_element_type=F32
            )[0:1]
            spot = jnp.where(mine, before + base, -1.0)
            base = base + jnp.sum(sel, axis=1, keepdims=True)
            onehot = jnp.where(place == spot, 1.0, 0.0).astype(BF16)
            codes = jnp.where(
                iota((8, 128), 0) == 0,
                jnp.broadcast_to(p_local, (8, 128)),
                jnp.broadcast_to(r_block, (8, 128)),
            )
            codes = jnp.where(jnp.broadcast_to(mine, (8, 128)), codes, 0.0).astype(BF16)
            total = total + lax.dot_general(
                codes, onehot, (((1,), (1,)), ((), ())), preferred_element_type=F32
            )
        list_ref[step : step + 1, :] = (total[0:1] * 128.0 + total[1:2]).astype(jnp.int32)
        list_ref[4 + step : 5 + step, :] = jnp.broadcast_to(base, (1, 512)).astype(jnp.int32)


def one_hots(nodes_ref, rows_ref, lanes_ref):
    for s in range(16):
        ids = nodes_ref[s : s + 1, :]
        at = slice(128 * s, 128 * s + 128)
        rows_ref[:, at] = jnp.where(iota((96, 128), 0) == ids // 128, 1.0, 0.0).astype(BF16)
        lanes_ref[:, at] = jnp.where(iota((128, 128), 0) == ids % 128, 1.0, 0.0).astype(BF16)


def pair_loop(list_ref, step, first_row, all_ref, base, force_ref):
    def body(q, carry):
        code = list_ref[step, q]
        p_local = code // 128
        r_block = code % 128
        p_block = p_local + base
        r_src, r_row = r_block // 16, first_row + (r_block % 16) * 3
        p_src, p_row = p_block // 16, first_row + (p_block % 16) * 3
        xi, xj = [], []
        for c in range(3):
            xi.append(jnp.broadcast_to(all_ref[p_src, pl.ds(p_row + c, 1), :] * SCALE, (8, 128)))
            wide = jnp.broadcast_to(all_ref[r_src, pl.ds(r_row + c, 1), :] * SCALE, (8, 128))
            xj.append(pltpu.roll(wide, 0, 1, stride=1, stride_axis=0))
        acc = [jnp.zeros((8, 128), F32)] * 3
        for k in range(16):
            diff = [xi[c] - (pltpu.roll(xj[c], 8 * k, 1) if k else xj[c]) for c in range(3)]
            dist = diff[0] * diff[0] + diff[1] * diff[1] + diff[2] * diff[2]
            w = jnp.exp2(-dist)
            acc = [acc[c] + w * diff[c] for c in range(3)]
        for c in range(3):
            force_ref[p_local - 16, c] += acc[c]
        return carry

    lax.fori_loop(0, list_ref[4 + step, 0], body, 0)


def scatter(force_ref, rows_ref, lanes_ref, lhs_ref):
    for s in range(16):
        at = slice(128 * s, 128 * s + 128)
        hot = rows_ref[:, at].astype(F32)
        for c in range(3):
            f = jnp.sum(force_ref[s, c], axis=0, keepdims=True) * (1.0 / SCALE)
            hi, lo = split2(f)
            lhs_ref[96 * c : 96 * c + 96, at] = (hot * hi.astype(F32)).astype(BF16)
            lhs_ref[288 + 96 * c : 384 + 96 * c, at] = (hot * lo.astype(F32)).astype(BF16)
    out = lax.dot_general(
        lhs_ref[...], lanes_ref[...], (((1,), (1,)), ((), ())), preferred_element_type=F32
    )
    return out[:288] + out[288:]


def contact_kernel(list_ref, me_ref, all_ref, nodes_ref, *rest, steps, first_rows):
    outs = rest[: len(steps)]
    rows_ref, lanes_ref, lhs_ref, force_ref = rest[len(steps) :]
    one_hots(nodes_ref, rows_ref, lanes_ref)
    base = 16 * me_ref[0] - 16
    for step, first_row, out_ref in zip(steps, first_rows, outs):
        force_ref[...] = jnp.zeros_like(force_ref)
        pair_loop(list_ref, step, first_row, all_ref, base, force_ref)
        out_ref[...] = scatter(force_ref, rows_ref, lanes_ref, lhs_ref)


def contact(lists, me, everyone, nodes, steps, first_rows):
    return pl.pallas_call(
        functools.partial(contact_kernel, steps=steps, first_rows=first_rows),
        out_shape=[jax.ShapeDtypeStruct((288, 128), F32) for _ in steps],
        in_specs=[
            pl.BlockSpec(memory_space=pltpu.SMEM),
            pl.BlockSpec(memory_space=pltpu.SMEM),
            pl.BlockSpec(memory_space=pltpu.VMEM),
            pl.BlockSpec(memory_space=pltpu.VMEM),
        ],
        out_specs=[pl.BlockSpec(memory_space=pltpu.VMEM) for _ in steps],
        scratch_shapes=[
            pltpu.VMEM((96, 2048), BF16),
            pltpu.VMEM((128, 2048), BF16),
            pltpu.VMEM((576, 2048), BF16),
            pltpu.VMEM((16, 3, 8, 128), F32),
        ],
        compiler_params=PARAMS,
    )(lists, me, everyone, nodes)


def gather_kernel(disp_ref, coords_ref, nodes_ref, out_ref, rows_ref, lanes_ref):
    one_hots(nodes_ref, rows_ref, lanes_ref)
    hot = jnp.concatenate([rows_ref[...], rows_ref[...]], axis=0)
    for c in range(3):
        field = jnp.concatenate(list(split2(disp_ref[96 * c : 96 * c + 96, :])), axis=0)
        picked = lax.dot_general(field, hot, (((0,), (0,)), ((), ())), preferred_element_type=F32)
        value = jnp.sum(picked * lanes_ref[...].astype(F32), axis=0, keepdims=True)
        for s in range(16):
            row = value[:, 128 * s : 128 * s + 128] + coords_ref[3 * s + c : 3 * s + c + 1, :]
            for dest in range(8):
                out_ref[dest, 3 * s + c : 3 * s + c + 1, :] = row


def gather_positions(disp, coords, nodes):
    return pl.pallas_call(
        gather_kernel,
        out_shape=jax.ShapeDtypeStruct((8, 48, 128), F32),
        scratch_shapes=[pltpu.VMEM((96, 2048), BF16), pltpu.VMEM((128, 2048), BF16)],
        compiler_params=PARAMS,
    )(disp, coords, nodes)


def first_payload(surf_coords, routes, pairs, me):
    earlier = iota((16, 16), 0) > iota((16, 16), 1)
    same = routes[:, :, None] == routes[:, None, :]
    rank = jnp.sum(jnp.where(same & earlier[None], 1, 0), axis=2)
    keys = (routes * 32 + me * 4 + rank).astype(F32)
    keys = jnp.where((iota((4, 128), 1) // 16) == me, jnp.tile(keys, (1, 8)), 0.0)
    both = jnp.swapaxes(pairs[:, 0], 1, 2).reshape(4, 128).astype(F32)
    return jnp.concatenate([surf_coords.reshape(48, 128), keys, both], axis=0)


def exchange(blocks):
    return lax.all_to_all(blocks, "gz", split_axis=0, concat_axis=0, tiled=True)


def make_lists(everyone, me):
    return pl.pallas_call(
        functools.partial(plan_kernel, around=()),
        out_shape=jax.ShapeDtypeStruct((8, 512), jnp.int32),
        in_specs=[pl.BlockSpec(memory_space=pltpu.SMEM), pl.BlockSpec(memory_space=pltpu.VMEM)],
        compiler_params=PARAMS,
    )(me, everyone)


CORNERS = [(0, 0, 0), (0, 0, 1), (0, 1, 0), (0, 1, 1), (1, 0, 0), (1, 0, 1), (1, 1, 0), (1, 1, 1)]


def padded_2(x, sides, width):
    for axis, dim in sides:
        count, length = (lax.axis_size(axis), x.shape[dim])
        up = [(i, (i + 1) % count) for i in range(count - 1)]
        down = [(j, i) for i, j in up]
        last = lax.slice_in_dim(x, length - width, length, axis=dim)
        first = lax.slice_in_dim(x, 0, width, axis=dim)
        before = lax.ppermute(last, axis, up)
        after = lax.ppermute(first, axis, down)
        x = jnp.concatenate([before, x, after], axis=dim)
    return x


def corner(field, offsets):
    size_x = field.shape[1] - 1
    size_y = field.shape[2] - 1
    size_z = field.shape[3] - 1
    return field[
        :,
        offsets[0] : offsets[0] + size_x,
        offsets[1] : offsets[1] + size_y,
        offsets[2] : offsets[2] + size_z,
    ]


def element_stress(disp, modulus):
    grads = []
    for axis in range(3):
        parts = []
        for first in (0, 1):
            for second in (0, 1):
                upper = [first, second]
                upper.insert(axis, 1)
                lower = [first, second]
                lower.insert(axis, 0)
                parts.append(corner(disp, upper) - corner(disp, lower))
        grads.append(0.25 * (parts[0] + parts[1] + parts[2] + parts[3]))
    strain_xx = grads[0][0]
    strain_yy = grads[1][1]
    strain_zz = grads[2][2]
    strain_xy = 0.5 * (grads[1][0] + grads[0][1])
    strain_yz = 0.5 * (grads[2][1] + grads[1][2])
    strain_zx = 0.5 * (grads[0][2] + grads[2][0])
    trace = strain_xx + strain_yy + strain_zz
    return jnp.stack(
        [
            modulus * (2.0 * strain_xx + trace),
            modulus * (2.0 * strain_yy + trace),
            modulus * (2.0 * strain_zz + trace),
            modulus * 2.0 * strain_xy,
            modulus * 2.0 * strain_yz,
            modulus * 2.0 * strain_zx,
        ]
    )


def node_forces(stress, load):
    rows = (
        (stress[0], stress[3], stress[5]),
        (stress[3], stress[1], stress[4]),
        (stress[5], stress[4], stress[2]),
    )
    total = jnp.float32(0.0)
    for offsets in CORNERS:
        signs = [2.0 * offsets[0] - 1.0, 2.0 * offsets[1] - 1.0, 2.0 * offsets[2] - 1.0]
        pieces = []
        for index in range(3):
            row = rows[index]
            pieces.append(
                -0.25 * (signs[0] * row[0] + signs[1] * row[1] + signs[2] * row[2])
                + 0.125 * load[index]
            )
        term = jnp.stack(pieces)
        total = total + jnp.pad(
            term,
            (
                (0, 0),
                (offsets[0], 1 - offsets[0]),
                (offsets[1], 1 - offsets[1]),
                (offsets[2], 1 - offsets[2]),
            ),
        )
    return total


def node_mass(density):
    share = 0.125 * density
    total = jnp.float32(0.0)
    for offsets in CORNERS:
        total = total + jnp.pad(
            share,
            (
                (offsets[0], 1 - offsets[0]),
                (offsets[1], 1 - offsets[1]),
                (offsets[2], 1 - offsets[2]),
            ),
        )
    return total


def element_mean(vel):
    total = jnp.float32(0.0)
    for offsets in CORNERS:
        total = total + corner(vel, offsets)
    return 0.125 * total


def fold_rim(padded, dim):
    length = padded.shape[dim]
    inner = lax.slice_in_dim(padded, 1, length - 1, axis=dim)
    lower = lax.slice_in_dim(padded, 0, 1, axis=dim)
    upper = lax.slice_in_dim(padded, length - 1, length, axis=dim)
    first = lax.slice_in_dim(inner, 0, 1, axis=dim) + lower
    middle = lax.slice_in_dim(inner, 1, length - 3, axis=dim)
    last = lax.slice_in_dim(inner, length - 3, length - 2, axis=dim) + upper
    return jnp.concatenate([first, middle, last], axis=dim)


def shared_sum(partial_value):
    padded = padded_2(partial_value, (("gx", 1), ("gy", 2), ("gz", 3)), 1)
    return fold_rim(fold_rim(fold_rim(padded, 1), 2), 3)


def owned(field):
    return field[:, :8, :12, :128].reshape(288, 128)


def partial_of(contact_rows):
    return jnp.pad(contact_rows.reshape(3, 8, 12, 128), ((0, 0), (0, 1), (0, 1), (0, 1)))


def per_device(stiffness, density, load, alive, surf_coords, surf_nodes, routes, pairs):
    me = lax.axis_index("gz")
    me_arr = jnp.reshape(me, (1,)).astype(jnp.int32)
    coords = surf_coords.reshape(48, 128)
    payload = first_payload(surf_coords, routes, pairs, me)
    everyone = exchange(jnp.broadcast_to(payload[None], (8,) + payload.shape))
    mass = shared_sum(node_mass(density)[None])[0]
    lists = make_lists(everyone, me_arr)
    c0, c1 = contact(lists, me_arr, everyone, surf_nodes, (0, 1), (0, 0))
    zero = jnp.zeros((6,) + stiffness.shape, F32)
    force = shared_sum(node_forces(zero, load) + partial_of(c0))
    vel = TIME_STEP * force / mass[None]
    disp1 = TIME_STEP * vel
    spots = exchange(gather_positions(owned(disp1), coords, surf_nodes))
    modulus = [stiffness * alive[t].astype(F32) for t in range(4)]
    force = shared_sum(node_forces(element_stress(disp1, modulus[1]), load) + partial_of(c1))
    vel = vel + TIME_STEP * force / mass[None]
    disp2 = disp1 + TIME_STEP * vel
    spots3 = exchange(gather_positions(owned(disp2), coords, surf_nodes))
    (c2,) = contact(lists, me_arr, spots, surf_nodes, (2,), (0,))
    force = shared_sum(node_forces(element_stress(disp2, modulus[2]), load) + partial_of(c2))
    vel = vel + TIME_STEP * force / mass[None]
    disp = disp2 + TIME_STEP * vel
    (c3,) = contact(lists, me_arr, spots3, surf_nodes, (3,), (0,))
    force = shared_sum(node_forces(element_stress(disp, modulus[3]), load) + partial_of(c3))
    vel = vel + TIME_STEP * force / mass[None]
    disp = disp + TIME_STEP * vel
    return (element_mean(vel), element_stress(disp, modulus[3]))


def solution(mesh):
    return jax.shard_map(
        per_device,
        mesh=mesh,
        in_specs=(
            P("gx", "gy", "gz"),
            P("gx", "gy", "gz"),
            P(None, "gx", "gy", "gz"),
            P(None, "gx", "gy", "gz"),
            P(("gx", "gy", "gz"), None, None),
            P(("gx", "gy", "gz"), None),
            P(None, ("gx", "gy", "gz")),
            P(None, ("gx", "gy", "gz"), None, None),
        ),
        out_specs=(P(None, "gx", "gy", "gz"), P(None, "gx", "gy", "gz")),
        check_vma=False,
    )
```

profile of v0, /device:TPU:80, one launch (start us, length us, event | category | flops | bytes accessed | tf_op | source)
XLA Modules:
  0.0 330.7 jit_solution(187981437001225519)
XLA Ops:
  1.7 1.9 collective-permute-start.6
  3.6 3.6 %collective-permute-start.7 = (f32[1,1,13,129]{3,1,2,0:T(1,128)S(1)}, f32[1,1,13,129]{3,1,2,0:T(1,128)S(1)}, u32[]{:S(2)}, u32[]{:S(2)}) collective-permute-start(f32[1,1,13,129]{3,1,2,0:T(1,128)S(1)} %get-tuple-element.169), channel_id=1, source_target_pairs={{32,0},{64,32},{96,64},{128,96},{160,128},{192,160},{224,192},{33,... | collective-permute-start | bytes 20132 | tf_op jit(solution)/shard_map/ppermute | solution.py:213
  10.2 9.3 %all-to-all-start = ((f32[8,56,128]{2,1,0:T(8,128)}), f32[8,56,128]{2,1,0:T(8,128)S(1)}, u32[]{:S(2)}, u32[]{:S(2)}) async-start(f32[8,56,128]{2,1,0:T(8,128)} %broadcast_in_dim.27), calls=%async_computation | async-start | bytes 458752 | tf_op jit(solution)/shard_map/all_to_all | solution.py:190
  21.0 2.9 collective-permute-start.8
  23.9 2.9 collective-permute-start.9
  26.9 2.8 collective-permute-done.9
  29.8 7.7 %collective-permute-start.10 = (f32[1,11,15,1]{3,1,2,0:T(8,128)S(1)}, f32[1,11,15,1]{3,1,2,0:T(8,128)S(1)}, u32[]{:S(2)}, u32[]{:S(2)}) collective-permute-start(f32[1,11,15,1]{3,1,2,0:T(8,128)S(1)} %get-tuple-element.162), channel_id=1, source_target_pairs={{0,1},{1,2},{2,3},{3,4},{4,5},{5,6},{6,7},{8,9},{9,10},{10,11},{11... | collective-permute-start | bytes 1988 | tf_op jit(solution)/shard_map/ppermute | solution.py:212
  40.1 9.5 %collective-permute-done.11 = f32[1,11,15,1]{3,1,2,0:T(8,128)S(1)} collective-permute-done((f32[1,11,15,1]{3,1,2,0:T(8,128)S(1)}, f32[1,11,15,1]{3,1,2,0:T(8,128)S(1)}, u32[]{:S(2)}, u32[]{:S(2)}) %collective-permute-start.11) | collective-permute-done | bytes 692 | tf_op jit(solution)/shard_map/ppermute | solution.py:213
  51.0 2.4 shard_map.95.list_ref
  53.4 32.1 %shard_map.96 = (f32[288,128]{1,0:T(8,128)S(1)}, f32[288,128]{1,0:T(8,128)S(1)}) custom-call(s32[8,512]{1,0:T(8,128)S(1)} %shard_map.95.list_ref, s32[1]{0:T(128)} %bitcast.me_ref, f32[8,56,128]{2,1,0:T(8,128)S(1)} %all-to-all-done.all_ref, s32[16,128]{1,0:T(8,128)S(1)} %copy-done), custom_call_target="tpu_custom_call" | custom-call | tf_op jit(solution)/shard_map/pallas_call | solution.py:137
  86.1 2.1 collective-permute-start
  88.1 3.6 %collective-permute-start.1 = (f32[3,1,13,129]{3,2,1,0:T(8,128)S(1)}, f32[3,1,13,129]{3,2,1,0:T(8,128)S(1)}, u32[]{:S(2)}, u32[]{:S(2)}) collective-permute-start(f32[3,1,13,129]{3,2,1,0:T(8,128)S(1)} %get-tuple-element.98), channel_id=1, source_target_pairs={{32,0},{64,32},{96,64},{128,96},{160,128},{192,160},{224,192},{33,... | collective-permute-start | bytes 60380 | tf_op jit(solution)/shard_map/ppermute | solution.py:213
  91.8 2.0 collective-permute-done.1
  93.9 2.1 collective-permute-start.2
  96.0 3.8 %collective-permute-start.3 = (f32[3,11,1,129]{3,2,1,0:T(1,128)S(1)}, f32[3,11,1,129]{3,2,1,0:T(1,128)S(1)}, u32[]{:S(2)}, u32[]{:S(2)}) collective-permute-start(f32[3,11,1,129]{3,2,1,0:T(1,128)S(1)} %get-tuple-element.64), channel_id=1, source_target_pairs={{8,0},{16,8},{24,16},{9,1},{17,9},{25,17},{10,2},{18,10},{26,18},{... | collective-permute-start | bytes 51092 | tf_op jit(solution)/shard_map/ppermute | solution.py:213
  100.0 1.8 collective-permute-done.3
  102.0 9.4 %collective-permute-start.4 = (f32[3,11,15,1]{3,2,1,0:T(8,128)S(1)}, f32[3,11,15,1]{3,2,1,0:T(8,128)S(1)}, u32[]{:S(2)}, u32[]{:S(2)}) collective-permute-start(f32[3,11,15,1]{3,2,1,0:T(8,128)S(1)} %get-tuple-element.61), channel_id=1, source_target_pairs={{0,1},{1,2},{2,3},{3,4},{4,5},{5,6},{6,7},{8,9},{9,10},{10,11},{11... | collective-permute-start | bytes 5948 | tf_op jit(solution)/shard_map/ppermute | solution.py:212
  112.9 6.6 %collective-permute-done.4 = f32[3,11,15,1]{3,2,1,0:T(8,128)S(1)} collective-permute-done((f32[3,11,15,1]{3,2,1,0:T(8,128)S(1)}, f32[3,11,15,1]{3,2,1,0:T(8,128)S(1)}, u32[]{:S(2)}, u32[]{:S(2)}) %collective-permute-start.4) | collective-permute-done | bytes 2012 | tf_op jit(solution)/shard_map/ppermute | solution.py:212
  119.5 15.8 %collective-permute-done.5 = f32[3,11,15,1]{3,2,1,0:T(8,128)S(1)} collective-permute-done((f32[3,11,15,1]{3,2,1,0:T(8,128)S(1)}, f32[3,11,15,1]{3,2,1,0:T(8,128)S(1)}, u32[]{:S(2)}, u32[]{:S(2)}) %collective-permute-start.5) | collective-permute-done | bytes 2012 | tf_op jit(solution)/shard_map/ppermute | solution.py:213
  138.9 1.9 collective-permute-start.12
  140.8 3.6 %collective-permute-start.13 = (f32[3,1,13,129]{3,2,1,0:T(8,128)S(1)}, f32[3,1,13,129]{3,2,1,0:T(8,128)S(1)}, u32[]{:S(2)}, u32[]{:S(2)}) collective-permute-start(f32[3,1,13,129]{3,2,1,0:T(8,128)S(1)} %get-tuple-element.92), channel_id=1, source_target_pairs={{32,0},{64,32},{96,64},{128,96},{160,128},{192,160},{224,192},{33,... | collective-permute-start | bytes 60380 | tf_op jit(solution)/shard_map/ppermute | solution.py:213
  144.5 1.7 collective-permute-done.13
  146.2 1.9 collective-permute-start.14
  148.2 3.9 %collective-permute-start.15 = (f32[3,11,1,129]{3,2,1,0:T(1,128)S(1)}, f32[3,11,1,129]{3,2,1,0:T(1,128)S(1)}, u32[]{:S(2)}, u32[]{:S(2)}) collective-permute-start(f32[3,11,1,129]{3,2,1,0:T(1,128)S(1)} %get-tuple-element.60), channel_id=1, source_target_pairs={{8,0},{16,8},{24,16},{9,1},{17,9},{25,17},{10,2},{18,10},{26,18},{... | collective-permute-start | bytes 51092 | tf_op jit(solution)/shard_map/ppermute | solution.py:213
  152.1 1.9 collective-permute-done.15
  154.9 5.7 %collective-permute-start.16 = (f32[3,11,15,1]{3,2,1,0:T(8,128)}, f32[3,11,15,1]{3,2,1,0:T(8,128)S(1)}, u32[]{:S(2)}, u32[]{:S(2)}) collective-permute-start(f32[3,11,15,1]{3,2,1,0:T(8,128)} %get-tuple-element.57), channel_id=1, source_target_pairs={{0,1},{1,2},{2,3},{3,4},{4,5},{5,6},{6,7},{8,9},{9,10},{10,11},{11... | collective-permute-start | bytes 5948 | tf_op jit(solution)/shard_map/ppermute | solution.py:212
  163.5 7.8 %all-to-all-start.1 = ((f32[8,48,128]{2,1,0:T(8,128)}), f32[8,48,128]{2,1,0:T(8,128)S(1)}, u32[]{:S(2)}, u32[]{:S(2)}) async-start(f32[8,48,128]{2,1,0:T(8,128)} %shard_map.97), calls=%async_computation.1 | async-start | bytes 393216 | tf_op jit(solution)/shard_map/all_to_all | solution.py:190
  171.3 2.4 collective-permute-done.16
  173.7 13.2 %collective-permute-done.17 = f32[3,11,15,1]{3,2,1,0:T(8,128)S(1)} collective-permute-done((f32[3,11,15,1]{3,2,1,0:T(8,128)S(1)}, f32[3,11,15,1]{3,2,1,0:T(8,128)S(1)}, u32[]{:S(2)}, u32[]{:S(2)}) %collective-permute-start.17) | collective-permute-done | bytes 2012 | tf_op jit(solution)/shard_map/ppermute | solution.py:213
  191.5 15.6 %shard_map.98 = f32[288,128]{1,0:T(8,128)S(1)} custom-call(s32[8,512]{1,0:T(8,128)S(1)} %shard_map.95.list_ref, s32[1]{0:T(128)} %bitcast.me_ref, f32[8,48,128]{2,1,0:T(8,128)S(1)} %all-to-all-done.1.all_ref, s32[16,128]{1,0:T(8,128)S(1)} %copy-done), custom_call_target="tpu_custom_call" | custom-call | tf_op jit(solution)/shard_map/pallas_call | solution.py:137
  209.5 1.9 collective-permute-start.18
  211.5 3.6 %collective-permute-start.19 = (f32[3,1,13,129]{3,2,1,0:T(8,128)S(1)}, f32[3,1,13,129]{3,2,1,0:T(8,128)S(1)}, u32[]{:S(2)}, u32[]{:S(2)}) collective-permute-start(f32[3,1,13,129]{3,2,1,0:T(8,128)S(1)} %get-tuple-element.83), channel_id=1, source_target_pairs={{32,0},{64,32},{96,64},{128,96},{160,128},{192,160},{224,192},{33,... | collective-permute-start | bytes 60380 | tf_op jit(solution)/shard_map/ppermute | solution.py:213
  215.1 1.7 collective-permute-done.19
  216.9 1.9 collective-permute-start.20
  218.8 3.9 %collective-permute-start.21 = (f32[3,11,1,129]{3,2,1,0:T(1,128)S(1)}, f32[3,11,1,129]{3,2,1,0:T(1,128)S(1)}, u32[]{:S(2)}, u32[]{:S(2)}) collective-permute-start(f32[3,11,1,129]{3,2,1,0:T(1,128)S(1)} %get-tuple-element.56), channel_id=1, source_target_pairs={{8,0},{16,8},{24,16},{9,1},{17,9},{25,17},{10,2},{18,10},{26,18},{... | collective-permute-start | bytes 51092 | tf_op jit(solution)/shard_map/ppermute | solution.py:213
  222.8 1.9 collective-permute-done.21
  224.8 5.7 %collective-permute-start.22 = (f32[3,11,15,1]{3,2,1,0:T(8,128)S(1)}, f32[3,11,15,1]{3,2,1,0:T(8,128)S(1)}, u32[]{:S(2)}, u32[]{:S(2)}) collective-permute-start(f32[3,11,15,1]{3,2,1,0:T(8,128)S(1)} %get-tuple-element.53), channel_id=1, source_target_pairs={{0,1},{1,2},{2,3},{3,4},{4,5},{5,6},{6,7},{8,9},{9,10},{10,11},{11... | collective-permute-start | bytes 5948 | tf_op jit(solution)/shard_map/ppermute | solution.py:212
  233.5 7.8 %all-to-all-start.2 = ((f32[8,48,128]{2,1,0:T(8,128)}), f32[8,48,128]{2,1,0:T(8,128)S(1)}, u32[]{:S(2)}, u32[]{:S(2)}) async-start(f32[8,48,128]{2,1,0:T(8,128)} %shard_map.99), calls=%async_computation.2 | async-start | bytes 393216 | tf_op jit(solution)/shard_map/all_to_all | solution.py:190
  241.6 16.3 %collective-permute-done.23 = f32[3,11,15,1]{3,2,1,0:T(8,128)S(1)} collective-permute-done((f32[3,11,15,1]{3,2,1,0:T(8,128)S(1)}, f32[3,11,15,1]{3,2,1,0:T(8,128)S(1)}, u32[]{:S(2)}, u32[]{:S(2)}) %collective-permute-start.23) | collective-permute-done | bytes 2012 | tf_op jit(solution)/shard_map/ppermute | solution.py:213
  260.0 16.0 %shard_map.100 = f32[288,128]{1,0:T(8,128)S(1)} custom-call(s32[8,512]{1,0:T(8,128)S(1)} %shard_map.95.list_ref, s32[1]{0:T(128)} %bitcast.me_ref, f32[8,48,128]{2,1,0:T(8,128)S(1)} %all-to-all-done.2.all_ref, s32[16,128]{1,0:T(8,128)S(1)} %copy-done), custom_call_target="tpu_custom_call" | custom-call | tf_op jit(solution)/shard_map/pallas_call | solution.py:137
  277.8 1.9 collective-permute-start.24
  279.7 4.8 %collective-permute-start.25 = (f32[3,1,13,129]{3,2,1,0:T(8,128)S(1)}, f32[3,1,13,129]{3,2,1,0:T(8,128)S(1)}, u32[]{:S(2)}, u32[]{:S(2)}) collective-permute-start(f32[3,1,13,129]{3,2,1,0:T(8,128)S(1)} %get-tuple-element.72), channel_id=1, source_target_pairs={{32,0},{64,32},{96,64},{128,96},{160,128},{192,160},{224,192},{33,... | collective-permute-start | bytes 60380 | tf_op jit(solution)/shard_map/ppermute | solution.py:213
  284.6 1.7 collective-permute-done.25
  286.3 1.9 collective-permute-start.26
  288.3 3.9 %collective-permute-start.27 = (f32[3,11,1,129]{3,2,1,0:T(1,128)S(1)}, f32[3,11,1,129]{3,2,1,0:T(1,128)S(1)}, u32[]{:S(2)}, u32[]{:S(2)}) collective-permute-start(f32[3,11,1,129]{3,2,1,0:T(1,128)S(1)} %get-tuple-element.52), channel_id=1, source_target_pairs={{8,0},{16,8},{24,16},{9,1},{17,9},{25,17},{10,2},{18,10},{26,18},{... | collective-permute-start | bytes 51092 | tf_op jit(solution)/shard_map/ppermute | solution.py:213
  292.2 1.9 collective-permute-done.27
  297.3 8.9 %collective-permute-done.28 = f32[3,11,15,1]{3,2,1,0:T(8,128)S(1)} collective-permute-done((f32[3,11,15,1]{3,2,1,0:T(8,128)S(1)}, f32[3,11,15,1]{3,2,1,0:T(8,128)S(1)}, u32[]{:S(2)}, u32[]{:S(2)}) %collective-permute-start.28) | collective-permute-done | bytes 2012 | tf_op jit(solution)/shard_map/ppermute | solution.py:212
  306.3 20.2 %collective-permute-done.29 = f32[3,11,15,1]{3,2,1,0:T(8,128)S(1)} collective-permute-done((f32[3,11,15,1]{3,2,1,0:T(8,128)S(1)}, f32[3,11,15,1]{3,2,1,0:T(8,128)S(1)}, u32[]{:S(2)}, u32[]{:S(2)}) %collective-permute-start.29) | collective-permute-done | bytes 2012 | tf_op jit(solution)/shard_map/ppermute | solution.py:213
  (181 shorter events, 40.7 us)
Async XLA Ops:
  1.7 19.3 %collective-permute-start.6 = (f32[1,1,13,129]{3,1,2,0:T(1,128)S(1)}, f32[1,1,13,129]{3,1,2,0:T(1,128)S(1)}, u32[]{:S(2)}, u32[]{:S(2)}) collective-permute-start(f32[1,1,13,129]{3,1,2,0:T(1,128)S(1)} %get-tuple-element.168), channel_id=1, source_target_pairs={{0,32},{32,64},{64,96},{96,128},{128,160},{160,192},{192,224},{1,3... | collective-permute-start | bytes 20132 | tf_op jit(solution)/shard_map/ppermute | solution.py:212
  3.6 17.4 %collective-permute-start.7 = (f32[1,1,13,129]{3,1,2,0:T(1,128)S(1)}, f32[1,1,13,129]{3,1,2,0:T(1,128)S(1)}, u32[]{:S(2)}, u32[]{:S(2)}) collective-permute-start(f32[1,1,13,129]{3,1,2,0:T(1,128)S(1)} %get-tuple-element.169), channel_id=1, source_target_pairs={{32,0},{64,32},{96,64},{128,96},{160,128},{192,160},{224,192},{33,... | collective-permute-start | bytes 20132 | tf_op jit(solution)/shard_map/ppermute | solution.py:213
  7.3 0.7 copy-start.9
  8.0 0.7 copy-start.8
  8.7 0.7 copy-start.7
  10.2 9.3 %copy-start.5 = (f32[3,8,12,128]{3,1,2,0:T(8,128)S(1)}, f32[3,8,12,128]{3,1,2,0:T(8,128)}, u32[]{:S(2)}) copy-start(f32[3,8,12,128]{3,1,2,0:T(8,128)} %param.10) | copy-start | bytes 442372
  10.2 40.8 %all-to-all-start = ((f32[8,56,128]{2,1,0:T(8,128)}), f32[8,56,128]{2,1,0:T(8,128)S(1)}, u32[]{:S(2)}, u32[]{:S(2)}) async-start(f32[8,56,128]{2,1,0:T(8,128)} %broadcast_in_dim.27), calls=%async_computation | async-start | bytes 458752 | tf_op jit(solution)/shard_map/all_to_all | solution.py:190
  19.4 0.9 copy-start.6
  21.0 5.9 %collective-permute-start.8 = (f32[1,11,1,129]{3,1,2,0:T(8,128)S(1)}, f32[1,11,1,129]{3,1,2,0:T(8,128)S(1)}, u32[]{:S(2)}, u32[]{:S(2)}) collective-permute-start(f32[1,11,1,129]{3,1,2,0:T(8,128)S(1)} %get-tuple-element.164), channel_id=1, source_target_pairs={{0,8},{8,16},{16,24},{1,9},{9,17},{17,25},{2,10},{10,18},{18,26},{... | collective-permute-start | bytes 17036 | tf_op jit(solution)/shard_map/ppermute | solution.py:212
  23.9 5.8 %collective-permute-start.9 = (f32[1,11,1,129]{3,1,2,0:T(8,128)S(1)}, f32[1,11,1,129]{3,1,2,0:T(8,128)S(1)}, u32[]{:S(2)}, u32[]{:S(2)}) collective-permute-start(f32[1,11,1,129]{3,1,2,0:T(8,128)S(1)} %get-tuple-element.165), channel_id=1, source_target_pairs={{8,0},{16,8},{24,16},{9,1},{17,9},{25,17},{10,2},{18,10},{26,18},{... | collective-permute-start | bytes 17036 | tf_op jit(solution)/shard_map/ppermute | solution.py:213
  29.8 10.2 %collective-permute-start.10 = (f32[1,11,15,1]{3,1,2,0:T(8,128)S(1)}, f32[1,11,15,1]{3,1,2,0:T(8,128)S(1)}, u32[]{:S(2)}, u32[]{:S(2)}) collective-permute-start(f32[1,11,15,1]{3,1,2,0:T(8,128)S(1)} %get-tuple-element.162), channel_id=1, source_target_pairs={{0,1},{1,2},{2,3},{3,4},{4,5},{5,6},{6,7},{8,9},{9,10},{10,11},{11... | collective-permute-start | bytes 1988 | tf_op jit(solution)/shard_map/ppermute | solution.py:212
  37.5 12.0 %collective-permute-start.11 = (f32[1,11,15,1]{3,1,2,0:T(8,128)S(1)}, f32[1,11,15,1]{3,1,2,0:T(8,128)S(1)}, u32[]{:S(2)}, u32[]{:S(2)}) collective-permute-start(f32[1,11,15,1]{3,1,2,0:T(8,128)S(1)} %get-tuple-element.163), channel_id=1, source_target_pairs={{1,0},{2,1},{3,2},{4,3},{5,4},{6,5},{7,6},{9,8},{10,9},{11,10},{12... | collective-permute-start | bytes 1988 | tf_op jit(solution)/shard_map/ppermute | solution.py:213
  50.3 0.7 copy-start.1
  51.0 2.4 copy-start
  86.0 5.7 %slice-start = ((f32[1,9,15,131]{3,1,2,0:T(8,128)}), f32[1,9,11,131]{3,1,2,0:T(8,128)S(1)}, s32[]{:S(2)}) async-start(f32[1,9,15,131]{3,1,2,0:T(8,128)} %copy-done.1), calls=%async_computation.3 | async-start | bytes 360448 | tf_op jit(solution)/shard_map/slice | solution.py:318
  86.1 5.7 %collective-permute-start = (f32[3,1,13,129]{3,2,1,0:T(8,128)S(1)}, f32[3,1,13,129]{3,2,1,0:T(8,128)S(1)}, u32[]{:S(2)}, u32[]{:S(2)}) collective-permute-start(f32[3,1,13,129]{3,2,1,0:T(8,128)S(1)} %get-tuple-element.97), channel_id=1, source_target_pairs={{0,32},{32,64},{64,96},{96,128},{128,160},{160,192},{192,224},{1,3... | collective-permute-start | bytes 60380 | tf_op jit(solution)/shard_map/ppermute | solution.py:212
  88.1 5.7 %collective-permute-start.1 = (f32[3,1,13,129]{3,2,1,0:T(8,128)S(1)}, f32[3,1,13,129]{3,2,1,0:T(8,128)S(1)}, u32[]{:S(2)}, u32[]{:S(2)}) collective-permute-start(f32[3,1,13,129]{3,2,1,0:T(8,128)S(1)} %get-tuple-element.98), channel_id=1, source_target_pairs={{32,0},{64,32},{96,64},{128,96},{160,128},{192,160},{224,192},{33,... | collective-permute-start | bytes 60380 | tf_op jit(solution)/shard_map/ppermute | solution.py:213
  93.9 6.1 %collective-permute-start.2 = (f32[3,11,1,129]{3,2,1,0:T(1,128)S(1)}, f32[3,11,1,129]{3,2,1,0:T(1,128)S(1)}, u32[]{:S(2)}, u32[]{:S(2)}) collective-permute-start(f32[3,11,1,129]{3,2,1,0:T(1,128)S(1)} %get-tuple-element.63), channel_id=1, source_target_pairs={{0,8},{8,16},{16,24},{1,9},{9,17},{17,25},{2,10},{10,18},{18,26},{... | collective-permute-start | bytes 51092 | tf_op jit(solution)/shard_map/ppermute | solution.py:212
  96.0 5.8 %collective-permute-start.3 = (f32[3,11,1,129]{3,2,1,0:T(1,128)S(1)}, f32[3,11,1,129]{3,2,1,0:T(1,128)S(1)}, u32[]{:S(2)}, u32[]{:S(2)}) collective-permute-start(f32[3,11,1,129]{3,2,1,0:T(1,128)S(1)} %get-tuple-element.64), channel_id=1, source_target_pairs={{8,0},{16,8},{24,16},{9,1},{17,9},{25,17},{10,2},{18,10},{26,18},{... | collective-permute-start | bytes 51092 | tf_op jit(solution)/shard_map/ppermute | solution.py:213
  102.0 17.6 %collective-permute-start.4 = (f32[3,11,15,1]{3,2,1,0:T(8,128)S(1)}, f32[3,11,15,1]{3,2,1,0:T(8,128)S(1)}, u32[]{:S(2)}, u32[]{:S(2)}) collective-permute-start(f32[3,11,15,1]{3,2,1,0:T(8,128)S(1)} %get-tuple-element.61), channel_id=1, source_target_pairs={{0,1},{1,2},{2,3},{3,4},{4,5},{5,6},{6,7},{8,9},{9,10},{10,11},{11... | collective-permute-start | bytes 5948 | tf_op jit(solution)/shard_map/ppermute | solution.py:212
  111.4 23.9 %collective-permute-start.5 = (f32[3,11,15,1]{3,2,1,0:T(8,128)S(1)}, f32[3,11,15,1]{3,2,1,0:T(8,128)S(1)}, u32[]{:S(2)}, u32[]{:S(2)}) collective-permute-start(f32[3,11,15,1]{3,2,1,0:T(8,128)S(1)} %get-tuple-element.62), channel_id=1, source_target_pairs={{1,0},{2,1},{3,2},{4,3},{5,4},{6,5},{7,6},{9,8},{10,9},{11,10},{12... | collective-permute-start | bytes 5948 | tf_op jit(solution)/shard_map/ppermute | solution.py:213
  137.1 0.8 copy-start.2
  138.9 5.6 %collective-permute-start.12 = (f32[3,1,13,129]{3,2,1,0:T(8,128)S(1)}, f32[3,1,13,129]{3,2,1,0:T(8,128)S(1)}, u32[]{:S(2)}, u32[]{:S(2)}) collective-permute-start(f32[3,1,13,129]{3,2,1,0:T(8,128)S(1)} %get-tuple-element.91), channel_id=1, source_target_pairs={{0,32},{32,64},{64,96},{96,128},{128,160},{160,192},{192,224},{1,3... | collective-permute-start | bytes 60380 | tf_op jit(solution)/shard_map/ppermute | solution.py:212
  140.8 5.4 %collective-permute-start.13 = (f32[3,1,13,129]{3,2,1,0:T(8,128)S(1)}, f32[3,1,13,129]{3,2,1,0:T(8,128)S(1)}, u32[]{:S(2)}, u32[]{:S(2)}) collective-permute-start(f32[3,1,13,129]{3,2,1,0:T(8,128)S(1)} %get-tuple-element.92), channel_id=1, source_target_pairs={{32,0},{64,32},{96,64},{128,96},{160,128},{192,160},{224,192},{33,... | collective-permute-start | bytes 60380 | tf_op jit(solution)/shard_map/ppermute | solution.py:213
  146.2 5.9 %collective-permute-start.14 = (f32[3,11,1,129]{3,2,1,0:T(1,128)S(1)}, f32[3,11,1,129]{3,2,1,0:T(1,128)S(1)}, u32[]{:S(2)}, u32[]{:S(2)}) collective-permute-start(f32[3,11,1,129]{3,2,1,0:T(1,128)S(1)} %get-tuple-element.59), channel_id=1, source_target_pairs={{0,8},{8,16},{16,24},{1,9},{9,17},{17,25},{2,10},{10,18},{18,26},{... | collective-permute-start | bytes 51092 | tf_op jit(solution)/shard_map/ppermute | solution.py:212
  148.2 5.8 %collective-permute-start.15 = (f32[3,11,1,129]{3,2,1,0:T(1,128)S(1)}, f32[3,11,1,129]{3,2,1,0:T(1,128)S(1)}, u32[]{:S(2)}, u32[]{:S(2)}) collective-permute-start(f32[3,11,1,129]{3,2,1,0:T(1,128)S(1)} %get-tuple-element.60), channel_id=1, source_target_pairs={{8,0},{16,8},{24,16},{9,1},{17,9},{25,17},{10,2},{18,10},{26,18},{... | collective-permute-start | bytes 51092 | tf_op jit(solution)/shard_map/ppermute | solution.py:213
  154.9 18.8 %collective-permute-start.16 = (f32[3,11,15,1]{3,2,1,0:T(8,128)}, f32[3,11,15,1]{3,2,1,0:T(8,128)S(1)}, u32[]{:S(2)}, u32[]{:S(2)}) collective-permute-start(f32[3,11,15,1]{3,2,1,0:T(8,128)} %get-tuple-element.57), channel_id=1, source_target_pairs={{0,1},{1,2},{2,3},{3,4},{4,5},{5,6},{6,7},{8,9},{9,10},{10,11},{11... | collective-permute-start | bytes 5948 | tf_op jit(solution)/shard_map/ppermute | solution.py:212
  160.6 26.4 %collective-permute-start.17 = (f32[3,11,15,1]{3,2,1,0:T(8,128)S(1)}, f32[3,11,15,1]{3,2,1,0:T(8,128)S(1)}, u32[]{:S(2)}, u32[]{:S(2)}) collective-permute-start(f32[3,11,15,1]{3,2,1,0:T(8,128)S(1)} %get-tuple-element.58), channel_id=1, source_target_pairs={{1,0},{2,1},{3,2},{4,3},{5,4},{6,5},{7,6},{9,8},{10,9},{11,10},{12... | collective-permute-start | bytes 5948 | tf_op jit(solution)/shard_map/ppermute | solution.py:213
  163.5 28.0 %all-to-all-start.1 = ((f32[8,48,128]{2,1,0:T(8,128)}), f32[8,48,128]{2,1,0:T(8,128)S(1)}, u32[]{:S(2)}, u32[]{:S(2)}) async-start(f32[8,48,128]{2,1,0:T(8,128)} %shard_map.97), calls=%async_computation.1 | async-start | bytes 393216 | tf_op jit(solution)/shard_map/all_to_all | solution.py:190
  207.1 0.8 copy-start.3
  209.5 5.6 %collective-permute-start.18 = (f32[3,1,13,129]{3,2,1,0:T(8,128)S(1)}, f32[3,1,13,129]{3,2,1,0:T(8,128)S(1)}, u32[]{:S(2)}, u32[]{:S(2)}) collective-permute-start(f32[3,1,13,129]{3,2,1,0:T(8,128)S(1)} %get-tuple-element.82), channel_id=1, source_target_pairs={{0,32},{32,64},{64,96},{96,128},{128,160},{160,192},{192,224},{1,3... | collective-permute-start | bytes 60380 | tf_op jit(solution)/shard_map/ppermute | solution.py:212
  211.5 5.4 %collective-permute-start.19 = (f32[3,1,13,129]{3,2,1,0:T(8,128)S(1)}, f32[3,1,13,129]{3,2,1,0:T(8,128)S(1)}, u32[]{:S(2)}, u32[]{:S(2)}) collective-permute-start(f32[3,1,13,129]{3,2,1,0:T(8,128)S(1)} %get-tuple-element.83), channel_id=1, source_target_pairs={{32,0},{64,32},{96,64},{128,96},{160,128},{192,160},{224,192},{33,... | collective-permute-start | bytes 60380 | tf_op jit(solution)/shard_map/ppermute | solution.py:213
  216.9 5.9 %collective-permute-start.20 = (f32[3,11,1,129]{3,2,1,0:T(1,128)S(1)}, f32[3,11,1,129]{3,2,1,0:T(1,128)S(1)}, u32[]{:S(2)}, u32[]{:S(2)}) collective-permute-start(f32[3,11,1,129]{3,2,1,0:T(1,128)S(1)} %get-tuple-element.55), channel_id=1, source_target_pairs={{0,8},{8,16},{16,24},{1,9},{9,17},{17,25},{2,10},{10,18},{18,26},{... | collective-permute-start | bytes 51092 | tf_op jit(solution)/shard_map/ppermute | solution.py:212
  218.8 5.8 %collective-permute-start.21 = (f32[3,11,1,129]{3,2,1,0:T(1,128)S(1)}, f32[3,11,1,129]{3,2,1,0:T(1,128)S(1)}, u32[]{:S(2)}, u32[]{:S(2)}) collective-permute-start(f32[3,11,1,129]{3,2,1,0:T(1,128)S(1)} %get-tuple-element.56), channel_id=1, source_target_pairs={{8,0},{16,8},{24,16},{9,1},{17,9},{25,17},{10,2},{18,10},{26,18},{... | collective-permute-start | bytes 51092 | tf_op jit(solution)/shard_map/ppermute | solution.py:213
  224.8 16.8 %collective-permute-start.22 = (f32[3,11,15,1]{3,2,1,0:T(8,128)S(1)}, f32[3,11,15,1]{3,2,1,0:T(8,128)S(1)}, u32[]{:S(2)}, u32[]{:S(2)}) collective-permute-start(f32[3,11,15,1]{3,2,1,0:T(8,128)S(1)} %get-tuple-element.53), channel_id=1, source_target_pairs={{0,1},{1,2},{2,3},{3,4},{4,5},{5,6},{6,7},{8,9},{9,10},{10,11},{11... | collective-permute-start | bytes 5948 | tf_op jit(solution)/shard_map/ppermute | solution.py:212
  230.6 27.3 %collective-permute-start.23 = (f32[3,11,15,1]{3,2,1,0:T(8,128)S(1)}, f32[3,11,15,1]{3,2,1,0:T(8,128)S(1)}, u32[]{:S(2)}, u32[]{:S(2)}) collective-permute-start(f32[3,11,15,1]{3,2,1,0:T(8,128)S(1)} %get-tuple-element.54), channel_id=1, source_target_pairs={{1,0},{2,1},{3,2},{4,3},{5,4},{6,5},{7,6},{9,8},{10,9},{11,10},{12... | collective-permute-start | bytes 5948 | tf_op jit(solution)/shard_map/ppermute | solution.py:213
  233.5 26.6 %all-to-all-start.2 = ((f32[8,48,128]{2,1,0:T(8,128)}), f32[8,48,128]{2,1,0:T(8,128)S(1)}, u32[]{:S(2)}, u32[]{:S(2)}) async-start(f32[8,48,128]{2,1,0:T(8,128)} %shard_map.99), calls=%async_computation.2 | async-start | bytes 393216 | tf_op jit(solution)/shard_map/all_to_all | solution.py:190
  276.1 0.8 copy-start.4
  277.8 6.8 %collective-permute-start.24 = (f32[3,1,13,129]{3,2,1,0:T(8,128)S(1)}, f32[3,1,13,129]{3,2,1,0:T(8,128)S(1)}, u32[]{:S(2)}, u32[]{:S(2)}) collective-permute-start(f32[3,1,13,129]{3,2,1,0:T(8,128)S(1)} %get-tuple-element.71), channel_id=1, source_target_pairs={{0,32},{32,64},{64,96},{96,128},{128,160},{160,192},{192,224},{1,3... | collective-permute-start | bytes 60380 | tf_op jit(solution)/shard_map/ppermute | solution.py:212
  279.7 6.6 %collective-permute-start.25 = (f32[3,1,13,129]{3,2,1,0:T(8,128)S(1)}, f32[3,1,13,129]{3,2,1,0:T(8,128)S(1)}, u32[]{:S(2)}, u32[]{:S(2)}) collective-permute-start(f32[3,1,13,129]{3,2,1,0:T(8,128)S(1)} %get-tuple-element.72), channel_id=1, source_target_pairs={{32,0},{64,32},{96,64},{128,96},{160,128},{192,160},{224,192},{33,... | collective-permute-start | bytes 60380 | tf_op jit(solution)/shard_map/ppermute | solution.py:213
  286.3 5.9 %collective-permute-start.26 = (f32[3,11,1,129]{3,2,1,0:T(1,128)S(1)}, f32[3,11,1,129]{3,2,1,0:T(1,128)S(1)}, u32[]{:S(2)}, u32[]{:S(2)}) collective-permute-start(f32[3,11,1,129]{3,2,1,0:T(1,128)S(1)} %get-tuple-element.51), channel_id=1, source_target_pairs={{0,8},{8,16},{16,24},{1,9},{9,17},{17,25},{2,10},{10,18},{18,26},{... | collective-permute-start | bytes 51092 | tf_op jit(solution)/shard_map/ppermute | solution.py:212
  288.3 5.8 %collective-permute-start.27 = (f32[3,11,1,129]{3,2,1,0:T(1,128)S(1)}, f32[3,11,1,129]{3,2,1,0:T(1,128)S(1)}, u32[]{:S(2)}, u32[]{:S(2)}) collective-permute-start(f32[3,11,1,129]{3,2,1,0:T(1,128)S(1)} %get-tuple-element.52), channel_id=1, source_target_pairs={{8,0},{16,8},{24,16},{9,1},{17,9},{25,17},{10,2},{18,10},{26,18},{... | collective-permute-start | bytes 51092 | tf_op jit(solution)/shard_map/ppermute | solution.py:213
  294.3 12.0 %collective-permute-start.28 = (f32[3,11,15,1]{3,2,1,0:T(8,128)S(1)}, f32[3,11,15,1]{3,2,1,0:T(8,128)S(1)}, u32[]{:S(2)}, u32[]{:S(2)}) collective-permute-start(f32[3,11,15,1]{3,2,1,0:T(8,128)S(1)} %get-tuple-element.49), channel_id=1, source_target_pairs={{0,1},{1,2},{2,3},{3,4},{4,5},{5,6},{6,7},{8,9},{9,10},{10,11},{11... | collective-permute-start | bytes 5948 | tf_op jit(solution)/shard_map/ppermute | solution.py:212
  295.8 30.7 %collective-permute-start.29 = (f32[3,11,15,1]{3,2,1,0:T(8,128)S(1)}, f32[3,11,15,1]{3,2,1,0:T(8,128)S(1)}, u32[]{:S(2)}, u32[]{:S(2)}) collective-permute-start(f32[3,11,15,1]{3,2,1,0:T(8,128)S(1)} %get-tuple-element.50), channel_id=1, source_target_pairs={{1,0},{2,1},{3,2},{4,3},{5,4},{6,5},{7,6},{9,8},{10,9},{11,10},{12... | collective-permute-start | bytes 5948 | tf_op jit(solution)/shard_map/ppermute | solution.py:213
where the time goes:
time: 337 us; the launch traced here: 331 us
  starting transfers between devices  120 us (36%)
  waiting for transfers between devices  112 us (33%)
  Pallas kernels  69.3 us (21%)
  other arithmetic  17.5 us (5%)
  local copies, waits for them, and re-layouts  10.3 us (3%)
    ppermute x15, waiting for transfers between devices, padded_2(): after = lax.ppermute(first, axis, down)  92.4 us
    pallas_call x3, Pallas kernels, contact(): pl.pallas_call(functools.partial(contact_kernel, steps=steps, first_rows=...  63.7 us
    ppermute x15, starting transfers between devices, padded_2(): before = lax.ppermute(last, axis, up)  50.6 us
    ppermute x15, starting transfers between devices, padded_2(): after = lax.ppermute(first, axis, down)  44.5 us
    all_to_all x3, starting transfers between devices, exchange(): return lax.all_to_all(blocks, 'gz', split_axis=0, concat_axis=0, tiled=True)  24.9 us
    ppermute x15, waiting for transfers between devices, padded_2(): before = lax.ppermute(last, axis, up)  19.5 us
    unnamed x23, local copies, waits for them, and re-layouts  6.87 us
  transfers between devices with their start and end apart: 33, of which 19 were waited for; matrix products, arithmetic and copies ran while one was open for 3% of the time, Pallas kernels for 1%

commit v1 on v0

v1 whole, which is shorter than its diff:
```python
import functools
import math
import jax
import jax.numpy as jnp
from jax import lax
from jax.experimental import pallas as pl
from jax.experimental.pallas import tpu as pltpu
from jax.sharding import PartitionSpec as P

F32 = jnp.float32
BF16 = jnp.bfloat16
SCALE = math.sqrt(math.log2(math.e) / 0.08)
DT = 0.2
PARAMS = pltpu.CompilerParams(vmem_limit_bytes=56 * 2**20)
VMEM = pl.BlockSpec(memory_space=pltpu.VMEM)
SMEM = pl.BlockSpec(memory_space=pltpu.SMEM)
KEYS, PAIRS, NODES, PLANES = 48, 52, 56, 72
ROWS_1 = 128
LATE, PLANES_2 = 48, 96
ROWS_2 = 144


def split2(x):
    hi = x.astype(BF16)
    return hi, (x - hi.astype(F32)).astype(BF16)


def iota(shape, dim):
    return lax.broadcasted_iota(jnp.int32, shape, dim)


def rim_lanes(shape):
    lane = iota(shape, len(shape) - 1)
    return (lane >= 126) | (lane < 3)


def roll_last(x, shift):
    shift = shift % x.shape[-1]
    return pltpu.roll(x, shift, x.ndim - 1) if shift else x


def pack(tiles):
    total = None
    for f, tile in enumerate(tiles):
        part = roll_last(jnp.where(rim_lanes(tile.shape), tile, 0.0), 8 * f)
        total = part if total is None else total + part
    return total


def unpack(packed, f):
    return jnp.where(rim_lanes(packed.shape), roll_last(packed, -8 * f), 0.0)


def both(main, rim):
    return jnp.concatenate([main, rim], axis=-1)


def fill16(x):
    pad = 16 - x.shape[-2]
    if not pad:
        return x
    return jnp.concatenate([x, jnp.zeros(x.shape[:-2] + (pad, x.shape[-1]), x.dtype)], axis=-2)


def next_y(x):
    return pltpu.roll(x, x.shape[1] - 1, 1)


def prev_y(x):
    return pltpu.roll(x, 1, 1)


def next_z(x):
    return roll_last(x, -1)


def prev_z(x):
    return roll_last(x, 1)


def planes_to_rows(packed, square_ref, count):
    square_ref[...] = jnp.zeros_like(square_ref)
    for i in range(packed.shape[0]):
        square_ref[13 * i : 13 * i + 13, :] = packed[i, 0:13, :]
    return jnp.transpose(roll_last(square_ref[...], 2))[0:count]


def rows_to_planes(rows, square_ref, planes):
    full = jnp.concatenate([rows, jnp.zeros((128 - rows.shape[0], 128), F32)], axis=0)
    square_ref[...] = roll_last(jnp.transpose(full), -2)
    return jnp.stack([fill16(square_ref[13 * i : 13 * i + 13, :]) for i in range(planes)])


def neighbour_planes(all_ref, first_row, count, me, last, square_ref, planes):
    low = all_ref[jnp.maximum(me - 1, 0), first_row : first_row + count, :]
    up = all_ref[jnp.minimum(me + 1, last), first_row : first_row + count, :]
    kind = iota((count, 128), 0) % 8
    low = jnp.where((kind < 2) & (me > 0), low, 0.0)
    up = jnp.where((kind >= 2) & (me < last), up, 0.0)
    return rows_to_planes(low + up, square_ref, planes)


def prep_kernel(coords_ref, rows_ref, nodes_ref, stiff_ref, dens_ref, load_ref, alive_ref, out_ref, square_ref):
    fields = [load_ref[0], load_ref[1], load_ref[2], dens_ref[...]]
    for step in (1, 2, 3):
        fields.append(stiff_ref[...] * alive_ref[step].astype(F32))
    rows = planes_to_rows(pack([fill16(f) for f in fields]), square_ref, 56)
    nodes = nodes_ref[...].astype(F32)
    for dest in range(8):
        out_ref[dest, 0:48, :] = coords_ref[...]
        out_ref[dest, 48:56, :] = rows_ref[...]
        out_ref[dest, 56:72, :] = nodes
        out_ref[dest, 72:128, :] = rows


def plan_kernel(me_ref, all_ref, list_ref):
    me = me_ref[0]
    lane = iota((1, 128), 1)
    block_of = iota((128, 128), 0).astype(F32)
    eye = iota((128, 128), 0) == iota((128, 128), 1)
    upper = (iota((128, 128), 0) < iota((128, 128), 1)).astype(BF16)
    place = iota((512, 128), 0).astype(F32)
    own, low, up0, up1 = [], [], [], []
    for src in range(8):
        ids = all_ref[src, NODES : NODES + 16, :]
        k = ids - 128.0 * jnp.floor(ids * (1.0 / 128.0))

        def some(want):
            return jnp.max(jnp.where(k == want, 1.0, 0.0), axis=1, keepdims=True)

        one = jnp.ones((16, 1), F32)
        own.append(one * jnp.where(me == src, 1.0, 0.0))
        low.append(some(127.0) * jnp.where(me == src + 1, 1.0, 0.0))
        is_up = jnp.where(me == src - 1, 1.0, 0.0)
        up0.append(some(0.0) * is_up)
        up1.append(some(1.0) * is_up)
    own, low, up0, up1 = [jnp.concatenate(x, axis=0) for x in (own, low, up0, up1)]
    allowed = [own + low + up0, own, own + low + jnp.maximum(up0, up1), own + up0]
    for step in range(4):
        keys = all_ref[0, KEYS + step : KEYS + 1 + step, :]
        for src in range(1, 8):
            keys = keys + all_ref[src, KEYS + step : KEYS + 1 + step, :]
        key_col = jnp.sum(jnp.where(eye, keys, 0.0), axis=1, keepdims=True)
        first_col = jnp.where(allowed[step] > 0.0, key_col, -1.0)
        base = jnp.zeros((1, 1), F32)
        total = jnp.zeros((8, 512), F32)
        for row in range(4):
            even = all_ref[2 * row, PAIRS + step : PAIRS + 1 + step, :]
            odd = all_ref[2 * row + 1, PAIRS + step : PAIRS + 1 + step, :]
            left = lane < 64
            first = jnp.where(left, even, pltpu.roll(odd, 64, 1))
            second = jnp.where(left, pltpu.roll(even, 64, 1), odd)
            box = jnp.where(left, 64.0 * row, 64.0 * row + 32.0)
            hit_first = first_col == first + box
            hit_second = key_col == second + box
            p_block = jnp.sum(jnp.where(hit_first, block_of, 0.0), axis=0, keepdims=True)
            r_block = jnp.sum(jnp.where(hit_second, block_of, 0.0), axis=0, keepdims=True)
            live = jnp.sum(jnp.where(hit_first, 1.0, 0.0), axis=0, keepdims=True) * jnp.sum(
                jnp.where(hit_second, 1.0, 0.0), axis=0, keepdims=True
            )
            p_slot = p_block - (16 * me - 16).astype(F32)
            mine = live > 0.0
            sel = jnp.where(mine, 1.0, 0.0)
            before = jnp.dot(
                jnp.broadcast_to(sel, (8, 128)).astype(BF16), upper, preferred_element_type=F32
            )[0:1]
            spot = jnp.where(mine, before + base, -1.0)
            base = base + jnp.sum(sel, axis=1, keepdims=True)
            onehot = jnp.where(place == spot, 1.0, 0.0).astype(BF16)
            codes = jnp.where(
                iota((8, 128), 0) == 0,
                jnp.broadcast_to(p_slot, (8, 128)),
                jnp.broadcast_to(r_block, (8, 128)),
            )
            codes = jnp.where(jnp.broadcast_to(mine, (8, 128)), codes, 0.0).astype(BF16)
            total = total + lax.dot_general(
                codes, onehot, (((1,), (1,)), ((), ())), preferred_element_type=F32
            )
        code = jnp.where(
            iota((1, 512), 1).astype(F32) < base, total[0:1] * 128.0 + total[1:2], 48.0 * 128.0
        )
        list_ref[step : step + 1, :] = code.astype(jnp.int32)
        list_ref[4 + step : 5 + step, :] = jnp.broadcast_to(base, (1, 512)).astype(jnp.int32)


UNROLL = 4


def fill_table(all_ref, first_row, table_ref):
    def body(src, carry):
        for row in range(48):
            wide = jnp.broadcast_to(all_ref[src, first_row + row : first_row + row + 1, :] * SCALE, (8, 128))
            table_ref[src * 16 + row // 3, row % 3] = pltpu.roll(wide, 0, 1, stride=1, stride_axis=0)
        return carry

    lax.fori_loop(0, 8, body, 0)


def pair_loop(list_ref, step, me, table_ref, force_ref):
    force_ref[...] = jnp.zeros_like(force_ref)

    def one(q):
        code = list_ref[step, q]
        slot = lax.shift_right_logical(code, 7)
        r = code & 127
        p = jnp.minimum(slot + (16 * me - 16), 127)
        xi = [jnp.broadcast_to(table_ref[p, c, 0:1, :], (8, 128)) for c in range(3)]
        xj = [table_ref[r, c] for c in range(3)]
        acc = [jnp.zeros((8, 128), F32)] * 3
        for k in range(16):
            diff = [xi[c] - roll_last(xj[c], 8 * k) for c in range(3)]
            dist = diff[0] * diff[0] + diff[1] * diff[1] + diff[2] * diff[2]
            w = jnp.exp2(-dist)
            acc = [acc[c] + w * diff[c] for c in range(3)]
        return slot, acc

    def body(g, carry):
        done = [one(g * UNROLL + u) for u in range(UNROLL)]
        for slot, acc in done:
            for c in range(3):
                force_ref[slot, c] += acc[c]
        return carry

    lax.fori_loop(0, (list_ref[4 + step, 0] + (UNROLL - 1)) // UNROLL, body, 0)


def row_and_lane(ids):
    line = jnp.floor(ids * (1.0 / 128.0))
    lane = ids - 128.0 * line
    i = jnp.floor((line + 0.5) * (1.0 / 12.0))
    return line + 4.0 * i, lane


def one_hot(at, rows=128):
    return jnp.where(iota((rows, 128), 0).astype(F32) == at, 1.0, 0.0)


def block_force(force_ref, slot, c):
    return jnp.sum(force_ref[slot, c], axis=0, keepdims=True) * (1.0 / SCALE)


def scatter_own(force_ref, all_ref, me, lhs_ref, lanes_ref):
    for s in range(16):
        at = slice(128 * s, 128 * s + 128)
        row, lane = row_and_lane(all_ref[me, NODES + s : NODES + s + 1, :])
        hot = one_hot(row)
        lanes_ref[:, at] = one_hot(lane).astype(BF16)
        for c in range(3):
            hi, lo = split2(block_force(force_ref, 16 + s, c))
            lhs_ref[128 * c : 128 * c + 128, at] = (hot * hi.astype(F32)).astype(BF16)
            lhs_ref[384 + 128 * c : 512 + 128 * c, at] = (hot * lo.astype(F32)).astype(BF16)
    out = lax.dot_general(
        lhs_ref[...], lanes_ref[...], (((1,), (1,)), ((), ())), preferred_element_type=F32
    )
    return (out[:384] + out[384:]).reshape(3, 8, 16, 128)


def scatter_rim(force_ref, all_ref, me, last, square_ref, low, ups):
    square_ref[...] = jnp.zeros_like(square_ref)
    sides = ([(jnp.maximum(me - 1, 0), 0, (127.0,))] if low else []) + [
        (jnp.minimum(me + 1, last), 32, ups)
    ]
    for src, first_slot, wants in sides:
        total = jnp.zeros((16, 128), F32)
        for s in range(16):
            row, lane = row_and_lane(all_ref[src, NODES + s : NODES + s + 1, :])
            hot = one_hot(row).astype(BF16)
            lines = []
            for want in wants:
                for c in range(3):
                    f = jnp.where(lane == want, block_force(force_ref, first_slot + s, c), 0.0)
                    lines.append(f)
            lines += [jnp.zeros((8 - len(lines), 128), F32)]
            hi, lo = split2(jnp.concatenate(lines, axis=0))
            total = total + lax.dot_general(
                jnp.concatenate([hi, lo], axis=0), hot, (((1,), (1,)), ((), ())), preferred_element_type=F32
            )
        summed = total[0:8] + total[8:16]
        for w, want in enumerate(wants):
            for c in range(3):
                at = int(want + 8 * c) % 128
                square_ref[at : at + 1, :] = summed[3 * w + c : 3 * w + c + 1]
    return jnp.transpose(square_ref[...]).reshape(8, 16, 128)


def node_sum(elements):
    e = 0.125 * elements
    e = e + prev_z(e)
    e = e + prev_y(e)
    zero = jnp.zeros((1,) + e.shape[1:], F32)
    return jnp.concatenate([e, zero], axis=0) + jnp.concatenate([zero, e], axis=0)


def first_contact_kernel(
    me_ref, list_ref, all_ref, load_ref, dens_ref, stiff_ref, alive_ref,
    fm_ref, c0_ref, m1_ref, up_ref, down_ref,
    table_ref, force_ref, lhs_ref, lanes_ref, square_ref,
):
    me, last = me_ref[0], 7
    planes = neighbour_planes(all_ref, PLANES, 56, me, last, square_ref, 8)
    fields = [load_ref[0], load_ref[1], load_ref[2], dens_ref[...]]
    sums = [node_sum(both(fill16(f), unpack(planes, n))) for n, f in enumerate(fields)]
    m1 = both(fill16(stiff_ref[...] * alive_ref[1].astype(F32)), unpack(planes, 4))
    m1_ref[...] = m1
    fill_table(all_ref, 0, table_ref)
    pair_loop(list_ref, 0, me, table_ref, force_ref)
    own = scatter_own(force_ref, all_ref, me, lhs_ref, lanes_ref)
    rim = scatter_rim(force_ref, all_ref, me, last, square_ref, True, (0.0,))
    zero = jnp.zeros((1, 16, 256), F32)
    for c in range(3):
        full = jnp.concatenate([both(own[c], unpack(rim, c)), zero], axis=0)
        c0_ref[c] = full
        sums[c] = sums[c] + full
    for n in range(4):
        fm_ref[n] = sums[n]
    ups = [s[7] for s in sums] + [s[8] for s in sums] + [m1[7]]
    downs = [s[0] for s in sums]
    send_planes(ups, up_ref)
    send_planes(downs, down_ref)


def send_planes(planes, out_ref):
    count = len(planes)
    for n, plane in enumerate(planes):
        out_ref[n] = plane[:, :128]
    for g in range(0, count, 16):
        out_ref[count + g // 16] = pack([p[:, 128:] for p in planes[g : g + 16]])


def get_plane(ref, n, count):
    return both(ref[n], unpack(ref[count + n // 16], n % 16))


def step_contact_kernel(me_ref, list_ref, all_ref, out_ref, table_ref, force_ref, lhs_ref, lanes_ref):
    me = me_ref[0]
    fill_table(all_ref, 0, table_ref)
    pair_loop(list_ref, 1, me, table_ref, force_ref)
    out_ref[...] = scatter_own(force_ref, all_ref, me, lhs_ref, lanes_ref)


def x_extended_1(fm_ref, m1_ref, ups_ref, downs_ref):
    out = []
    for n in range(4):
        own = fm_ref[n]
        low, add = get_plane(ups_ref, n, 9), get_plane(ups_ref, 4 + n, 9)
        high = get_plane(downs_ref, n, 4)
        out.append(
            jnp.concatenate([low[None], (own[0] + add)[None], own[1:8], (own[8] + high)[None]], axis=0)
        )
    m1 = jnp.concatenate(
        [get_plane(ups_ref, 8, 9)[None], m1_ref[...], jnp.zeros((1, 16, 256), F32)], axis=0
    )
    return out, m1


def rows16(x, j):
    return fill16(x[:, j, :])


def y_send_1_kernel(fm_ref, m1_ref, ups_ref, downs_ref, up_ref, down_ref):
    fields, m1 = x_extended_1(fm_ref, m1_ref, ups_ref, downs_ref)
    ups = [rows16(f, 11) for f in fields] + [rows16(f, 12) for f in fields] + [rows16(m1, 11)]
    send_planes(ups, up_ref)
    send_planes([rows16(f, 0) for f in fields], down_ref)


def stress_of(disp, modulus):
    grads = []
    for u in disp:
        s, d = u[1:] + u[:-1], u[1:] - u[:-1]
        sn = next_y(s)
        ss, sd = sn + s, sn - s
        ds = next_y(d) + d
        grads.append((ds + next_z(ds), sd + next_z(sd), next_z(ss) - ss))
    m = 0.25 * modulus
    exx, eyy, ezz = grads[0][0], grads[1][1], grads[2][2]
    trace = exx + eyy + ezz
    return (
        m * (2.0 * exx + trace),
        m * (2.0 * eyy + trace),
        m * (2.0 * ezz + trace),
        m * (grads[1][0] + grads[0][1]),
        m * (grads[2][1] + grads[1][2]),
        m * (grads[0][2] + grads[2][0]),
    )


def force_of(stress):
    xx, yy, zz, xy, yz, zx = stress
    out = []
    for a, b, c in ((xx, xy, zx), (xy, yy, yz), (zx, yz, zz)):
        az, bz, cz = a + prev_z(a), b + prev_z(b), prev_z(c) - c
        ay = az + prev_y(az)
        bc = (prev_y(bz) - bz) + (prev_y(cz) + cz)
        out.append(-0.25 * ((ay[:-1] - ay[1:]) + (bc[:-1] + bc[1:])))
    return out


def shift_rows(x, by):
    return pltpu.roll(x, by % x.shape[1], 1)


def gather_rows(disp, coords_ref, all_ids, lanes_ref, rows_ref):
    hot = rows_ref[...]
    values = []
    for c in range(3):
        hi, lo = split2(disp[c])
        field = jnp.concatenate([hi, lo], axis=0)
        picked = lax.dot_general(field, hot, (((0,), (0,)), ((), ())), preferred_element_type=F32)
        values.append(jnp.sum(picked * lanes_ref[...].astype(F32), axis=0, keepdims=True))
    return values


def second_step_kernel(
    flags_ref, fm_ref, c0_ref, m1_ref, xu_ref, xd_ref, yu_ref, yd_ref, c1_ref, coords_ref, nodes_ref,
    out_ref, state_ref, rows_ref, lanes_ref, square_ref,
):
    fields, m1 = x_extended_1(fm_ref, m1_ref, xu_ref, xd_ref)
    row = iota((10, 16, 256), 1)

    def extend(x, low, add, high):
        x = x + jnp.where(row == 0, add[:10, None, :], 0.0)
        if high is not None:
            x = x + jnp.where(row == 12, high[:10, None, :], 0.0)
        x = shift_rows(jnp.where(row < 13, x, 0.0), 1)
        return jnp.where(row == 0, low[:10, None, :], x)

    zero = jnp.zeros((16, 256), F32)
    fields = [
        extend(fields[n], get_plane(yu_ref, n, 9), get_plane(yu_ref, 4 + n, 9), get_plane(yd_ref, n, 4))
        for n in range(4)
    ]
    m1 = extend(m1, get_plane(yu_ref, 8, 9), zero, None)
    mass = fields[3]
    inv = jnp.where(mass > 0.0, DT / jnp.where(mass > 0.0, mass, 1.0), 0.0)
    disp1 = [DT * (inv * fields[c]) for c in range(3)]
    edge = jnp.zeros((1, 16, 256), F32)
    force = force_of([jnp.concatenate([x, edge], axis=0) for x in stress_of(disp1, m1[:9])])
    inv9 = inv[1:]
    flag_z = flags_ref[2]
    lane = iota((9, 16, 256), 2)
    rowj = iota((9, 16, 256), 1)
    packs = []
    disp2s, vel2s = [], []
    for c in range(3):
        c1 = jnp.concatenate([c1_ref[c], jnp.zeros((1, 16, 128), F32)], axis=0)
        c1 = shift_rows(both(c1, jnp.zeros((9, 16, 128), F32)), 1)
        c0 = shift_rows(c0_ref[c], 1)
        total = fields[c][1:]
        accel = inv9 * (total - c0)
        vel2 = inv9 * total + inv9 * force[c] + (accel + inv9 * c1)
        disp2 = disp1[c][1:] + DT * vel2
        good = (rowj > 0) & (rowj < 14)
        back = [shift_rows(jnp.where(good, x, 0.0), -1) for x in (disp2, vel2, accel)]
        disp2s.append(back[0])
        vel2s.append(back[1])
        state_ref[c] = back[0]
        state_ref[3 + c] = back[1]
        state_ref[6 + c] = back[2]
    state_ref[9] = shift_rows(jnp.where(good, inv9, 0.0), -1)
    for s in range(16):
        at = slice(128 * s, 128 * s + 128)
        r, l = row_and_lane(nodes_ref[s : s + 1, :].astype(F32))
        hot = one_hot(r).astype(BF16)
        rows_ref[0:128, at] = hot
        rows_ref[128:256, at] = hot
        lanes_ref[:, at] = one_hot(l).astype(BF16)
    for first, disp in (
        (0, [shift_rows(d[1:9], -1)[:, :, :128] for d in disp1]),
        (LATE, [d[0:8, :, :128] for d in disp2s]),
    ):
        values = gather_rows([d.reshape(128, 128) for d in disp], None, None, lanes_ref, rows_ref)
        for s in range(16):
            for c in range(3):
                line = values[c][:, 128 * s : 128 * s + 128] + coords_ref[3 * s + c : 3 * s + c + 1, :]
                for dest in range(8):
                    out_ref[dest, first + 3 * s + c : first + 3 * s + c + 1, :] = line
    rows = planes_to_rows(pack([x[:, :, :128] for x in disp2s + vel2s]), square_ref, 48)
    for dest in range(8):
        out_ref[dest, PLANES_2:ROWS_2, :] = rows


UPS = 13
DOWNS = 23


def late_contact_kernel(
    me_ref, list_ref, first_ref, all_ref, state_ref, stiff_ref, alive_ref,
    own_ref, up_ref, down_ref,
    table_ref, force_ref, lhs_ref, lanes_ref, square_ref,
):
    me, last = me_ref[0], 7
    zplanes = neighbour_planes(all_ref, PLANES_2, 48, me, last, square_ref, 9)
    mplanes = neighbour_planes(first_ref, PLANES, 56, me, last, square_ref, 8)
    at_last = me == last
    lane = iota((9, 16, 128), 2)
    inv = state_ref[9]
    zero = jnp.zeros((1, 16, 256), F32)

    def with_rim(own, n):
        rim = jnp.where((lane == 0) & at_last, own[:, :, 128:], unpack(zplanes, n))
        return both(own[:, :, :128], rim)

    contacts = []
    for step, first_row, low, ups in ((2, 0, True, (0.0, 1.0)), (3, LATE, False, (0.0,))):
        fill_table(all_ref, first_row, table_ref)
        pair_loop(list_ref, step, me, table_ref, force_ref)
        own = scatter_own(force_ref, first_ref, me, lhs_ref, lanes_ref)
        rim = scatter_rim(force_ref, first_ref, me, last, square_ref, low, ups)
        contacts.append(
            [jnp.concatenate([both(own[c], unpack(rim, c)), zero], axis=0) for c in range(3)]
        )
    for c in range(3):
        own_ref[c] = with_rim(state_ref[c], c)
        own_ref[3 + c] = with_rim(state_ref[3 + c], 3 + c) + state_ref[6 + c] + inv * contacts[0][c]
        own_ref[6 + c] = state_ref[6 + c] + inv * contacts[1][c]
    own_ref[9] = inv
    for n, step in ((10, 2), (11, 3)):
        m = both(fill16(stiff_ref[...] * alive_ref[step].astype(F32)), unpack(mplanes, 3 + step))
        own_ref[n] = jnp.concatenate([m, zero], axis=0)
    send_planes([own_ref[n, i] for n, i in UP_LIST], up_ref)
    send_planes([own_ref[n, i] for n, i in DOWN_LIST(0)], down_ref)


UP_LIST = (
    [(n, 6) for n in range(3)] + [(n, 7) for n in range(3)] + [(n, 7) for n in (3, 4, 5, 9)]
    + [(10, 6), (10, 7), (11, 7)]
)


def DOWN_LIST(base):
    return (
        [(n, p) for p in (0, 1, 2) for n in range(3)]
        + [(n, p) for p in (0, 1) for n in (3, 4, 5)]
        + [(n, 0) for n in (6, 7, 8)]
        + [(9, 0), (9, 1), (10, 0), (10, 1), (11, 0)]
    )


def UP_PLANE(n, i):
    return UP_LIST.index((n, i)) if (n, i) in UP_LIST else None


def DOWN_PLANE(n, i):
    lst = DOWN_LIST(0)
    return lst.index((n, i)) if (n, i) in lst else None


def x_extended_2(own_ref, ups_ref, downs_ref, at_last):
    zero = jnp.zeros((16, 256), F32)
    out = []
    for n in range(12):
        planes = []
        for i in (6, 7):
            at = UP_PLANE(n, i)
            planes.append(zero if at is None else get_plane(ups_ref, at, UPS))
        own = own_ref[n]
        for i in range(8):
            planes.append(own[i])
        for i in range(3):
            at = DOWN_PLANE(n, i)
            got = zero if at is None else get_plane(downs_ref, at, DOWNS)
            if i == 0:
                got = jnp.where(at_last, own[8], got)
            planes.append(got)
        out.append(jnp.stack(planes))
    return out


def y_send_2_kernel(flags_ref, own_ref, ups_ref, downs_ref, up_ref, down_ref):
    fields = x_extended_2(own_ref, ups_ref, downs_ref, flags_ref[0] > 0)
    up_list = [(n, j + 4) for n, j in UP_LIST]
    send_planes([fill16(fields[n][:, j, :]) for n, j in up_list], up_ref)
    send_planes([fill16(fields[n][:, j, :]) for n, j in DOWN_LIST(0)], down_ref)


def last_kernel(
    flags_ref, own_ref, xu_ref, xd_ref, yu_ref, yd_ref, vel_ref, stress_ref
):
    fields = x_extended_2(own_ref, xu_ref, xd_ref, flags_ref[0] > 0)
    y_last = flags_ref[1] > 0
    row = iota((13, 24, 256), 1)
    wide = []
    for n in range(12):
        x = jnp.concatenate([fields[n], jnp.zeros((13, 8, 256), F32)], axis=1)
        keep = (row < 12) | ((row == 12) & y_last)
        x = shift_rows(jnp.where(keep, x, 0.0), 2)
        for t, j in enumerate((6, 7)):
            at = UP_PLANE(n, j)
            if at is not None:
                x = x + jnp.where(row == t, get_plane(yu_ref, at, UPS)[:13, None, :], 0.0)
        for t in range(3):
            at = DOWN_PLANE(n, t)
            if at is not None:
                x = x + jnp.where(row == 14 + t, get_plane(yd_ref, at, DOWNS)[:13, None, :], 0.0)
        wide.append(x)
    disp2, vh3, g3, inv, m2, m3 = wide[0:3], wide[3:6], wide[6:9], wide[9], wide[10], wide[11]
    force = force_of(stress_of(disp2, m2[:12]))
    vel3 = [vh3[c][1:12] + inv[1:12] * force[c] for c in range(3)]
    disp3 = [disp2[c][1:12] + DT * vel3[c] for c in range(3)]
    force = force_of(stress_of(disp3, m3[1:11]))
    vel4 = [vel3[c][1:10] + (inv[2:11] * force[c] + g3[c][2:11]) for c in range(3)]
    disp4 = [disp3[c][1:10] + DT * vel4[c] for c in range(3)]
    stress = stress_of(disp4, m3[2:10])
    for n in range(6):
        stress_ref[n] = stress[n][:, 2:14, :128]
    for c in range(3):
        s = vel4[c][1:] + vel4[c][:-1]
        s = s + next_y(s)
        s = s + next_z(s)
        vel_ref[c] = 0.125 * s[:, 2:14, :128]


def call(kernel, outs, specs, scratch=()):
    return pl.pallas_call(
        kernel,
        out_shape=[jax.ShapeDtypeStruct(s, d) for s, d in outs],
        in_specs=specs,
        out_specs=[VMEM] * len(outs),
        scratch_shapes=list(scratch),
        compiler_params=PARAMS,
    )


def small_rows(routes, pairs, me):
    earlier = iota((16, 16), 0) > iota((16, 16), 1)
    same = routes[:, :, None] == routes[:, None, :]
    rank = jnp.sum(jnp.where(same & earlier[None], 1, 0), axis=2)
    keys = (routes * 32 + me * 4 + rank).astype(F32)
    keys = jnp.where((iota((4, 128), 1) // 16) == me, jnp.tile(keys, (1, 8)), 0.0)
    both_lists = jnp.swapaxes(pairs[:, 0], 1, 2).reshape(4, 128).astype(F32)
    return jnp.concatenate([keys, both_lists], axis=0)


def share(blocks):
    return lax.all_to_all(blocks, "gz", split_axis=0, concat_axis=0, tiled=True)


def neighbours(up, down, axis):
    count = lax.axis_size(axis)
    ahead = [(i, i + 1) for i in range(count - 1)]
    return lax.ppermute(up, axis, ahead), lax.ppermute(down, axis, [(j, i) for i, j in ahead])


TABLE = pltpu.VMEM((128, 3, 8, 128), F32)
FORCE = pltpu.VMEM((49, 3, 8, 128), F32)
LHS = pltpu.VMEM((768, 2048), BF16)
LANES = pltpu.VMEM((128, 2048), BF16)
SQUARE = pltpu.VMEM((128, 128), F32)


def per_device(stiffness, density, load, alive, surf_coords, surf_nodes, routes, pairs):
    index = [lax.axis_index(a) for a in ("gx", "gy", "gz")]
    me = jnp.reshape(index[2], (1,)).astype(jnp.int32)
    flags = jnp.stack(
        [(i == lax.axis_size(a) - 1).astype(jnp.int32) for i, a in zip(index, ("gx", "gy", "gz"))]
    )
    coords = surf_coords.reshape(48, 128)
    rows = small_rows(routes, pairs, index[2])
    (payload,) = call(prep_kernel, [((8, ROWS_1, 128), F32)], [VMEM] * 7, [SQUARE])(
        coords, rows, surf_nodes, stiffness, density, load, alive
    )
    everyone = share(payload)
    (lists,) = call(plan_kernel, [((8, 512), jnp.int32)], [SMEM, VMEM])(me, everyone)
    fm, c0, m1, up, down = call(
        first_contact_kernel,
        [((4, 9, 16, 256), F32), ((3, 9, 16, 256), F32), ((8, 16, 256), F32), ((10, 16, 128), F32),
         ((5, 16, 128), F32)],
        [SMEM, SMEM] + [VMEM] * 5,
        [TABLE, FORCE, LHS, LANES, SQUARE],
    )(me, lists, everyone, load, density, stiffness, alive)
    xu, xd = neighbours(up, down, "gx")
    (c1,) = call(
        step_contact_kernel, [((3, 8, 16, 128), F32)], [SMEM, SMEM, VMEM], [TABLE, FORCE, LHS, LANES]
    )(me, lists, everyone)
    up, down = call(y_send_1_kernel, [((10, 16, 128), F32), ((5, 16, 128), F32)], [VMEM] * 4)(
        fm, m1, xu, xd
    )
    yu, yd = neighbours(up, down, "gy")
    payload, state = call(
        second_step_kernel,
        [((8, ROWS_2, 128), F32), ((10, 9, 16, 256), F32)],
        [SMEM] + [VMEM] * 10,
        [pltpu.VMEM((256, 2048), BF16), LANES, SQUARE],
    )(flags, fm, c0, m1, xu, xd, yu, yd, c1, coords, surf_nodes)
    late = share(payload)
    own, up, down = call(
        late_contact_kernel,
        [((12, 9, 16, 256), F32), ((UPS + 1, 16, 128), F32), ((DOWNS + 2, 16, 128), F32)],
        [SMEM, SMEM] + [VMEM] * 5,
        [TABLE, FORCE, LHS, LANES, SQUARE],
    )(me, lists, everyone, late, state, stiffness, alive)
    xu, xd = neighbours(up, down, "gx")
    up, down = call(
        y_send_2_kernel,
        [((UPS + 1, 16, 128), F32), ((DOWNS + 2, 16, 128), F32)],
        [SMEM] + [VMEM] * 3,
    )(flags, own, xu, xd)
    yu, yd = neighbours(up, down, "gy")
    vel, stress = call(
        last_kernel,
        [((3, 8, 12, 128), F32), ((6, 8, 12, 128), F32)],
        [SMEM] + [VMEM] * 5,
    )(flags, own, xu, xd, yu, yd)
    return vel, stress


def solution(mesh):
    return jax.shard_map(
        per_device,
        mesh=mesh,
        in_specs=(
            P("gx", "gy", "gz"),
            P("gx", "gy", "gz"),
            P(None, "gx", "gy", "gz"),
            P(None, "gx", "gy", "gz"),
            P(("gx", "gy", "gz"), None, None),
            P(("gx", "gy", "gz"), None),
            P(None, ("gx", "gy", "gz")),
            P(None, ("gx", "gy", "gz"), None, None),
        ),
        out_specs=(P(None, "gx", "gy", "gz"), P(None, "gx", "gy", "gz")),
        check_vma=False,
    )
```

time: 337 us -> 181 us (0.54)
  the two profiles are of different devices: /device:TPU:80 before, /device:TPU:74 now
where the time goes in v1:
time: 181 us; the launch traced here: 180 us
  Pallas kernels  77.8 us (43%)
  blocking collectives  53.3 us (29%)
  starting transfers between devices  21.5 us (12%)
  local copies, waits for them, and re-layouts  14.5 us (8%)
  waiting for transfers between devices  8.83 us (5%)
  other arithmetic  3.56 us (2%)
    all_to_all x2, blocking collectives, share(): return lax.all_to_all(blocks, 'gz', split_axis=0, concat_axis=0, tiled=True)  53.3 us
    pallas_call x1, Pallas kernels, per_device(): call(late_contact_kernel, [((12, 9, 16, 256), F32), ((UPS + 1, 16, 128),...  30 us
    pallas_call x1, Pallas kernels, per_device(): call(first_contact_kernel, [((4, 9, 16, 256), F32), ((3, 9, 16, 256), F32...  16.5 us
    ppermute x4, starting transfers between devices, neighbours(): lax.ppermute(up, axis, ahead)  12.2 us
    unnamed x21, local copies, waits for them, and re-layouts  10.2 us
    ppermute x4, starting transfers between devices, neighbours(): lax.ppermute(down, axis, [(j, i) for i, j in ahead])  9.37 us
    pallas_call x1, Pallas kernels, per_device(): call(step_contact_kernel, [((3, 8, 16, 128), F32)], [SMEM, SMEM, VMEM], [...  7.96 us
    ppermute x4, waiting for transfers between devices, neighbours(): lax.ppermute(up, axis, ahead)  6.87 us
  transfers between devices with their start and end apart: 8, of which 3 were waited for; matrix products, arithmetic and copies ran while one was open for 0% of the time, Pallas kernels for 4%

profile of v1, /device:TPU:74, one launch (start us, length us, event | category | flops | bytes accessed | tf_op | source)
XLA Modules:
  0.0 180.3 jit_solution(16038410162993848872)
XLA Ops:
  0.7 0.7 convert_bitcast_fusion
  1.4 0.1 convert_element_type.22
  1.5 1.0 select_reduce_fusion
  2.4 0.7 add_convert_fusion
  3.1 0.1 tile.10
  3.2 0.8 copy.36
  4.0 0.6 reshape.27.coords_ref
  4.6 1.4 copy.37.stiff_ref
  6.0 1.4 copy.38.dens_ref
  7.4 1.6 copy.39.load_ref
  9.1 1.7 copy.40.alive_ref
  10.7 0.6 pad_maximum_fusion.rows_ref
  11.3 2.3 %shard_map.95 = f32[8,128,128]{2,1,0:T(8,128)} custom-call(f32[48,128]{1,0:T(8,128)} %reshape.27.coords_ref, f32[8,128]{1,0:T(8,128)} %pad_maximum_fusion.rows_ref, s32[16,128]{1,0:T(8,128)} %nodes_ref.3, f32[8,12,128]{2,1,0:T(8,128)} %copy.37.stiff_ref, f32[8,12,128]{2,1,0:T(8,128)} %copy.38.dens_ref, f32[3,8,12,128]{3,2,1,0:T(8,128)} %copy.39.load_ref, ...), custom_call_target="tpu_custom_call" | custom-call | tf_op jit(solution)/shard_map/pallas_call | solution.py:660
  13.6 27.6 %all_to_all.10.all_ref.first_ref = f32[8,128,128]{2,1,0:T(8,128)} all-to-all(f32[8,128,128]{2,1,0:T(8,128)} %shard_map.95), channel_id=1, replica_groups=mesh['gx'=8,'gy'=4,'gz'=8] {'gz'}, dimensions={0} | all-to-all | bytes 1048576 | tf_op jit(solution)/shard_map/all_to_all | solution.py:636
  41.2 4.2 %shard_map.96.list_ref = s32[8,512]{1,0:T(8,128)} custom-call(s32[1]{0:T(128)} %bitcast.3.me_ref, f32[8,128,128]{2,1,0:T(8,128)} %all_to_all.10.all_ref.first_ref), custom_call_target="tpu_custom_call" | custom-call | tf_op jit(solution)/shard_map/pallas_call | solution.py:664
  45.4 16.5 %shard_map.97 = (f32[4,9,16,256]{3,2,1,0:T(8,128)}, f32[3,9,16,256]{3,2,1,0:T(8,128)}, f32[8,16,256]{2,1,0:T(8,128)}, f32[10,16,128]{2,1,0:T(8,128)}, f32[5,16,128]{2,1,0:T(8,128)}) custom-call(s32[1]{0:T(128)} %bitcast.3.me_ref, s32[8,512]{1,0:T(8,128)} %shard_map.96.list_ref, f32[8,128,128]{2,1,0:T(8,128)} %all_to_all.10.all_ref.first_ref, ...), custom_call_target="tpu_custom_call" | custom-call | tf_op jit(solution)/shard_map/pallas_call | solution.py:665
  61.9 1.9 %collective-permute-start = (f32[10,16,128]{2,1,0:T(8,128)}, f32[10,16,128]{2,1,0:T(8,128)S(1)}, u32[]{:S(2)}, u32[]{:S(2)}) collective-permute-start(f32[10,16,128]{2,1,0:T(8,128)} %get-tuple-element.19), channel_id=1, source_target_pairs={{0,32},{32,64},{64,96},{96,128},{128,160},{160,192},{192,224},{1,3... | collective-permute-start | bytes 245768 | tf_op jit(solution)/shard_map/ppermute | solution.py:642
  63.8 3.6 %collective-permute-start.1 = (f32[5,16,128]{2,1,0:T(8,128)}, f32[5,16,128]{2,1,0:T(8,128)S(1)}, u32[]{:S(2)}, u32[]{:S(2)}) collective-permute-start(f32[5,16,128]{2,1,0:T(8,128)} %get-tuple-element.20), channel_id=1, source_target_pairs={{32,0},{64,32},{96,64},{128,96},{160,128},{192,160},{224,192},{33,... | collective-permute-start | bytes 122888 | tf_op jit(solution)/shard_map/ppermute | solution.py:642
  67.5 2.0 %collective-permute-done.1.downs_ref.xd_ref = f32[5,16,128]{2,1,0:T(8,128)S(1)} collective-permute-done((f32[5,16,128]{2,1,0:T(8,128)}, f32[5,16,128]{2,1,0:T(8,128)S(1)}, u32[]{:S(2)}, u32[]{:S(2)}) %collective-permute-start.1) | collective-permute-done | bytes 40992 | tf_op jit(solution)/shard_map/ppermute | solution.py:642
  69.4 0.0 collective-permute-done.ups_ref.xu_ref
  69.4 0.6 copy-done.4
  70.0 0.0 copy-done.2
  70.1 2.0 %shard_map.98 = (f32[10,16,128]{2,1,0:T(8,128)}, f32[5,16,128]{2,1,0:T(8,128)}) custom-call(f32[4,9,16,256]{3,2,1,0:T(8,128)} %get-tuple-element.16.fm_ref, f32[8,16,256]{2,1,0:T(8,128)} %get-tuple-element.18.m1_ref, f32[10,16,128]{2,1,0:T(8,128)} %copy-done.2, f32[5,16,128]{2,1,0:T(8,128)} %copy-done.4), custom_call_target="tpu_custom_call" | custom-call | tf_op jit(solution)/shard_map/pallas_call | solution.py:676
  72.1 1.9 %collective-permute-start.3 = (f32[5,16,128]{2,1,0:T(8,128)}, f32[5,16,128]{2,1,0:T(8,128)S(1)}, u32[]{:S(2)}, u32[]{:S(2)}) collective-permute-start(f32[5,16,128]{2,1,0:T(8,128)} %get-tuple-element.22), channel_id=1, source_target_pairs={{8,0},{16,8},{24,16},{9,1},{17,9},{25,17},{10,2},{18,10},{26,18},{... | collective-permute-start | bytes 122888 | tf_op jit(solution)/shard_map/ppermute | solution.py:642
  74.0 3.9 %collective-permute-start.2 = (f32[10,16,128]{2,1,0:T(8,128)}, f32[10,16,128]{2,1,0:T(8,128)S(1)}, u32[]{:S(2)}, u32[]{:S(2)}) collective-permute-start(f32[10,16,128]{2,1,0:T(8,128)} %get-tuple-element.21), channel_id=1, source_target_pairs={{0,8},{8,16},{16,24},{1,9},{9,17},{17,25},{2,10},{10,18},{18,26},{... | collective-permute-start | bytes 245768 | tf_op jit(solution)/shard_map/ppermute | solution.py:642
  77.9 0.6 add_convert_fusion.1.flags_ref
  78.5 8.0 %shard_map.99.c1_ref = f32[3,8,16,128]{3,2,1,0:T(8,128)} custom-call(s32[1]{0:T(128)} %bitcast.3.me_ref, s32[8,512]{1,0:T(8,128)} %shard_map.96.list_ref, f32[8,128,128]{2,1,0:T(8,128)} %all_to_all.10.all_ref.first_ref), custom_call_target="tpu_custom_call" | custom-call | tf_op jit(solution)/shard_map/pallas_call | solution.py:673
  86.5 0.0 collective-permute-done.3.yd_ref
  86.5 0.0 collective-permute-done.2.yu_ref
  86.5 0.6 copy-done.7
  87.1 0.1 copy-done.6
  87.1 5.6 %shard_map.100 = (f32[8,144,128]{2,1,0:T(8,128)}, f32[10,9,16,256]{3,2,1,0:T(8,128)}) custom-call(s32[3]{0:T(128)} %add_convert_fusion.1.flags_ref, f32[4,9,16,256]{3,2,1,0:T(8,128)} %get-tuple-element.16.fm_ref, f32[3,9,16,256]{3,2,1,0:T(8,128)} %get-tuple-element.17.c0_ref, f32[8,16,256]{2,1,0:T(8,128)} %get-tuple-element.18.m1_ref, ...), custom_call_target="tpu_custom_call" | custom-call | tf_op jit(solution)/shard_map/pallas_call | solution.py:680
  92.7 25.7 %all_to_all.11.all_ref = f32[8,144,128]{2,1,0:T(8,128)} all-to-all(f32[8,144,128]{2,1,0:T(8,128)} %get-tuple-element.23), channel_id=1, replica_groups=mesh['gx'=8,'gy'=4,'gz'=8] {'gz'}, dimensions={0} | all-to-all | bytes 1179648 | tf_op jit(solution)/shard_map/all_to_all | solution.py:636
  118.4 30.0 %shard_map.101 = (f32[12,9,16,256]{3,2,1,0:T(8,128)}, f32[14,16,128]{2,1,0:T(8,128)}, f32[25,16,128]{2,1,0:T(8,128)}) custom-call(s32[1]{0:T(128)} %bitcast.3.me_ref, s32[8,512]{1,0:T(8,128)} %shard_map.96.list_ref, f32[8,128,128]{2,1,0:T(8,128)} %all_to_all.10.all_ref.first_ref, f32[8,144,128]{2,1,0:T(8,128)} %all_to_all.11.all_ref, ...), custom_call_target="tpu_custom_call" | custom-call | tf_op jit(solution)/shard_map/pallas_call | solution.py:687
  148.4 1.9 %collective-permute-start.5 = (f32[25,16,128]{2,1,0:T(8,128)}, f32[25,16,128]{2,1,0:T(8,128)S(1)}, u32[]{:S(2)}, u32[]{:S(2)}) collective-permute-start(f32[25,16,128]{2,1,0:T(8,128)} %get-tuple-element.27), channel_id=1, source_target_pairs={{32,0},{64,32},{96,64},{128,96},{160,128},{192,160},{224,192},{33,... | collective-permute-start | bytes 614408 | tf_op jit(solution)/shard_map/ppermute | solution.py:642
  150.3 2.4 %collective-permute-start.4 = (f32[14,16,128]{2,1,0:T(8,128)}, f32[14,16,128]{2,1,0:T(8,128)S(1)}, u32[]{:S(2)}, u32[]{:S(2)}) collective-permute-start(f32[14,16,128]{2,1,0:T(8,128)} %get-tuple-element.26), channel_id=1, source_target_pairs={{0,32},{32,64},{64,96},{96,128},{128,160},{160,192},{192,224},{1,3... | collective-permute-start | bytes 344072 | tf_op jit(solution)/shard_map/ppermute | solution.py:642
  152.7 3.9 %collective-permute-done.4.ups_ref.xu_ref = f32[14,16,128]{2,1,0:T(8,128)S(1)} collective-permute-done((f32[14,16,128]{2,1,0:T(8,128)}, f32[14,16,128]{2,1,0:T(8,128)S(1)}, u32[]{:S(2)}, u32[]{:S(2)}) %collective-permute-start.4) | collective-permute-done | bytes 114720 | tf_op jit(solution)/shard_map/ppermute | solution.py:642
  156.6 0.6 copy-done.1
  157.3 0.1 copy-done
  157.3 2.6 %shard_map.102 = (f32[14,16,128]{2,1,0:T(8,128)}, f32[25,16,128]{2,1,0:T(8,128)}) custom-call(s32[3]{0:T(128)} %add_convert_fusion.1.flags_ref, f32[12,9,16,256]{3,2,1,0:T(8,128)} %get-tuple-element.25.own_ref, f32[14,16,128]{2,1,0:T(8,128)} %copy-done.1, f32[25,16,128]{2,1,0:T(8,128)} %copy-done), custom_call_target="tpu_custom_call" | custom-call | tf_op jit(solution)/shard_map/pallas_call | solution.py:694
  159.9 1.9 %collective-permute-start.7 = (f32[25,16,128]{2,1,0:T(8,128)}, f32[25,16,128]{2,1,0:T(8,128)S(1)}, u32[]{:S(2)}, u32[]{:S(2)}) collective-permute-start(f32[25,16,128]{2,1,0:T(8,128)} %get-tuple-element.29), channel_id=1, source_target_pairs={{8,0},{16,8},{24,16},{9,1},{17,9},{25,17},{10,2},{18,10},{26,18},{... | collective-permute-start | bytes 614408 | tf_op jit(solution)/shard_map/ppermute | solution.py:642
  161.8 3.9 %collective-permute-start.6 = (f32[14,16,128]{2,1,0:T(8,128)}, f32[14,16,128]{2,1,0:T(8,128)S(1)}, u32[]{:S(2)}, u32[]{:S(2)}) collective-permute-start(f32[14,16,128]{2,1,0:T(8,128)} %get-tuple-element.28), channel_id=1, source_target_pairs={{0,8},{8,16},{16,24},{1,9},{9,17},{17,25},{2,10},{10,18},{18,26},{... | collective-permute-start | bytes 344072 | tf_op jit(solution)/shard_map/ppermute | solution.py:642
  165.8 3.0 %collective-permute-done.6.yu_ref = f32[14,16,128]{2,1,0:T(8,128)S(1)} collective-permute-done((f32[14,16,128]{2,1,0:T(8,128)}, f32[14,16,128]{2,1,0:T(8,128)S(1)}, u32[]{:S(2)}, u32[]{:S(2)}) %collective-permute-start.6) | collective-permute-done | bytes 114720 | tf_op jit(solution)/shard_map/ppermute | solution.py:642
  168.7 0.6 copy-done.5
  169.4 0.7 copy-done.3
  170.0 6.8 %shard_map.103 = (f32[3,8,12,128]{3,2,1,0:T(8,128)}, f32[6,8,12,128]{3,2,1,0:T(8,128)}) custom-call(s32[3]{0:T(128)} %add_convert_fusion.1.flags_ref, f32[12,9,16,256]{3,2,1,0:T(8,128)} %get-tuple-element.25.own_ref, f32[14,16,128]{2,1,0:T(8,128)} %copy-done.1, f32[25,16,128]{2,1,0:T(8,128)} %copy-done, f32[14,16,128]{2,1,0:T(8,128)} %copy-done.5, ...), custom_call_target="tpu_custom_call" | custom-call | tf_op jit(solution)/shard_map/pallas_call | solution.py:700
  176.8 1.6 copy.47
  178.5 1.8 copy.48
  (15 shorter events, 0.0 us)
Async XLA Ops:
  61.9 7.5 %collective-permute-start = (f32[10,16,128]{2,1,0:T(8,128)}, f32[10,16,128]{2,1,0:T(8,128)S(1)}, u32[]{:S(2)}, u32[]{:S(2)}) collective-permute-start(f32[10,16,128]{2,1,0:T(8,128)} %get-tuple-element.19), channel_id=1, source_target_pairs={{0,32},{32,64},{64,96},{96,128},{128,160},{160,192},{192,224},{1,3... | collective-permute-start | bytes 245768 | tf_op jit(solution)/shard_map/ppermute | solution.py:642
  63.8 5.6 %collective-permute-start.1 = (f32[5,16,128]{2,1,0:T(8,128)}, f32[5,16,128]{2,1,0:T(8,128)S(1)}, u32[]{:S(2)}, u32[]{:S(2)}) collective-permute-start(f32[5,16,128]{2,1,0:T(8,128)} %get-tuple-element.20), channel_id=1, source_target_pairs={{32,0},{64,32},{96,64},{128,96},{160,128},{192,160},{224,192},{33,... | collective-permute-start | bytes 122888 | tf_op jit(solution)/shard_map/ppermute | solution.py:642
  69.4 0.6 copy-start.4
  69.4 0.6 copy-start.2
  72.1 14.4 %collective-permute-start.3 = (f32[5,16,128]{2,1,0:T(8,128)}, f32[5,16,128]{2,1,0:T(8,128)S(1)}, u32[]{:S(2)}, u32[]{:S(2)}) collective-permute-start(f32[5,16,128]{2,1,0:T(8,128)} %get-tuple-element.22), channel_id=1, source_target_pairs={{8,0},{16,8},{24,16},{9,1},{17,9},{25,17},{10,2},{18,10},{26,18},{... | collective-permute-start | bytes 122888 | tf_op jit(solution)/shard_map/ppermute | solution.py:642
  74.0 12.5 %collective-permute-start.2 = (f32[10,16,128]{2,1,0:T(8,128)}, f32[10,16,128]{2,1,0:T(8,128)S(1)}, u32[]{:S(2)}, u32[]{:S(2)}) collective-permute-start(f32[10,16,128]{2,1,0:T(8,128)} %get-tuple-element.21), channel_id=1, source_target_pairs={{0,8},{8,16},{16,24},{1,9},{9,17},{17,25},{2,10},{10,18},{18,26},{... | collective-permute-start | bytes 245768 | tf_op jit(solution)/shard_map/ppermute | solution.py:642
  86.5 0.6 copy-start.7
  86.5 0.7 copy-start.6
  148.4 8.2 %collective-permute-start.5 = (f32[25,16,128]{2,1,0:T(8,128)}, f32[25,16,128]{2,1,0:T(8,128)S(1)}, u32[]{:S(2)}, u32[]{:S(2)}) collective-permute-start(f32[25,16,128]{2,1,0:T(8,128)} %get-tuple-element.27), channel_id=1, source_target_pairs={{32,0},{64,32},{96,64},{128,96},{160,128},{192,160},{224,192},{33,... | collective-permute-start | bytes 614408 | tf_op jit(solution)/shard_map/ppermute | solution.py:642
  150.3 6.3 %collective-permute-start.4 = (f32[14,16,128]{2,1,0:T(8,128)}, f32[14,16,128]{2,1,0:T(8,128)S(1)}, u32[]{:S(2)}, u32[]{:S(2)}) collective-permute-start(f32[14,16,128]{2,1,0:T(8,128)} %get-tuple-element.26), channel_id=1, source_target_pairs={{0,32},{32,64},{64,96},{96,128},{128,160},{160,192},{192,224},{1,3... | collective-permute-start | bytes 344072 | tf_op jit(solution)/shard_map/ppermute | solution.py:642
  156.6 0.6 copy-start.1
  156.6 0.7 copy-start
  159.9 8.8 %collective-permute-start.7 = (f32[25,16,128]{2,1,0:T(8,128)}, f32[25,16,128]{2,1,0:T(8,128)S(1)}, u32[]{:S(2)}, u32[]{:S(2)}) collective-permute-start(f32[25,16,128]{2,1,0:T(8,128)} %get-tuple-element.29), channel_id=1, source_target_pairs={{8,0},{16,8},{24,16},{9,1},{17,9},{25,17},{10,2},{18,10},{26,18},{... | collective-permute-start | bytes 614408 | tf_op jit(solution)/shard_map/ppermute | solution.py:642
  161.8 6.9 %collective-permute-start.6 = (f32[14,16,128]{2,1,0:T(8,128)}, f32[14,16,128]{2,1,0:T(8,128)S(1)}, u32[]{:S(2)}, u32[]{:S(2)}) collective-permute-start(f32[14,16,128]{2,1,0:T(8,128)} %get-tuple-element.28), channel_id=1, source_target_pairs={{0,8},{8,16},{16,24},{1,9},{9,17},{17,25},{2,10},{10,18},{18,26},{... | collective-permute-start | bytes 344072 | tf_op jit(solution)/shard_map/ppermute | solution.py:642
  168.7 0.6 copy-start.5
  169.4 0.7 copy-start.3

commit v2 on v1

v2 whole, which is shorter than its diff:
```python
import functools
import math
import jax
import jax.numpy as jnp
from jax import lax
from jax.experimental import pallas as pl
from jax.experimental.pallas import tpu as pltpu
from jax.sharding import PartitionSpec as P

F32 = jnp.float32
BF16 = jnp.bfloat16
SCALE = math.sqrt(math.log2(math.e) / 0.08)
DT = 0.2
PARAMS = pltpu.CompilerParams(vmem_limit_bytes=56 * 2**20)
VMEM = pl.BlockSpec(memory_space=pltpu.VMEM)
SMEM = pl.BlockSpec(memory_space=pltpu.SMEM)
KEYS, PAIRS, NODES, PLANES = 48, 52, 56, 72
ROWS_1 = 104
LATE, PLANES_2 = 48, 96
ROWS_2 = 128
PLANE_ROWS = 32


def split2(x):
    hi = x.astype(BF16)
    return hi, (x - hi.astype(F32)).astype(BF16)


def iota(shape, dim):
    return lax.broadcasted_iota(jnp.int32, shape, dim)


def rim_lanes(shape, above=3):
    lane = iota(shape, len(shape) - 1)
    return (lane >= 126) | (lane < above)


def roll_last(x, shift):
    shift = shift % x.shape[-1]
    return pltpu.roll(x, shift, x.ndim - 1) if shift else x


def pack(tiles, stride=8):
    total = None
    for f, tile in enumerate(tiles):
        part = roll_last(jnp.where(rim_lanes(tile.shape, min(stride - 2, 3)), tile, 0.0), stride * f)
        total = part if total is None else total + part
    return total


def unpack(packed, f, stride=8):
    return jnp.where(
        rim_lanes(packed.shape, min(stride - 2, 3)), roll_last(packed, -stride * f), 0.0
    )


def both(main, rim):
    return jnp.concatenate([main, rim], axis=-1)


def fill16(x):
    pad = 16 - x.shape[-2]
    if not pad:
        return x
    return jnp.concatenate([x, jnp.zeros(x.shape[:-2] + (pad, x.shape[-1]), x.dtype)], axis=-2)


def next_x(x):
    return pltpu.roll(x, x.shape[1] - 1, 1)


def prev_x(x):
    return pltpu.roll(x, 1, 1)


def next_z(x):
    return roll_last(x, -1)


def prev_z(x):
    return roll_last(x, 1)


def planes_to_rows(packed, square_ref):
    square_ref[...] = jnp.zeros_like(square_ref)
    for j in range(packed.shape[0]):
        square_ref[9 * j : 9 * j + 9, :] = packed[j, 0:9, :]
    return jnp.transpose(roll_last(square_ref[...], 2))[0:PLANE_ROWS]


def rows_to_planes(rows, square_ref, planes):
    full = jnp.concatenate([rows, jnp.zeros((128 - PLANE_ROWS, 128), F32)], axis=0)
    square_ref[...] = roll_last(jnp.transpose(full), -2)
    return jnp.stack([fill16(square_ref[9 * j : 9 * j + 9, :]) for j in range(planes)])


def neighbour_planes(all_ref, first_row, stride, me, square_ref, planes):
    low = all_ref[jnp.maximum(me - 1, 0), first_row : first_row + PLANE_ROWS, :]
    up = all_ref[jnp.minimum(me + 1, 7), first_row : first_row + PLANE_ROWS, :]
    kind = iota((PLANE_ROWS, 128), 0) % stride
    low = jnp.where((kind < 2) & (me > 0), low, 0.0)
    up = jnp.where((kind >= 2) & (me < 7), up, 0.0)
    return rows_to_planes(low + up, square_ref, planes)


def spread(x, first):
    to = (iota((x.shape[1], 128), 1) == iota((x.shape[1], 128), 0) + first).astype(BF16)
    return jnp.dot(x.astype(BF16), to, preferred_element_type=F32)


def prep_kernel(
    at_ref, coords_ref, routes_ref, pairs_ref, nodes_ref, stiff_ref, dens_ref, load_ref, alive_ref,
    out_ref, square_ref,
):
    me = at_ref[2]
    fields = [load_ref[0], load_ref[1], load_ref[2], dens_ref[...]]
    for step in (1, 2, 3):
        fields.append(stiff_ref[...] * alive_ref[step].astype(F32))
    rows = planes_to_rows(pack([fill16(f) for f in fields], 4), square_ref)
    nodes = nodes_ref[...].astype(F32)
    routes = routes_ref[...].astype(F32)
    rank = jnp.zeros((4, 16), F32)
    later = iota((4, 16), 1)
    for s in range(15):
        same = jnp.broadcast_to(routes[:, s : s + 1], (4, 16)) == routes
        rank = rank + jnp.where(same & (later > s), 1.0, 0.0)
    keys = spread(routes * 32.0 + rank + 4.0 * me.astype(F32), 16 * me)
    lists = spread(pairs_ref[:, 0, :].astype(F32), 0) + spread(pairs_ref[:, 1, :].astype(F32), 64)
    for dest in range(8):
        for c in range(3):
            out_ref[dest, 16 * c : 16 * c + 16, :] = coords_ref[c]
        out_ref[dest, KEYS : KEYS + 4, :] = keys
        out_ref[dest, PAIRS : PAIRS + 4, :] = lists
        out_ref[dest, NODES : NODES + 16, :] = nodes
        out_ref[dest, PLANES:ROWS_1, :] = rows


def plan_kernel(at_ref, all_ref, list_ref):
    me = at_ref[2]
    lane = iota((1, 128), 1)
    block_of = iota((128, 128), 0).astype(F32)
    eye = iota((128, 128), 0) == iota((128, 128), 1)
    upper = (iota((128, 128), 0) < iota((128, 128), 1)).astype(BF16)
    place = iota((128, 128), 0).astype(F32)
    own, low, up0, up1 = [], [], [], []
    for src in range(8):
        ids = all_ref[src, NODES : NODES + 16, :]
        k = ids - 128.0 * jnp.floor(ids * (1.0 / 128.0))

        def some(want):
            return jnp.max(jnp.where(k == want, 1.0, 0.0), axis=1, keepdims=True)

        one = jnp.ones((16, 1), F32)
        own.append(one * jnp.where(me == src, 1.0, 0.0))
        low.append(some(127.0) * jnp.where(me == src + 1, 1.0, 0.0))
        is_up = jnp.where(me == src - 1, 1.0, 0.0)
        up0.append(some(0.0) * is_up)
        up1.append(some(1.0) * is_up)
    own, low, up0, up1 = [jnp.concatenate(x, axis=0) for x in (own, low, up0, up1)]
    allowed = [own + low + up0, own, own + low + jnp.maximum(up0, up1), own + up0]
    for step in range(4):
        keys = all_ref[0, KEYS + step : KEYS + 1 + step, :]
        for src in range(1, 8):
            keys = keys + all_ref[src, KEYS + step : KEYS + 1 + step, :]
        key_col = jnp.sum(jnp.where(eye, keys, 0.0), axis=1, keepdims=True)
        first_col = jnp.where(allowed[step] > 0.0, key_col, -1.0)
        base = jnp.zeros((1, 1), F32)
        spots, codes = [], []
        for row in range(4):
            even = all_ref[2 * row, PAIRS + step : PAIRS + 1 + step, :]
            odd = all_ref[2 * row + 1, PAIRS + step : PAIRS + 1 + step, :]
            left = lane < 64
            first = jnp.where(left, even, pltpu.roll(odd, 64, 1))
            second = jnp.where(left, pltpu.roll(even, 64, 1), odd)
            box = jnp.where(left, 64.0 * row, 64.0 * row + 32.0)
            hit_first = first_col == first + box
            hit_second = key_col == second + box
            p_block = jnp.sum(jnp.where(hit_first, block_of, 0.0), axis=0, keepdims=True)
            r_block = jnp.sum(jnp.where(hit_second, block_of, 0.0), axis=0, keepdims=True)
            live = jnp.sum(jnp.where(hit_first, 1.0, 0.0), axis=0, keepdims=True) * jnp.sum(
                jnp.where(hit_second, 1.0, 0.0), axis=0, keepdims=True
            )
            p_slot = p_block - (16 * me - 16).astype(F32)
            mine = live > 0.0
            sel = jnp.where(mine, 1.0, 0.0)
            before = jnp.dot(
                jnp.broadcast_to(sel, (8, 128)).astype(BF16), upper, preferred_element_type=F32
            )[0:1]
            spots.append(jnp.where(mine, before + base, -1.0))
            base = base + jnp.sum(sel, axis=1, keepdims=True)
            code = jnp.where(
                iota((8, 128), 0) == 0,
                jnp.broadcast_to(p_slot, (8, 128)),
                jnp.broadcast_to(r_block, (8, 128)),
            )
            codes.append(jnp.where(jnp.broadcast_to(mine, (8, 128)), code, 0.0).astype(BF16))
        list_ref[4 + step : 5 + step, :] = jnp.broadcast_to(base, (1, 512)).astype(jnp.int32)
        count = jnp.max(base)
        for part in range(4):

            def write(part=part, spots=spots, codes=codes, base=base):
                total = jnp.zeros((8, 128), F32)
                for row in range(4):
                    onehot = jnp.where(place == spots[row] - 128.0 * part, 1.0, 0.0).astype(BF16)
                    total = total + lax.dot_general(
                        codes[row], onehot, (((1,), (1,)), ((), ())), preferred_element_type=F32
                    )
                used = (lane + 128 * part).astype(F32) < base
                code = jnp.where(used, total[0:1] * 128.0 + total[1:2], 48.0 * 128.0)
                list_ref[step : step + 1, 128 * part : 128 * part + 128] = code.astype(jnp.int32)

            if part == 0:
                write()
            else:
                pl.when(count + 8.0 > 128.0 * part)(write)


UNROLL = 8


def fill_table(all_ref, first_row, table_ref):
    def body(src, carry):
        for row in range(48):
            wide = jnp.broadcast_to(all_ref[src, first_row + row : first_row + row + 1, :] * SCALE, (8, 128))
            table_ref[src * 16 + row % 16, row // 16] = pltpu.roll(wide, 0, 1, stride=1, stride_axis=0)
        return carry

    lax.fori_loop(0, 8, body, 0)


def pair_loop(list_ref, step, me, table_ref, force_ref):
    force_ref[...] = jnp.zeros_like(force_ref)

    def one(q):
        code = list_ref[step, q]
        slot = lax.shift_right_logical(code, 7)
        r = code & 127
        p = jnp.minimum(slot + (16 * me - 16), 127)
        xi = [jnp.broadcast_to(table_ref[p, c, 0:1, :], (8, 128)) for c in range(3)]
        xj = [table_ref[r, c] for c in range(3)]
        acc = [jnp.zeros((8, 128), F32)] * 3
        for k in range(16):
            diff = [xi[c] - roll_last(xj[c], 8 * k) for c in range(3)]
            dist = diff[0] * diff[0] + diff[1] * diff[1] + diff[2] * diff[2]
            w = jnp.exp2(-dist)
            acc = [acc[c] + w * diff[c] for c in range(3)]
        return slot, acc

    def body(g, carry):
        done = [one(g * UNROLL + u) for u in range(UNROLL)]
        for slot, acc in done:
            for c in range(3):
                force_ref[slot, c] += acc[c]
        return carry

    lax.fori_loop(0, (list_ref[4 + step, 0] + (UNROLL - 1)) // UNROLL, body, 0)


def row_and_lane(ids):
    line = jnp.floor(ids * (1.0 / 128.0))
    lane = ids - 128.0 * line
    i = jnp.floor((line + 0.5) * (1.0 / 12.0))
    return 8.0 * line - 95.0 * i, lane


def one_hot(at, rows):
    return jnp.where(iota((rows, 128), 0).astype(F32) == at, 1.0, 0.0)


def block_force(force_ref, slot, c):
    return jnp.sum(force_ref[slot, c], axis=0, keepdims=True) * (1.0 / SCALE)


def scatter_own(force_ref, all_ref, me, lhs_ref, lanes_ref):
    for s in range(16):
        at = slice(128 * s, 128 * s + 128)
        row, lane = row_and_lane(all_ref[me, NODES + s : NODES + s + 1, :])
        hot = one_hot(row, 96)
        lanes_ref[:, at] = one_hot(lane, 128).astype(BF16)
        for c in range(3):
            hi, lo = split2(block_force(force_ref, 16 + s, c))
            lhs_ref[96 * c : 96 * c + 96, at] = (hot * hi.astype(F32)).astype(BF16)
            lhs_ref[288 + 96 * c : 384 + 96 * c, at] = (hot * lo.astype(F32)).astype(BF16)
    out = lax.dot_general(
        lhs_ref[...], lanes_ref[...], (((1,), (1,)), ((), ())), preferred_element_type=F32
    )
    return (out[:288] + out[288:]).reshape(3, 12, 8, 128)


def scatter_rim(force_ref, all_ref, me, square_ref, low, ups):
    square_ref[...] = jnp.zeros_like(square_ref)
    sides = ([(jnp.maximum(me - 1, 0), 0, (127.0,))] if low else []) + [
        (jnp.minimum(me + 1, 7), 32, ups)
    ]
    for src, first_slot, wants in sides:
        total = jnp.zeros((16, 128), F32)
        for s in range(16):
            row, lane = row_and_lane(all_ref[src, NODES + s : NODES + s + 1, :])
            hot = one_hot(row, 128).astype(BF16)
            lines = []
            for want in wants:
                for c in range(3):
                    f = jnp.where(lane == want, block_force(force_ref, first_slot + s, c), 0.0)
                    lines.append(f)
            lines += [jnp.zeros((8 - len(lines), 128), F32)]
            hi, lo = split2(jnp.concatenate(lines, axis=0))
            total = total + lax.dot_general(
                jnp.concatenate([hi, lo], axis=0), hot, (((1,), (1,)), ((), ())), preferred_element_type=F32
            )
        summed = total[0:8] + total[8:16]
        for w, want in enumerate(wants):
            for c in range(3):
                at = int(want + 8 * c) % 128
                square_ref[at : at + 1, :] = summed[3 * w + c : 3 * w + c + 1]
    return fill16(jnp.transpose(square_ref[...])[0:96].reshape(12, 8, 128))


def node_sum(elements):
    e = 0.125 * elements
    e = e + prev_z(e)
    e = e + prev_x(e)
    zero = jnp.zeros((1,) + e.shape[1:], F32)
    return jnp.concatenate([e, zero], axis=0) + jnp.concatenate([zero, e], axis=0)


def send_planes(planes, out_ref):
    count = len(planes)
    for n, plane in enumerate(planes):
        out_ref[n] = plane[:, :128]
    for g in range(0, count, 16):
        out_ref[count + g // 16] = pack([p[:, 128:] for p in planes[g : g + 16]])


def get_plane(ref, n, count):
    return both(ref[n], unpack(ref[count + n // 16], n % 16))


def row_plane(x, i):
    return fill16(x[:, i, :])


def first_contact_kernel(
    at_ref, list_ref, all_ref, load_ref, dens_ref, stiff_ref, alive_ref,
    fm_ref, c0_ref, m1_ref, up_ref, down_ref,
    table_ref, force_ref, lhs_ref, lanes_ref, square_ref,
):
    me = at_ref[2]
    planes = neighbour_planes(all_ref, PLANES, 4, me, square_ref, 12)
    fields = [load_ref[0], load_ref[1], load_ref[2], dens_ref[...]]
    sums = [node_sum(both(fill16(f), unpack(planes, n, 4))) for n, f in enumerate(fields)]
    m1 = both(fill16(stiff_ref[...] * alive_ref[1].astype(F32)), unpack(planes, 4, 4))
    zero = jnp.zeros((1, 16, 256), F32)
    m1 = jnp.concatenate([m1, zero], axis=0)
    m1_ref[...] = m1
    fm_ref[3] = sums[3]
    for c in range(3):
        fm_ref[c] = sums[c]
    fill_table(all_ref, 0, table_ref)
    pair_loop(list_ref, 0, me, table_ref, force_ref)
    own = scatter_own(force_ref, all_ref, me, lhs_ref, lanes_ref)
    rim = scatter_rim(force_ref, all_ref, me, square_ref, True, (0.0,))
    for c in range(3):
        full = jnp.concatenate([both(fill16(own[c]), unpack(rim, c)), zero], axis=0)
        c0_ref[c] = full
        fm_ref[c] = fm_ref[c] + full
    ups = [row_plane(fm_ref[n], 7) for n in range(4)] + [row_plane(fm_ref[n], 8) for n in range(4)]
    send_planes(ups + [row_plane(m1, 7)], up_ref)
    send_planes([row_plane(fm_ref[n], 0) for n in range(4)], down_ref)


def step_contact_kernel(at_ref, list_ref, all_ref, out_ref, table_ref, force_ref, lhs_ref, lanes_ref):
    me = at_ref[2]
    fill_table(all_ref, 0, table_ref)
    pair_loop(list_ref, 1, me, table_ref, force_ref)
    out_ref[...] = scatter_own(force_ref, all_ref, me, lhs_ref, lanes_ref)


def shift_rows(x, by):
    return pltpu.roll(x, by % x.shape[1], 1)


def x_extended_1(fm_ref, m1_ref, ups_ref, downs_ref, pick):
    lines = sorted(pick)
    row = iota((len(lines), 16, 256), 1)

    def lift(plane):
        return jnp.stack([jnp.broadcast_to(plane[j : j + 1], (16, 256)) for j in lines])

    def take(x):
        return jnp.stack([x[j] for j in lines])

    def extend(x, low, add, high):
        if add is not None:
            x = x + jnp.where(row == 0, lift(add), 0.0) + jnp.where(row == 8, lift(high), 0.0)
            x = jnp.where(row < 9, x, 0.0)
        else:
            x = jnp.where(row < 8, x, 0.0)
        return jnp.where(row == 0, lift(low), shift_rows(x, 1))

    out = [
        extend(
            take(fm_ref[n]),
            get_plane(ups_ref, n, 9),
            get_plane(ups_ref, 4 + n, 9),
            get_plane(downs_ref, n, 4),
        )
        for n in range(4)
    ]
    return out, extend(take(m1_ref[...]), get_plane(ups_ref, 8, 9), None, None)


def y_send_1_kernel(fm_ref, m1_ref, ups_ref, downs_ref, up_ref, down_ref):
    fields, m1 = x_extended_1(fm_ref, m1_ref, ups_ref, downs_ref, (0, 11, 12))
    send_planes([f[1] for f in fields] + [f[2] for f in fields] + [m1[1]], up_ref)
    send_planes([f[0] for f in fields], down_ref)


def stress_of(disp, modulus):
    grads = []
    for u in disp:
        s, d = u[1:] + u[:-1], u[1:] - u[:-1]
        sn = next_x(s)
        ss, xd = sn + s, sn - s
        yd = next_x(d) + d
        grads.append((xd + next_z(xd), yd + next_z(yd), next_z(ss) - ss))
    m = 0.25 * modulus
    exx, eyy, ezz = grads[0][0], grads[1][1], grads[2][2]
    trace = exx + eyy + ezz
    return (
        m * (2.0 * exx + trace),
        m * (2.0 * eyy + trace),
        m * (2.0 * ezz + trace),
        m * (grads[1][0] + grads[0][1]),
        m * (grads[2][1] + grads[1][2]),
        m * (grads[0][2] + grads[2][0]),
    )


def force_of(stress):
    xx, yy, zz, xy, yz, zx = stress
    out = []
    for a, b, c in ((xx, xy, zx), (xy, yy, yz), (zx, yz, zz)):
        az, bz, cz = a + prev_z(a), b + prev_z(b), prev_z(c) - c
        ac = (prev_x(az) - az) + (prev_x(cz) + cz)
        by = prev_x(bz) + bz
        out.append(-0.25 * ((ac[:-1] + ac[1:]) + (by[:-1] - by[1:])))
    return out


def gather_rows(disp, lanes_ref, rows_ref):
    hot = rows_ref[...]
    values = []
    for c in range(3):
        hi, lo = split2(disp[c])
        field = jnp.concatenate([hi, lo], axis=0)
        picked = lax.dot_general(field, hot, (((0,), (0,)), ((), ())), preferred_element_type=F32)
        values.append(jnp.sum(picked * lanes_ref[...].astype(F32), axis=0, keepdims=True))
    return values


def second_step_kernel(
    fm_ref, c0_ref, m1_ref, xu_ref, xd_ref, yu_ref, yd_ref, c1_ref, coords_ref, nodes_ref,
    out_ref, state_ref, rows_ref, lanes_ref, square_ref,
):
    fields, m1 = x_extended_1(fm_ref, m1_ref, xu_ref, xd_ref, range(13))
    zero = jnp.zeros((1, 16, 256), F32)
    for n in range(4):
        low, add = get_plane(yu_ref, n, 9), get_plane(yu_ref, 4 + n, 9)
        own = fields[n]
        fields[n] = jnp.concatenate(
            [low[None], (own[0] + add)[None], own[1:12], (own[12] + get_plane(yd_ref, n, 4))[None]],
            axis=0,
        )
    m1 = jnp.concatenate([get_plane(yu_ref, 8, 9)[None], m1[:12]], axis=0)
    mass = fields[3]
    inv = jnp.where(mass > 0.0, DT / jnp.where(mass > 0.0, mass, 1.0), 0.0)
    disp1 = [DT * (inv * fields[c]) for c in range(3)]
    force = force_of([jnp.concatenate([x, zero], axis=0) for x in stress_of(disp1, m1)])
    inv = inv[1:]
    row = iota((13, 16, 256), 1)
    good = (row > 0) & (row < 10)
    disp2s, vel2s = [], []
    for c in range(3):
        c1 = jnp.concatenate([fill16(c1_ref[c]), jnp.zeros((1, 16, 128), F32)], axis=0)
        c1 = shift_rows(both(c1, jnp.zeros((13, 16, 128), F32)), 1)
        total = fields[c][1:]
        accel = inv * (total - shift_rows(c0_ref[c], 1))
        vel2 = inv * total + inv * force[c] + (accel + inv * c1)
        disp2 = disp1[c][1:] + DT * vel2
        back = [shift_rows(jnp.where(good, x, 0.0), -1) for x in (disp2, vel2, accel)]
        disp2s.append(back[0])
        vel2s.append(back[1])
        state_ref[c] = back[0]
        state_ref[3 + c] = back[1]
        state_ref[6 + c] = back[2]
    state_ref[9] = shift_rows(jnp.where(good, inv, 0.0), -1)
    for s in range(16):
        at = slice(128 * s, 128 * s + 128)
        r, l = row_and_lane(nodes_ref[s : s + 1, :].astype(F32))
        hot = one_hot(r, 96).astype(BF16)
        rows_ref[0:96, at] = hot
        rows_ref[96:192, at] = hot
        lanes_ref[:, at] = one_hot(l, 128).astype(BF16)
    for first, disp in (
        (0, [shift_rows(d[1:13], -1)[:, :8, :128] for d in disp1]),
        (LATE, [d[0:12, :8, :128] for d in disp2s]),
    ):
        values = gather_rows([d.reshape(96, 128) for d in disp], lanes_ref, rows_ref)
        for c in range(3):
            block = jnp.concatenate(
                [values[c][:, 128 * s : 128 * s + 128] for s in range(16)], axis=0
            ) + coords_ref[c]
            for dest in range(8):
                out_ref[dest, first + 16 * c : first + 16 * c + 16, :] = block
    rows = planes_to_rows(pack([x[:, :, :128] for x in disp2s + vel2s], 5), square_ref)
    for dest in range(8):
        out_ref[dest, PLANES_2:ROWS_2, :] = rows


UP_LIST = (
    [(n, 0) for n in range(3)] + [(n, 1) for n in range(3)] + [(n, 1) for n in (3, 4, 5, 9)]
    + [(10, 0), (10, 1), (11, 1)]
)
DOWN_LIST = (
    [(n, p) for p in (0, 1, 2) for n in range(3)]
    + [(n, p) for p in (0, 1) for n in (3, 4, 5)]
    + [(n, 0) for n in (6, 7, 8)]
    + [(9, 0), (9, 1), (10, 0), (10, 1), (11, 0)]
)
UPS, DOWNS = len(UP_LIST), len(DOWN_LIST)


def plane_of(ref, listed, n, p):
    return get_plane(ref, listed.index((n, p)), len(listed)) if (n, p) in listed else None


def late_contact_kernel(
    at_ref, list_ref, first_ref, all_ref, state_ref, stiff_ref, alive_ref,
    own_ref, up_ref, down_ref,
    table_ref, force_ref, lhs_ref, lanes_ref, square_ref,
):
    me = at_ref[2]
    zplanes = neighbour_planes(all_ref, PLANES_2, 5, me, square_ref, 13)
    mplanes = neighbour_planes(first_ref, PLANES, 4, me, square_ref, 12)
    top = (iota((13, 16, 128), 2) == 0) & (me == 7)
    zero = jnp.zeros((1, 16, 256), F32)

    def with_rim(own, n):
        return both(own[:, :, :128], jnp.where(top, own[:, :, 128:], unpack(zplanes, n, 5)))

    inv = state_ref[9]
    own_ref[9] = inv
    for c in range(3):
        own_ref[c] = with_rim(state_ref[c], c)
        own_ref[3 + c] = with_rim(state_ref[3 + c], 3 + c) + state_ref[6 + c]
        own_ref[6 + c] = state_ref[6 + c]
    for n, step in ((10, 2), (11, 3)):
        m = both(fill16(stiff_ref[...] * alive_ref[step].astype(F32)), unpack(mplanes, 3 + step, 4))
        own_ref[n] = jnp.concatenate([m, zero], axis=0)
    for step, first_row, low, ups, n in ((2, 0, True, (0.0, 1.0), 3), (3, LATE, False, (0.0,), 6)):
        fill_table(all_ref, first_row, table_ref)
        pair_loop(list_ref, step, me, table_ref, force_ref)
        own = scatter_own(force_ref, first_ref, me, lhs_ref, lanes_ref)
        rim = scatter_rim(force_ref, first_ref, me, square_ref, low, ups)
        for c in range(3):
            full = both(fill16(own[c]), unpack(rim, c))
            own_ref[n + c, 0:12] = own_ref[n + c, 0:12] + own_ref[9, 0:12] * full
    send_planes([row_plane(own_ref[n], 6 + p) for n, p in UP_LIST], up_ref)
    send_planes([row_plane(own_ref[n], p) for n, p in DOWN_LIST], down_ref)


def x_extended_2(own_ref, ups_ref, downs_ref, at_last, lines):
    row = iota((len(lines), 16, 256), 1)
    keep = (row < 8) | ((row == 8) & at_last)

    def lift(plane):
        return jnp.stack([jnp.broadcast_to(plane[j : j + 1], (16, 256)) for j in lines])

    out = []
    for n in range(12):
        x = jnp.stack([own_ref[n, j] for j in lines])
        x = shift_rows(jnp.where(keep, x, 0.0), 2)
        for ref, listed, first, count in ((ups_ref, UP_LIST, 0, 2), (downs_ref, DOWN_LIST, 10, 3)):
            for p in range(count):
                got = plane_of(ref, listed, n, p)
                if got is not None:
                    add = lift(got)
                    if first + p == 10:
                        x = jnp.where((row == 10) & jnp.logical_not(at_last), add, x)
                    else:
                        x = jnp.where(row == first + p, add, x)
        out.append(x)
    return out


def y_send_2_kernel(at_ref, own_ref, ups_ref, downs_ref, up_ref, down_ref):
    fields = x_extended_2(own_ref, ups_ref, downs_ref, at_ref[0] == 7, (0, 1, 2, 10, 11))
    send_planes([fields[n][3 + p] for n, p in UP_LIST], up_ref)
    send_planes([fields[n][p] for n, p in DOWN_LIST], down_ref)


def last_kernel(at_ref, own_ref, xu_ref, xd_ref, yu_ref, yd_ref, vel_ref, stress_ref):
    fields = x_extended_2(own_ref, xu_ref, xd_ref, at_ref[0] == 7, range(13))
    y_last = at_ref[1] == 3
    none = jnp.zeros((16, 256), F32)
    wide = []
    for n in range(12):
        planes = [plane_of(yu_ref, UP_LIST, n, p) for p in (0, 1)]
        planes += [fields[n][j] for j in range(12)]
        after = [plane_of(yd_ref, DOWN_LIST, n, p) for p in (0, 1, 2)]
        after = [none if p is None else p for p in after]
        after[0] = jnp.where(y_last, fields[n][12], after[0])
        planes = [none if p is None else p for p in planes] + after
        wide.append(jnp.stack(planes))
    disp2, vh3, g3, inv, m2, m3 = wide[0:3], wide[3:6], wide[6:9], wide[9], wide[10], wide[11]
    force = force_of(stress_of(disp2, m2[:16]))
    vel3 = [vh3[c][1:16] + inv[1:16] * force[c] for c in range(3)]
    disp3 = [disp2[c][1:16] + DT * vel3[c] for c in range(3)]
    force = force_of(stress_of(disp3, m3[1:15]))
    vel4 = [vel3[c][1:14] + (inv[2:15] * force[c] + g3[c][2:15]) for c in range(3)]
    disp4 = [disp3[c][1:14] + DT * vel4[c] for c in range(3)]
    stress = stress_of(disp4, m3[2:14])
    for n in range(6):
        stress_ref[n] = shift_rows(stress[n][:, :, :128], -2)[:, :8, :]
    for c in range(3):
        s = vel4[c][1:] + vel4[c][:-1]
        s = s + next_x(s)
        s = s + next_z(s)
        vel_ref[c] = shift_rows(0.125 * s[:, :, :128], -2)[:, :8, :]


def call(kernel, outs, specs, scratch=()):
    return pl.pallas_call(
        kernel,
        out_shape=[jax.ShapeDtypeStruct(s, d) for s, d in outs],
        in_specs=specs,
        out_specs=[VMEM] * len(outs),
        scratch_shapes=list(scratch),
        compiler_params=PARAMS,
    )


def share(blocks):
    return lax.all_to_all(blocks, "gz", split_axis=0, concat_axis=0, tiled=True)


def neighbours(up, down, axis):
    count = lax.axis_size(axis)
    ahead = [(i, i + 1) for i in range(count - 1)]
    return lax.ppermute(up, axis, ahead), lax.ppermute(down, axis, [(j, i) for i, j in ahead])


TABLE = pltpu.VMEM((128, 3, 8, 128), F32)
FORCE = pltpu.VMEM((49, 3, 8, 128), F32)
LHS = pltpu.VMEM((576, 2048), BF16)
LANES = pltpu.VMEM((128, 2048), BF16)
SQUARE = pltpu.VMEM((128, 128), F32)


def per_device(stiffness, density, load, alive, surf_coords, surf_nodes, routes, pairs):
    at = jnp.stack([lax.axis_index(a) for a in ("gx", "gy", "gz")]).astype(jnp.int32)
    stiffness, density = jnp.swapaxes(stiffness, 0, 1), jnp.swapaxes(density, 0, 1)
    load, alive = jnp.swapaxes(load, 1, 2), jnp.swapaxes(alive, 1, 2)
    coords = jnp.swapaxes(surf_coords, 0, 1)
    pairs = jnp.swapaxes(pairs[:, 0], 1, 2)
    (payload,) = call(prep_kernel, [((8, ROWS_1, 128), F32)], [SMEM] + [VMEM] * 8, [SQUARE])(
        at, coords, routes, pairs, surf_nodes, stiffness, density, load, alive
    )
    everyone = share(payload)
    (lists,) = call(plan_kernel, [((8, 512), jnp.int32)], [SMEM, VMEM])(at, everyone)
    fm, c0, m1, up, down = call(
        first_contact_kernel,
        [((4, 13, 16, 256), F32), ((3, 13, 16, 256), F32), ((13, 16, 256), F32), ((10, 16, 128), F32),
         ((5, 16, 128), F32)],
        [SMEM, SMEM] + [VMEM] * 5,
        [TABLE, FORCE, LHS, LANES, SQUARE],
    )(at, lists, everyone, load, density, stiffness, alive)
    xu, xd = neighbours(up, down, "gx")
    (c1,) = call(
        step_contact_kernel, [((3, 12, 8, 128), F32)], [SMEM, SMEM, VMEM], [TABLE, FORCE, LHS, LANES]
    )(at, lists, everyone)
    up, down = call(y_send_1_kernel, [((10, 16, 128), F32), ((5, 16, 128), F32)], [VMEM] * 4)(
        fm, m1, xu, xd
    )
    yu, yd = neighbours(up, down, "gy")
    payload, state = call(
        second_step_kernel,
        [((8, ROWS_2, 128), F32), ((10, 13, 16, 256), F32)],
        [VMEM] * 10,
        [pltpu.VMEM((192, 2048), BF16), LANES, SQUARE],
    )(fm, c0, m1, xu, xd, yu, yd, c1, coords, surf_nodes)
    late = share(payload)
    own, up, down = call(
        late_contact_kernel,
        [((12, 13, 16, 256), F32), ((UPS + 1, 16, 128), F32), ((DOWNS + 2, 16, 128), F32)],
        [SMEM, SMEM] + [VMEM] * 5,
        [TABLE, FORCE, LHS, LANES, SQUARE],
    )(at, lists, everyone, late, state, stiffness, alive)
    xu, xd = neighbours(up, down, "gx")
    up, down = call(
        y_send_2_kernel,
        [((UPS + 1, 16, 128), F32), ((DOWNS + 2, 16, 128), F32)],
        [SMEM] + [VMEM] * 3,
    )(at, own, xu, xd)
    yu, yd = neighbours(up, down, "gy")
    vel, stress = call(
        last_kernel,
        [((3, 12, 8, 128), F32), ((6, 12, 8, 128), F32)],
        [SMEM] + [VMEM] * 5,
    )(at, own, xu, xd, yu, yd)
    return jnp.swapaxes(vel, 1, 2), jnp.swapaxes(stress, 1, 2)


def solution(mesh):
    return jax.shard_map(
        per_device,
        mesh=mesh,
        in_specs=(
            P("gx", "gy", "gz"),
            P("gx", "gy", "gz"),
            P(None, "gx", "gy", "gz"),
            P(None, "gx", "gy", "gz"),
            P(("gx", "gy", "gz"), None, None),
            P(("gx", "gy", "gz"), None),
            P(None, ("gx", "gy", "gz")),
            P(None, ("gx", "gy", "gz"), None, None),
        ),
        out_specs=(P(None, "gx", "gy", "gz"), P(None, "gx", "gy", "gz")),
        check_vma=False,
    )
```

time: 181 us -> 159 us (0.88)
  the two profiles are of different devices: /device:TPU:74 before, /device:TPU:80 now
where the time goes in v2:
time: 159 us; the launch traced here: 158 us
  Pallas kernels  67.5 us (42%)
  blocking collectives  52 us (33%)
  starting transfers between devices  24.4 us (15%)
  waiting for transfers between devices  9.33 us (6%)
  local copies, waits for them, and re-layouts  3.38 us (2%)
    all_to_all x2, blocking collectives, share(): return lax.all_to_all(blocks, 'gz', split_axis=0, concat_axis=0, tiled=True)  52 us
    pallas_call x1, Pallas kernels, per_device(): call(late_contact_kernel, [((12, 13, 16, 256), F32), ((UPS + 1, 16, 128),...  23.4 us
    ppermute x4, starting transfers between devices, neighbours(): lax.ppermute(down, axis, [(j, i) for i, j in ahead])  14.8 us
    pallas_call x1, Pallas kernels, per_device(): call(first_contact_kernel, [((4, 13, 16, 256), F32), ((3, 13, 16, 256), F...  13.4 us
    ppermute x4, starting transfers between devices, neighbours(): lax.ppermute(up, axis, ahead)  9.67 us
    ppermute x4, waiting for transfers between devices, neighbours(): lax.ppermute(up, axis, ahead)  7.36 us
    pallas_call x1, Pallas kernels, per_device(): call(last_kernel, [((3, 12, 8, 128), F32), ((6, 12, 8, 128), F32)], [SMEM...  6.59 us
    pallas_call x1, Pallas kernels, per_device(): call(step_contact_kernel, [((3, 12, 8, 128), F32)], [SMEM, SMEM, VMEM], [...  6.51 us
  transfers between devices with their start and end apart: 8, of which 3 were waited for; matrix products, arithmetic and copies ran while one was open for 0% of the time, Pallas kernels for 4%

profile of v2, /device:TPU:80, one launch (start us, length us, event | category | flops | bytes accessed | tf_op | source)
XLA Modules:
  0.0 158.0 jit_solution(2906626226654831120)
XLA Ops:
  0.6 0.6 pad_add_fusion.at_ref
  1.3 2.2 %shard_map.95 = f32[8,104,128]{2,1,0:T(8,128)} custom-call(s32[3]{0:T(128)} %pad_add_fusion.at_ref, f32[3,16,128]{2,1,0:T(8,128)} %bitcast.23, s32[4,16]{1,0:T(4,128)} %routes_ref.1, s32[4,2,64]{2,1,0:T(2,128)} %bitcast.25, s32[16,128]{1,0:T(8,128)} %nodes_ref.3, f32[12,8,128]{2,1,0:T(8,128)} %bitcast.18, f32[12,8,128]{2,1,0:T(8,128)} %bitcast.21, ...), custom_call_target="tpu_custom_call" | custom-call | tf_op jit(solution)/shard_map/pallas_call | solution.py:666
  3.4 26.8 %all_to_all.10.all_ref.first_ref = f32[8,104,128]{2,1,0:T(8,128)} all-to-all(f32[8,104,128]{2,1,0:T(8,128)} %shard_map.95), channel_id=1, replica_groups=mesh['gx'=8,'gy'=4,'gz'=8] {'gz'}, dimensions={0} | all-to-all | bytes 851968 | tf_op jit(solution)/shard_map/all_to_all | solution.py:644
  30.2 4.2 %shard_map.96.list_ref = s32[8,512]{1,0:T(8,128)} custom-call(s32[3]{0:T(128)} %pad_add_fusion.at_ref, f32[8,104,128]{2,1,0:T(8,128)} %all_to_all.10.all_ref.first_ref), custom_call_target="tpu_custom_call" | custom-call | tf_op jit(solution)/shard_map/pallas_call | solution.py:670
  34.4 13.4 %shard_map.97 = (f32[4,13,16,256]{3,2,1,0:T(8,128)}, f32[3,13,16,256]{3,2,1,0:T(8,128)}, f32[13,16,256]{2,1,0:T(8,128)}, f32[10,16,128]{2,1,0:T(8,128)}, f32[5,16,128]{2,1,0:T(8,128)}) custom-call(s32[3]{0:T(128)} %pad_add_fusion.at_ref, s32[8,512]{1,0:T(8,128)} %shard_map.96.list_ref, f32[8,104,128]{2,1,0:T(8,128)} %all_to_all.10.all_ref.first_ref, ...), custom_call_target="tpu_custom_call" | custom-call | tf_op jit(solution)/shard_map/pallas_call | solution.py:671
  47.8 1.9 %collective-permute-start = (f32[10,16,128]{2,1,0:T(8,128)}, f32[10,16,128]{2,1,0:T(8,128)S(1)}, u32[]{:S(2)}, u32[]{:S(2)}) collective-permute-start(f32[10,16,128]{2,1,0:T(8,128)} %get-tuple-element.21), channel_id=1, source_target_pairs={{0,32},{32,64},{64,96},{96,128},{128,160},{160,192},{192,224},{1,3... | collective-permute-start | bytes 245768 | tf_op jit(solution)/shard_map/ppermute | solution.py:650
  49.8 3.6 %collective-permute-start.1 = (f32[5,16,128]{2,1,0:T(8,128)}, f32[5,16,128]{2,1,0:T(8,128)S(1)}, u32[]{:S(2)}, u32[]{:S(2)}) collective-permute-start(f32[5,16,128]{2,1,0:T(8,128)} %get-tuple-element.22), channel_id=1, source_target_pairs={{32,0},{64,32},{96,64},{128,96},{160,128},{192,160},{224,192},{33,... | collective-permute-start | bytes 122888 | tf_op jit(solution)/shard_map/ppermute | solution.py:650
  53.4 2.0 %collective-permute-done.1.downs_ref.xd_ref = f32[5,16,128]{2,1,0:T(8,128)S(1)} collective-permute-done((f32[5,16,128]{2,1,0:T(8,128)}, f32[5,16,128]{2,1,0:T(8,128)S(1)}, u32[]{:S(2)}, u32[]{:S(2)}) %collective-permute-start.1) | collective-permute-done | bytes 40992 | tf_op jit(solution)/shard_map/ppermute | solution.py:650
  55.4 0.0 copy-start.4
  55.4 0.0 collective-permute-done.ups_ref.xu_ref
  55.4 0.0 copy-start.2
  55.4 0.6 copy-done.4
  56.0 0.0 copy-done.2
  56.0 2.1 %shard_map.98 = (f32[10,16,128]{2,1,0:T(8,128)}, f32[5,16,128]{2,1,0:T(8,128)}) custom-call(f32[4,13,16,256]{3,2,1,0:T(8,128)} %get-tuple-element.18.fm_ref, f32[13,16,256]{2,1,0:T(8,128)} %get-tuple-element.20.m1_ref, f32[10,16,128]{2,1,0:T(8,128)} %copy-done.2, f32[5,16,128]{2,1,0:T(8,128)} %copy-done.4), custom_call_target="tpu_custom_call" | custom-call | tf_op jit(solution)/shard_map/pallas_call | solution.py:682
  58.1 1.9 %collective-permute-start.2 = (f32[10,16,128]{2,1,0:T(8,128)}, f32[10,16,128]{2,1,0:T(8,128)S(1)}, u32[]{:S(2)}, u32[]{:S(2)}) collective-permute-start(f32[10,16,128]{2,1,0:T(8,128)} %get-tuple-element.23), channel_id=1, source_target_pairs={{0,8},{8,16},{16,24},{1,9},{9,17},{17,25},{2,10},{10,18},{18,26},{... | collective-permute-start | bytes 245768 | tf_op jit(solution)/shard_map/ppermute | solution.py:650
  60.0 3.9 %collective-permute-start.3 = (f32[5,16,128]{2,1,0:T(8,128)}, f32[5,16,128]{2,1,0:T(8,128)S(1)}, u32[]{:S(2)}, u32[]{:S(2)}) collective-permute-start(f32[5,16,128]{2,1,0:T(8,128)} %get-tuple-element.24), channel_id=1, source_target_pairs={{8,0},{16,8},{24,16},{9,1},{17,9},{25,17},{10,2},{18,10},{26,18},{... | collective-permute-start | bytes 122888 | tf_op jit(solution)/shard_map/ppermute | solution.py:650
  64.0 6.5 %shard_map.99.c1_ref = f32[3,12,8,128]{3,2,1,0:T(8,128)} custom-call(s32[3]{0:T(128)} %pad_add_fusion.at_ref, s32[8,512]{1,0:T(8,128)} %shard_map.96.list_ref, f32[8,104,128]{2,1,0:T(8,128)} %all_to_all.10.all_ref.first_ref), custom_call_target="tpu_custom_call" | custom-call | tf_op jit(solution)/shard_map/pallas_call | solution.py:679
  70.5 0.0 collective-permute-done.3.yd_ref
  70.5 0.0 copy-start.7
  70.5 0.0 collective-permute-done.2.yu_ref
  70.5 0.0 copy-start.6
  70.5 0.6 copy-done.7
  71.1 0.0 copy-done.6
  71.1 6.4 %shard_map.100 = (f32[8,128,128]{2,1,0:T(8,128)}, f32[10,13,16,256]{3,2,1,0:T(8,128)}) custom-call(f32[4,13,16,256]{3,2,1,0:T(8,128)} %get-tuple-element.18.fm_ref, f32[3,13,16,256]{3,2,1,0:T(8,128)} %get-tuple-element.19.c0_ref, f32[13,16,256]{2,1,0:T(8,128)} %get-tuple-element.20.m1_ref, f32[10,16,128]{2,1,0:T(8,128)} %copy-done.2, ...), custom_call_target="tpu_custom_call" | custom-call | tf_op jit(solution)/shard_map/pallas_call | solution.py:686
  77.5 25.2 %all_to_all.11.all_ref = f32[8,128,128]{2,1,0:T(8,128)} all-to-all(f32[8,128,128]{2,1,0:T(8,128)} %get-tuple-element.25), channel_id=1, replica_groups=mesh['gx'=8,'gy'=4,'gz'=8] {'gz'}, dimensions={0} | all-to-all | bytes 1048576 | tf_op jit(solution)/shard_map/all_to_all | solution.py:644
  102.7 23.4 %shard_map.101 = (f32[12,13,16,256]{3,2,1,0:T(8,128)}, f32[14,16,128]{2,1,0:T(8,128)}, f32[25,16,128]{2,1,0:T(8,128)}) custom-call(s32[3]{0:T(128)} %pad_add_fusion.at_ref, s32[8,512]{1,0:T(8,128)} %shard_map.96.list_ref, f32[8,104,128]{2,1,0:T(8,128)} %all_to_all.10.all_ref.first_ref, f32[8,128,128]{2,1,0:T(8,128)} %all_to_all.11.all_ref, ...), custom_call_target="tpu_custom_call" | custom-call | tf_op jit(solution)/shard_map/pallas_call | solution.py:693
  126.1 5.3 %collective-permute-start.5 = (f32[25,16,128]{2,1,0:T(8,128)}, f32[25,16,128]{2,1,0:T(8,128)S(1)}, u32[]{:S(2)}, u32[]{:S(2)}) collective-permute-start(f32[25,16,128]{2,1,0:T(8,128)} %get-tuple-element.29), channel_id=1, source_target_pairs={{32,0},{64,32},{96,64},{128,96},{160,128},{192,160},{224,192},{33,... | collective-permute-start | bytes 614408 | tf_op jit(solution)/shard_map/ppermute | solution.py:650
  131.4 1.9 %collective-permute-start.4 = (f32[14,16,128]{2,1,0:T(8,128)}, f32[14,16,128]{2,1,0:T(8,128)S(1)}, u32[]{:S(2)}, u32[]{:S(2)}) collective-permute-start(f32[14,16,128]{2,1,0:T(8,128)} %get-tuple-element.28), channel_id=1, source_target_pairs={{0,32},{32,64},{64,96},{96,128},{128,160},{160,192},{192,224},{1,3... | collective-permute-start | bytes 344072 | tf_op jit(solution)/shard_map/ppermute | solution.py:650
  133.3 4.4 %collective-permute-done.4.ups_ref.xu_ref = f32[14,16,128]{2,1,0:T(8,128)S(1)} collective-permute-done((f32[14,16,128]{2,1,0:T(8,128)}, f32[14,16,128]{2,1,0:T(8,128)S(1)}, u32[]{:S(2)}, u32[]{:S(2)}) %collective-permute-start.4) | collective-permute-done | bytes 114720 | tf_op jit(solution)/shard_map/ppermute | solution.py:650
  137.7 0.0 copy-start.1
  137.7 0.0 collective-permute-done.5.downs_ref.xd_ref
  137.7 0.0 copy-start
  137.7 0.6 copy-done.1
  138.3 0.1 copy-done
  138.5 2.8 %shard_map.102 = (f32[14,16,128]{2,1,0:T(8,128)}, f32[25,16,128]{2,1,0:T(8,128)}) custom-call(s32[3]{0:T(128)} %pad_add_fusion.at_ref, f32[12,13,16,256]{3,2,1,0:T(8,128)} %get-tuple-element.27.own_ref, f32[14,16,128]{2,1,0:T(8,128)} %copy-done.1, f32[25,16,128]{2,1,0:T(8,128)} %copy-done), custom_call_target="tpu_custom_call" | custom-call | tf_op jit(solution)/shard_map/pallas_call | solution.py:700
  141.2 1.9 %collective-permute-start.7 = (f32[25,16,128]{2,1,0:T(8,128)}, f32[25,16,128]{2,1,0:T(8,128)S(1)}, u32[]{:S(2)}, u32[]{:S(2)}) collective-permute-start(f32[25,16,128]{2,1,0:T(8,128)} %get-tuple-element.31), channel_id=1, source_target_pairs={{8,0},{16,8},{24,16},{9,1},{17,9},{25,17},{10,2},{18,10},{26,18},{... | collective-permute-start | bytes 614408 | tf_op jit(solution)/shard_map/ppermute | solution.py:650
  143.1 3.9 %collective-permute-start.6 = (f32[14,16,128]{2,1,0:T(8,128)}, f32[14,16,128]{2,1,0:T(8,128)S(1)}, u32[]{:S(2)}, u32[]{:S(2)}) collective-permute-start(f32[14,16,128]{2,1,0:T(8,128)} %get-tuple-element.30), channel_id=1, source_target_pairs={{0,8},{8,16},{16,24},{1,9},{9,17},{17,25},{2,10},{10,18},{18,26},{... | collective-permute-start | bytes 344072 | tf_op jit(solution)/shard_map/ppermute | solution.py:650
  147.1 3.0 %collective-permute-done.6.yu_ref = f32[14,16,128]{2,1,0:T(8,128)S(1)} collective-permute-done((f32[14,16,128]{2,1,0:T(8,128)}, f32[14,16,128]{2,1,0:T(8,128)S(1)}, u32[]{:S(2)}, u32[]{:S(2)}) %collective-permute-start.6) | collective-permute-done | bytes 114720 | tf_op jit(solution)/shard_map/ppermute | solution.py:650
  150.0 0.0 copy-start.5
  150.0 0.0 collective-permute-done.7.yd_ref
  150.0 0.7 copy-done.5
  150.7 0.0 copy-start.3
  150.7 0.7 copy-done.3
  151.4 6.6 %shard_map.103 = (f32[3,12,8,128]{3,2,1,0:T(8,128)}, f32[6,12,8,128]{3,2,1,0:T(8,128)}) custom-call(s32[3]{0:T(128)} %pad_add_fusion.at_ref, f32[12,13,16,256]{3,2,1,0:T(8,128)} %get-tuple-element.27.own_ref, f32[14,16,128]{2,1,0:T(8,128)} %copy-done.1, f32[25,16,128]{2,1,0:T(8,128)} %copy-done, f32[14,16,128]{2,1,0:T(8,128)} %copy-done.5, ...), custom_call_target="tpu_custom_call" | custom-call | tf_op jit(solution)/shard_map/pallas_call | solution.py:706
Async XLA Ops:
  47.8 7.5 %collective-permute-start = (f32[10,16,128]{2,1,0:T(8,128)}, f32[10,16,128]{2,1,0:T(8,128)S(1)}, u32[]{:S(2)}, u32[]{:S(2)}) collective-permute-start(f32[10,16,128]{2,1,0:T(8,128)} %get-tuple-element.21), channel_id=1, source_target_pairs={{0,32},{32,64},{64,96},{96,128},{128,160},{160,192},{192,224},{1,3... | collective-permute-start | bytes 245768 | tf_op jit(solution)/shard_map/ppermute | solution.py:650
  49.8 5.6 %collective-permute-start.1 = (f32[5,16,128]{2,1,0:T(8,128)}, f32[5,16,128]{2,1,0:T(8,128)S(1)}, u32[]{:S(2)}, u32[]{:S(2)}) collective-permute-start(f32[5,16,128]{2,1,0:T(8,128)} %get-tuple-element.22), channel_id=1, source_target_pairs={{32,0},{64,32},{96,64},{128,96},{160,128},{192,160},{224,192},{33,... | collective-permute-start | bytes 122888 | tf_op jit(solution)/shard_map/ppermute | solution.py:650
  55.4 0.6 copy-start.4
  55.4 0.6 copy-start.2
  58.1 12.4 %collective-permute-start.2 = (f32[10,16,128]{2,1,0:T(8,128)}, f32[10,16,128]{2,1,0:T(8,128)S(1)}, u32[]{:S(2)}, u32[]{:S(2)}) collective-permute-start(f32[10,16,128]{2,1,0:T(8,128)} %get-tuple-element.23), channel_id=1, source_target_pairs={{0,8},{8,16},{16,24},{1,9},{9,17},{17,25},{2,10},{10,18},{18,26},{... | collective-permute-start | bytes 245768 | tf_op jit(solution)/shard_map/ppermute | solution.py:650
  60.0 10.4 %collective-permute-start.3 = (f32[5,16,128]{2,1,0:T(8,128)}, f32[5,16,128]{2,1,0:T(8,128)S(1)}, u32[]{:S(2)}, u32[]{:S(2)}) collective-permute-start(f32[5,16,128]{2,1,0:T(8,128)} %get-tuple-element.24), channel_id=1, source_target_pairs={{8,0},{16,8},{24,16},{9,1},{17,9},{25,17},{10,2},{18,10},{26,18},{... | collective-permute-start | bytes 122888 | tf_op jit(solution)/shard_map/ppermute | solution.py:650
  70.5 0.6 copy-start.7
  70.5 0.6 copy-start.6
  126.1 11.6 %collective-permute-start.5 = (f32[25,16,128]{2,1,0:T(8,128)}, f32[25,16,128]{2,1,0:T(8,128)S(1)}, u32[]{:S(2)}, u32[]{:S(2)}) collective-permute-start(f32[25,16,128]{2,1,0:T(8,128)} %get-tuple-element.29), channel_id=1, source_target_pairs={{32,0},{64,32},{96,64},{128,96},{160,128},{192,160},{224,192},{33,... | collective-permute-start | bytes 614408 | tf_op jit(solution)/shard_map/ppermute | solution.py:650
  131.4 6.3 %collective-permute-start.4 = (f32[14,16,128]{2,1,0:T(8,128)}, f32[14,16,128]{2,1,0:T(8,128)S(1)}, u32[]{:S(2)}, u32[]{:S(2)}) collective-permute-start(f32[14,16,128]{2,1,0:T(8,128)} %get-tuple-element.28), channel_id=1, source_target_pairs={{0,32},{32,64},{64,96},{96,128},{128,160},{160,192},{192,224},{1,3... | collective-permute-start | bytes 344072 | tf_op jit(solution)/shard_map/ppermute | solution.py:650
  137.7 0.6 copy-start.1
  137.7 0.8 copy-start
  141.2 8.8 %collective-permute-start.7 = (f32[25,16,128]{2,1,0:T(8,128)}, f32[25,16,128]{2,1,0:T(8,128)S(1)}, u32[]{:S(2)}, u32[]{:S(2)}) collective-permute-start(f32[25,16,128]{2,1,0:T(8,128)} %get-tuple-element.31), channel_id=1, source_target_pairs={{8,0},{16,8},{24,16},{9,1},{17,9},{25,17},{10,2},{18,10},{26,18},{... | collective-permute-start | bytes 614408 | tf_op jit(solution)/shard_map/ppermute | solution.py:650
  143.1 6.9 %collective-permute-start.6 = (f32[14,16,128]{2,1,0:T(8,128)}, f32[14,16,128]{2,1,0:T(8,128)S(1)}, u32[]{:S(2)}, u32[]{:S(2)}) collective-permute-start(f32[14,16,128]{2,1,0:T(8,128)} %get-tuple-element.30), channel_id=1, source_target_pairs={{0,8},{8,16},{16,24},{1,9},{9,17},{17,25},{2,10},{10,18},{18,26},{... | collective-permute-start | bytes 344072 | tf_op jit(solution)/shard_map/ppermute | solution.py:650
  150.0 0.7 copy-start.5
  150.7 0.7 copy-start.3

commit v3 on v2

--- a/solution.py
+++ b/solution.py
@@ -135,36 +135,41 @@
         out_ref[dest, PLANES:ROWS_1, :] = rows
 
 
-def plan_kernel(at_ref, all_ref, list_ref):
+def plan_kernel(at_ref, all_ref, list_ref, task_ref):
     me = at_ref[2]
     lane = iota((1, 128), 1)
     block_of = iota((128, 128), 0).astype(F32)
     eye = iota((128, 128), 0) == iota((128, 128), 1)
     upper = (iota((128, 128), 0) < iota((128, 128), 1)).astype(BF16)
     place = iota((128, 128), 0).astype(F32)
-    own, low, up0, up1 = [], [], [], []
-    for src in range(8):
+    row8 = iota((8, 128), 0)
+    src_of = iota((128, 1), 0) // 16
+
+    def nodes_at(src, wants, real):
         ids = all_ref[src, NODES : NODES + 16, :]
         k = ids - 128.0 * jnp.floor(ids * (1.0 / 128.0))
-
-        def some(want):
-            return jnp.max(jnp.where(k == want, 1.0, 0.0), axis=1, keepdims=True)
-
-        one = jnp.ones((16, 1), F32)
-        own.append(one * jnp.where(me == src, 1.0, 0.0))
-        low.append(some(127.0) * jnp.where(me == src + 1, 1.0, 0.0))
-        is_up = jnp.where(me == src - 1, 1.0, 0.0)
-        up0.append(some(0.0) * is_up)
-        up1.append(some(1.0) * is_up)
-    own, low, up0, up1 = [jnp.concatenate(x, axis=0) for x in (own, low, up0, up1)]
-    allowed = [own + low + up0, own, own + low + jnp.maximum(up0, up1), own + up0]
+        hit = k == wants[0]
+        for want in wants[1:]:
+            hit = hit | (k == want)
+        count = jnp.sum(jnp.where(hit, 1.0, 0.0), axis=1, keepdims=True)
+        return jnp.where(src_of == real, jnp.concatenate([count] * 8, axis=0), 0.0)
+
+    low = nodes_at(jnp.maximum(me - 1, 0), (127.0,), me - 1)
+    up = jnp.minimum(me + 1, 7)
+    up0, up01 = nodes_at(up, (0.0,), me + 1), nodes_at(up, (0.0, 1.0), me + 1)
+    rims = {0: low + up0, 2: low + up01, 3: up0}
+    mine_first = (16 * me).astype(F32)
+
+    def prefix(x):
+        return jnp.dot(jnp.broadcast_to(x, (8, 128)).astype(BF16), upper, preferred_element_type=F32)[0:1]
+
     for step in range(4):
         keys = all_ref[0, KEYS + step : KEYS + 1 + step, :]
         for src in range(1, 8):
             keys = keys + all_ref[src, KEYS + step : KEYS + 1 + step, :]
         key_col = jnp.sum(jnp.where(eye, keys, 0.0), axis=1, keepdims=True)
-        first_col = jnp.where(allowed[step] > 0.0, key_col, -1.0)
         base = jnp.zeros((1, 1), F32)
+        tasks = jnp.zeros((1, 1), F32)
         spots, codes = [], []
         for row in range(4):
             even = all_ref[2 * row, PAIRS + step : PAIRS + 1 + step, :]
@@ -173,32 +178,38 @@
             first = jnp.where(left, even, pltpu.roll(odd, 64, 1))
             second = jnp.where(left, pltpu.roll(even, 64, 1), odd)
             box = jnp.where(left, 64.0 * row, 64.0 * row + 32.0)
-            hit_first = first_col == first + box
+            hit_first = key_col == first + box
             hit_second = key_col == second + box
-            p_block = jnp.sum(jnp.where(hit_first, block_of, 0.0), axis=0, keepdims=True)
-            r_block = jnp.sum(jnp.where(hit_second, block_of, 0.0), axis=0, keepdims=True)
-            live = jnp.sum(jnp.where(hit_first, 1.0, 0.0), axis=0, keepdims=True) * jnp.sum(
-                jnp.where(hit_second, 1.0, 0.0), axis=0, keepdims=True
-            )
-            p_slot = p_block - (16 * me - 16).astype(F32)
-            mine = live > 0.0
+            p_block = jnp.sum(jnp.where(hit_first, block_of + 1.0, 0.0), axis=0, keepdims=True) - 1.0
+            r_block = jnp.sum(jnp.where(hit_second, block_of + 1.0, 0.0), axis=0, keepdims=True) - 1.0
+            p_slot = p_block - mine_first
+            live = r_block >= 0.0
+            mine = live & (p_slot >= 0.0) & (p_slot < 16.0)
             sel = jnp.where(mine, 1.0, 0.0)
-            before = jnp.dot(
-                jnp.broadcast_to(sel, (8, 128)).astype(BF16), upper, preferred_element_type=F32
-            )[0:1]
-            spots.append(jnp.where(mine, before + base, -1.0))
+            spots.append(jnp.where(mine, prefix(sel) + base, -1.0))
             base = base + jnp.sum(sel, axis=1, keepdims=True)
             code = jnp.where(
-                iota((8, 128), 0) == 0,
-                jnp.broadcast_to(p_slot, (8, 128)),
-                jnp.broadcast_to(r_block, (8, 128)),
+                row8 == 0, jnp.broadcast_to(p_slot, (8, 128)), jnp.broadcast_to(r_block, (8, 128))
             )
             codes.append(jnp.where(jnp.broadcast_to(mine, (8, 128)), code, 0.0).astype(BF16))
+            if step in rims:
+                count = jnp.sum(jnp.where(hit_first, rims[step], 0.0), axis=0, keepdims=True)
+                count = jnp.where(live, count, 0.0)
+                start = prefix(count) + tasks
+                tasks = tasks + jnp.sum(count, axis=1, keepdims=True)
+                high = jnp.floor(start * (1.0 / 256.0))
+                rim_block = jnp.where(p_slot < 0.0, p_slot + 16.0, p_slot)
+                some = jnp.broadcast_to(count > 0.0, (8, 128))
+                table = jnp.zeros((8, 128), F32)
+                for n, line in enumerate((rim_block, r_block, high, start - 256.0 * high, start, count)):
+                    table = jnp.where(row8 == n, jnp.broadcast_to(line, (8, 128)), table)
+                task_ref[step, row] = jnp.where(some, table, 0.0)
         list_ref[4 + step : 5 + step, :] = jnp.broadcast_to(base, (1, 512)).astype(jnp.int32)
+        list_ref[8 + step : 9 + step, :] = jnp.broadcast_to(tasks, (1, 512)).astype(jnp.int32)
         count = jnp.max(base)
         for part in range(4):
 
-            def write(part=part, spots=spots, codes=codes, base=base):
+            def write(part=part, spots=spots, codes=codes, base=base, step=step):
                 total = jnp.zeros((8, 128), F32)
                 for row in range(4):
                     onehot = jnp.where(place == spots[row] - 128.0 * part, 1.0, 0.0).astype(BF16)
@@ -206,7 +217,7 @@
                         codes[row], onehot, (((1,), (1,)), ((), ())), preferred_element_type=F32
                     )
                 used = (lane + 128 * part).astype(F32) < base
-                code = jnp.where(used, total[0:1] * 128.0 + total[1:2], 48.0 * 128.0)
+                code = jnp.where(used, total[0:1] * 128.0 + total[1:2], 16.0 * 128.0)
                 list_ref[step : step + 1, 128 * part : 128 * part + 128] = code.astype(jnp.int32)
 
             if part == 0:
@@ -218,42 +229,51 @@
 UNROLL = 8
 
 
-def fill_table(all_ref, first_row, table_ref):
-    def body(src, carry):
-        for row in range(48):
-            wide = jnp.broadcast_to(all_ref[src, first_row + row : first_row + row + 1, :] * SCALE, (8, 128))
-            table_ref[src * 16 + row % 16, row // 16] = pltpu.roll(wide, 0, 1, stride=1, stride_axis=0)
-        return carry
-
-    lax.fori_loop(0, 8, body, 0)
-
-
-def pair_loop(list_ref, step, me, table_ref, force_ref):
+def pair_loop(list_ref, step, first_row, me, all_ref, turned_ref, force_ref, sum_ref):
     force_ref[...] = jnp.zeros_like(force_ref)
+    for c in range(3):
+        turned_ref[16, :, c] = jnp.zeros((4, 8, 128), F32)
+        for s in range(16):
+            wide = jnp.broadcast_to(all_ref[me, first_row + 16 * c + s : first_row + 16 * c + s + 1, :] * SCALE, (8, 128))
+            for a in range(4):
+                turned_ref[s, a, c] = roll_last(wide, 32 * a)
 
     def one(q):
         code = list_ref[step, q]
         slot = lax.shift_right_logical(code, 7)
-        r = code & 127
-        p = jnp.minimum(slot + (16 * me - 16), 127)
-        xi = [jnp.broadcast_to(table_ref[p, c, 0:1, :], (8, 128)) for c in range(3)]
-        xj = [table_ref[r, c] for c in range(3)]
-        acc = [jnp.zeros((8, 128), F32)] * 3
-        for k in range(16):
-            diff = [xi[c] - roll_last(xj[c], 8 * k) for c in range(3)]
-            dist = diff[0] * diff[0] + diff[1] * diff[1] + diff[2] * diff[2]
-            w = jnp.exp2(-dist)
-            acc = [acc[c] + w * diff[c] for c in range(3)]
-        return slot, acc
+        src = lax.shift_right_logical(code & 127, 4)
+        line = first_row + (code & 15)
+        xj = []
+        for c in range(3):
+            wide = jnp.broadcast_to(all_ref[src, pl.ds(line + 16 * c, 1), :] * SCALE, (8, 128))
+            wide = pltpu.roll(wide, 0, 1, stride=1, stride_axis=0)
+            xj.append([roll_last(wide, 8 * b) for b in range(4)])
+        out = []
+        for a in range(4):
+            xi = [turned_ref[slot, a, c] for c in range(3)]
+            acc = [None] * 3
+            for b in range(4):
+                diff = [xi[c] - xj[c][b] for c in range(3)]
+                dist = diff[0] * diff[0] + diff[1] * diff[1] + diff[2] * diff[2]
+                w = jnp.exp2(-dist)
+                acc = [w * diff[c] if b == 0 else acc[c] + w * diff[c] for c in range(3)]
+            out.append(acc)
+        return slot, out
 
     def body(g, carry):
         done = [one(g * UNROLL + u) for u in range(UNROLL)]
-        for slot, acc in done:
-            for c in range(3):
-                force_ref[slot, c] += acc[c]
+        for slot, out in done:
+            for a in range(4):
+                for c in range(3):
+                    force_ref[slot, a, c] += out[a][c]
         return carry
 
     lax.fori_loop(0, (list_ref[4 + step, 0] + (UNROLL - 1)) // UNROLL, body, 0)
+    for c in range(3):
+        total = force_ref[0:16, 0, c]
+        for a in range(1, 4):
+            total = total + roll_last(force_ref[0:16, a, c], -32 * a)
+        sum_ref[c] = jnp.sum(total, axis=1) * (1.0 / SCALE)
 
 
 def row_and_lane(ids):
@@ -267,18 +287,14 @@
     return jnp.where(iota((rows, 128), 0).astype(F32) == at, 1.0, 0.0)
 
 
-def block_force(force_ref, slot, c):
-    return jnp.sum(force_ref[slot, c], axis=0, keepdims=True) * (1.0 / SCALE)
-
-
-def scatter_own(force_ref, all_ref, me, lhs_ref, lanes_ref):
+def scatter_own(sum_ref, all_ref, me, lhs_ref, lanes_ref):
     for s in range(16):
         at = slice(128 * s, 128 * s + 128)
         row, lane = row_and_lane(all_ref[me, NODES + s : NODES + s + 1, :])
         hot = one_hot(row, 96)
         lanes_ref[:, at] = one_hot(lane, 128).astype(BF16)
         for c in range(3):
-            hi, lo = split2(block_force(force_ref, 16 + s, c))
+            hi, lo = split2(sum_ref[c, s : s + 1, :])
             lhs_ref[96 * c : 96 * c + 96, at] = (hot * hi.astype(F32)).astype(BF16)
             lhs_ref[288 + 96 * c : 384 + 96 * c, at] = (hot * lo.astype(F32)).astype(BF16)
     out = lax.dot_general(
@@ -287,31 +303,89 @@
     return (out[:288] + out[288:]).reshape(3, 12, 8, 128)
 
 
-def scatter_rim(force_ref, all_ref, me, square_ref, low, ups):
+def split3(x):
+    hi, rest = x.astype(BF16), x
+    rest = rest - hi.astype(F32)
+    mid = rest.astype(BF16)
+    return jnp.concatenate([hi, mid, (rest - mid.astype(F32)).astype(BF16)], axis=0)
+
+
+def contact_rim(list_ref, task_ref, step, first_row, me, pos_ref, ids_ref, rim, square_ref):
+    all_ref, near_ref, info_ref, sum_ref = rim
+    low, up = jnp.maximum(me - 1, 0), jnp.minimum(me + 1, 7)
+    for c in range(3):
+        at = first_row + 16 * c
+        block = jnp.concatenate([pos_ref[src, at : at + 16, :] for src in range(8)], axis=0)
+        all_ref[c] = split3(block * SCALE)
+        block = jnp.concatenate([pos_ref[low, at : at + 16, :], pos_ref[up, at : at + 16, :]], axis=0)
+        near_ref[c] = split3(block * SCALE)
+    ids = jnp.concatenate(
+        [ids_ref[low, NODES : NODES + 16, :], ids_ref[up, NODES : NODES + 16, :]], axis=0
+    )
+    line, lane = row_and_lane(ids)
+    below = iota((32, 128), 0) < 16
+    ghost = (below & (lane == 127.0)) | (jnp.logical_not(below) & (lane == 0.0))
+    if step == 2:
+        ghost = ghost | (jnp.logical_not(below) & (lane == 1.0))
+    upper = (iota((128, 128), 0) < iota((128, 128), 1)).astype(BF16)
+    rank = jnp.dot(jnp.where(ghost, 1.0, 0.0).astype(BF16), upper, preferred_element_type=F32)
+    info_ref[0] = jnp.where(ghost, rank, 255.0).astype(BF16)
+    info_ref[1] = line.astype(BF16)
+    info_ref[2] = jnp.where(below, 0.0, lane + 1.0).astype(BF16)
+    sum_ref[...] = jnp.zeros_like(sum_ref)
+    tasks = list_ref[8 + step, 0]
+
+    def pick(table, hot):
+        return lax.dot_general(table, hot, (((0,), (0,)), ((), ())), preferred_element_type=F32)
+
+    def body(part, carry):
+        first = part * 128
+        number = (iota((128, 128), 0) + first).astype(F32)
+        found = jnp.zeros((8, 128), F32)
+        for row in range(4):
+            entry = task_ref[step, row]
+            start, count = entry[4:5], entry[5:6]
+            hot = jnp.where((number >= start) & (number < start + count), 1.0, 0.0).astype(BF16)
+            found = found + lax.dot_general(
+                entry.astype(BF16), hot, (((1,), (1,)), ((), ())), preferred_element_type=F32
+            )
+        here = (iota((1, 128), 1) + first).astype(F32)
+        nth = here - (256.0 * found[2:3] + found[3:4])
+        live = here < tasks.astype(F32)
+        hot_p = jnp.where(iota((32, 128), 0).astype(F32) == found[0:1], 1.0, 0.0).astype(BF16)
+        hot_r = jnp.where(iota((128, 128), 0).astype(F32) == found[1:2], 1.0, 0.0).astype(BF16)
+        match = pick(info_ref[0], hot_p) == nth
+        line = jnp.sum(jnp.where(match, pick(info_ref[1], hot_p), 0.0), axis=0, keepdims=True)
+        plane = jnp.sum(jnp.where(match, pick(info_ref[2], hot_p), 0.0), axis=0, keepdims=True)
+        hot_p3 = jnp.concatenate([hot_p] * 3, axis=0)
+        hot_r3 = jnp.concatenate([hot_r] * 3, axis=0)
+        xi, xj = [], []
+        for c in range(3):
+            xi.append(jnp.sum(jnp.where(match, pick(near_ref[c], hot_p3), 0.0), axis=0, keepdims=True))
+            xj.append(pick(all_ref[c], hot_r3))
+        diff = [xi[c] - xj[c] for c in range(3)]
+        dist = diff[0] * diff[0] + diff[1] * diff[1] + diff[2] * diff[2]
+        w = jnp.exp2(-dist)
+        lines = []
+        for want in range(3):
+            for c in range(3):
+                f = jnp.sum(w * diff[c], axis=0, keepdims=True) * (1.0 / SCALE)
+                lines.append(jnp.where(live & (plane == want), f, 0.0))
+        lines.append(jnp.zeros((7, 128), F32))
+        hi, lo = split2(jnp.concatenate(lines, axis=0))
+        hot = one_hot(line, 128).astype(BF16)
+        got = lax.dot_general(
+            jnp.concatenate([hi, lo], axis=0), hot, (((1,), (1,)), ((), ())), preferred_element_type=F32
+        )
+        sum_ref[...] += got[0:16] + got[16:32]
+        return carry
+
+    lax.fori_loop(0, (tasks + 127) // 128, body, 0)
     square_ref[...] = jnp.zeros_like(square_ref)
-    sides = ([(jnp.maximum(me - 1, 0), 0, (127.0,))] if low else []) + [
-        (jnp.minimum(me + 1, 7), 32, ups)
-    ]
-    for src, first_slot, wants in sides:
-        total = jnp.zeros((16, 128), F32)
-        for s in range(16):
-            row, lane = row_and_lane(all_ref[src, NODES + s : NODES + s + 1, :])
-            hot = one_hot(row, 128).astype(BF16)
-            lines = []
-            for want in wants:
-                for c in range(3):
-                    f = jnp.where(lane == want, block_force(force_ref, first_slot + s, c), 0.0)
-                    lines.append(f)
-            lines += [jnp.zeros((8 - len(lines), 128), F32)]
-            hi, lo = split2(jnp.concatenate(lines, axis=0))
-            total = total + lax.dot_general(
-                jnp.concatenate([hi, lo], axis=0), hot, (((1,), (1,)), ((), ())), preferred_element_type=F32
-            )
-        summed = total[0:8] + total[8:16]
-        for w, want in enumerate(wants):
-            for c in range(3):
-                at = int(want + 8 * c) % 128
-                square_ref[at : at + 1, :] = summed[3 * w + c : 3 * w + c + 1]
+    for want, k in enumerate((127, 0, 1)):
+        for c in range(3):
+            at = (k + 8 * c) % 128
+            square_ref[at : at + 1, :] = sum_ref[3 * want + c : 3 * want + c + 1, :]
     return fill16(jnp.transpose(square_ref[...])[0:96].reshape(12, 8, 128))
 
 
@@ -340,9 +414,9 @@
 
 
 def first_contact_kernel(
-    at_ref, list_ref, all_ref, load_ref, dens_ref, stiff_ref, alive_ref,
+    at_ref, list_ref, task_ref, all_ref, load_ref, dens_ref, stiff_ref, alive_ref,
     fm_ref, c0_ref, m1_ref, up_ref, down_ref,
-    table_ref, force_ref, lhs_ref, lanes_ref, square_ref,
+    turned_ref, force_ref, sum_ref, lhs_ref, lanes_ref, square_ref, *rim,
 ):
     me = at_ref[2]
     planes = neighbour_planes(all_ref, PLANES, 4, me, square_ref, 12)
@@ -355,10 +429,9 @@
     fm_ref[3] = sums[3]
     for c in range(3):
         fm_ref[c] = sums[c]
-    fill_table(all_ref, 0, table_ref)
-    pair_loop(list_ref, 0, me, table_ref, force_ref)
-    own = scatter_own(force_ref, all_ref, me, lhs_ref, lanes_ref)
-    rim = scatter_rim(force_ref, all_ref, me, square_ref, True, (0.0,))
+    pair_loop(list_ref, 0, 0, me, all_ref, turned_ref, force_ref, sum_ref)
+    own = scatter_own(sum_ref, all_ref, me, lhs_ref, lanes_ref)
+    rim = contact_rim(list_ref, task_ref, 0, 0, me, all_ref, all_ref, rim, square_ref)
     for c in range(3):
         full = jnp.concatenate([both(fill16(own[c]), unpack(rim, c)), zero], axis=0)
         c0_ref[c] = full
@@ -368,11 +441,12 @@
     send_planes([row_plane(fm_ref[n], 0) for n in range(4)], down_ref)
 
 
-def step_contact_kernel(at_ref, list_ref, all_ref, out_ref, table_ref, force_ref, lhs_ref, lanes_ref):
+def step_contact_kernel(
+    at_ref, list_ref, all_ref, out_ref, turned_ref, force_ref, sum_ref, lhs_ref, lanes_ref
+):
     me = at_ref[2]
-    fill_table(all_ref, 0, table_ref)
-    pair_loop(list_ref, 1, me, table_ref, force_ref)
-    out_ref[...] = scatter_own(force_ref, all_ref, me, lhs_ref, lanes_ref)
+    pair_loop(list_ref, 1, 0, me, all_ref, turned_ref, force_ref, sum_ref)
+    out_ref[...] = scatter_own(sum_ref, all_ref, me, lhs_ref, lanes_ref)
 
 
 def shift_rows(x, by):
@@ -535,9 +609,9 @@
 
 
 def late_contact_kernel(
-    at_ref, list_ref, first_ref, all_ref, state_ref, stiff_ref, alive_ref,
+    at_ref, list_ref, task_ref, first_ref, all_ref, state_ref, stiff_ref, alive_ref,
     own_ref, up_ref, down_ref,
-    table_ref, force_ref, lhs_ref, lanes_ref, square_ref,
+    turned_ref, force_ref, sum_ref, lhs_ref, lanes_ref, square_ref, *rims,
 ):
     me = at_ref[2]
     zplanes = neighbour_planes(all_ref, PLANES_2, 5, me, square_ref, 13)
@@ -557,11 +631,10 @@
     for n, step in ((10, 2), (11, 3)):
         m = both(fill16(stiff_ref[...] * alive_ref[step].astype(F32)), unpack(mplanes, 3 + step, 4))
         own_ref[n] = jnp.concatenate([m, zero], axis=0)
-    for step, first_row, low, ups, n in ((2, 0, True, (0.0, 1.0), 3), (3, LATE, False, (0.0,), 6)):
-        fill_table(all_ref, first_row, table_ref)
-        pair_loop(list_ref, step, me, table_ref, force_ref)
-        own = scatter_own(force_ref, first_ref, me, lhs_ref, lanes_ref)
-        rim = scatter_rim(force_ref, first_ref, me, square_ref, low, ups)
+    for step, first_row, n in ((2, 0, 3), (3, LATE, 6)):
+        pair_loop(list_ref, step, first_row, me, all_ref, turned_ref, force_ref, sum_ref)
+        own = scatter_own(sum_ref, first_ref, me, lhs_ref, lanes_ref)
+        rim = contact_rim(list_ref, task_ref, step, first_row, me, all_ref, first_ref, rims, square_ref)
         for c in range(3):
             full = both(fill16(own[c]), unpack(rim, c))
             own_ref[n + c, 0:12] = own_ref[n + c, 0:12] + own_ref[9, 0:12] * full
@@ -650,8 +723,14 @@
     return lax.ppermute(up, axis, ahead), lax.ppermute(down, axis, [(j, i) for i, j in ahead])
 
 
-TABLE = pltpu.VMEM((128, 3, 8, 128), F32)
-FORCE = pltpu.VMEM((49, 3, 8, 128), F32)
+TURNED = pltpu.VMEM((17, 4, 3, 8, 128), F32)
+SUMS = pltpu.VMEM((3, 16, 128), F32)
+RIM = [
+    pltpu.VMEM((3, 384, 128), BF16),
+    pltpu.VMEM((3, 96, 128), BF16),
+    pltpu.VMEM((3, 32, 128), BF16),
+    pltpu.VMEM((16, 128), F32),
+]
 LHS = pltpu.VMEM((576, 2048), BF16)
 LANES = pltpu.VMEM((128, 2048), BF16)
 SQUARE = pltpu.VMEM((128, 128), F32)
@@ -667,17 +746,20 @@
         at, coords, routes, pairs, surf_nodes, stiffness, density, load, alive
     )
     everyone = share(payload)
-    (lists,) = call(plan_kernel, [((8, 512), jnp.int32)], [SMEM, VMEM])(at, everyone)
+    lists, tasks = call(plan_kernel, [((12, 512), jnp.int32), ((4, 4, 8, 128), F32)], [SMEM, VMEM])(at, everyone)
     fm, c0, m1, up, down = call(
         first_contact_kernel,
         [((4, 13, 16, 256), F32), ((3, 13, 16, 256), F32), ((13, 16, 256), F32), ((10, 16, 128), F32),
          ((5, 16, 128), F32)],
-        [SMEM, SMEM] + [VMEM] * 5,
-        [TABLE, FORCE, LHS, LANES, SQUARE],
-    )(at, lists, everyone, load, density, stiffness, alive)
+        [SMEM, SMEM] + [VMEM] * 6,
+        [TURNED, TURNED, SUMS, LHS, LANES, SQUARE] + RIM,
+    )(at, lists, tasks, everyone, load, density, stiffness, alive)
     xu, xd = neighbours(up, down, "gx")
     (c1,) = call(
-        step_contact_kernel, [((3, 12, 8, 128), F32)], [SMEM, SMEM, VMEM], [TABLE, FORCE, LHS, LANES]
+        step_contact_kernel,
+        [((3, 12, 8, 128), F32)],
+        [SMEM, SMEM, VMEM],
+        [TURNED, TURNED, SUMS, LHS, LANES],
     )(at, lists, everyone)
     up, down = call(y_send_1_kernel, [((10, 16, 128), F32), ((5, 16, 128), F32)], [VMEM] * 4)(
         fm, m1, xu, xd
@@ -693,9 +775,9 @@
     own, up, down = call(
         late_contact_kernel,
         [((12, 13, 16, 256), F32), ((UPS + 1, 16, 128), F32), ((DOWNS + 2, 16, 128), F32)],
-        [SMEM, SMEM] + [VMEM] * 5,
-        [TABLE, FORCE, LHS, LANES, SQUARE],
-    )(at, lists, everyone, late, state, stiffness, alive)
+        [SMEM, SMEM] + [VMEM] * 6,
+        [TURNED, TURNED, SUMS, LHS, LANES, SQUARE] + RIM,
+    )(at, lists, tasks, everyone, late, state, stiffness, alive)
     xu, xd = neighbours(up, down, "gx")
     up, down = call(
         y_send_2_kernel,

time: 159 us -> 145 us (0.912)
  Pallas kernels: 67.5 us -> 56.3 us
  starting transfers between devices: 24.4 us -> 21.8 us
  blocking collectives: 52 us -> 50 us
    pallas_call x1, Pallas kernels: 23.4 us -> 16.4 us  [per_device(): call(late_contact_kernel, [((12, 13, 16, 256), F32), ((UPS + 1, 16, 128),...]
    pallas_call x1, Pallas kernels: 13.4 us -> 9.36 us  [per_device(): call(first_contact_kernel, [((4, 13, 16, 256), F32), ((3, 13, 16, 256), F...]
    ppermute x4, starting transfers between devices: 14.8 us -> 12.5 us  [neighbours(): lax.ppermute(down, axis, [(j, i) for i, j in ahead])]
    all_to_all x2, blocking collectives: 52 us -> 50 us  [share(): return lax.all_to_all(blocks, 'gz', split_axis=0, concat_axis=0, tiled=True)]
  transfers between devices with their start and end apart: 8 -> 8, of which waited for: 3 -> 3; matrix products, arithmetic and copies ran while one was open for 0% -> 0% of each run, Pallas kernels for 4% -> 5%
where the time goes in v3:
time: 145 us; the launch traced here: 143 us
  Pallas kernels  56.3 us (39%)
  blocking collectives  50 us (34%)
  starting transfers between devices  21.8 us (15%)
  waiting for transfers between devices  9.79 us (7%)
  local copies, waits for them, and re-layouts  3.36 us (2%)
    all_to_all x2, blocking collectives, share(): return lax.all_to_all(blocks, 'gz', split_axis=0, concat_axis=0, tiled=True)  50 us
    pallas_call x1, Pallas kernels, per_device(): call(late_contact_kernel, [((12, 13, 16, 256), F32), ((UPS + 1, 16, 128),...  16.4 us
    ppermute x4, starting transfers between devices, neighbours(): lax.ppermute(down, axis, [(j, i) for i, j in ahead])  12.5 us
    pallas_call x1, Pallas kernels, per_device(): call(first_contact_kernel, [((4, 13, 16, 256), F32), ((3, 13, 16, 256), F...  9.36 us
    ppermute x4, starting transfers between devices, neighbours(): lax.ppermute(up, axis, ahead)  9.3 us
    ppermute x4, waiting for transfers between devices, neighbours(): lax.ppermute(up, axis, ahead)  7.81 us
    pallas_call x1, Pallas kernels, per_device(): call(step_contact_kernel, [((3, 12, 8, 128), F32)], [SMEM, SMEM, VMEM], [...  6.73 us
    pallas_call x1, Pallas kernels, per_device(): call(last_kernel, [((3, 12, 8, 128), F32), ((6, 12, 8, 128), F32)], [SMEM...  6.59 us
  transfers between devices with their start and end apart: 8, of which 3 were waited for; matrix products, arithmetic and copies ran while one was open for 0% of the time, Pallas kernels for 5%

profile of v3, /device:TPU:80, one launch (start us, length us, event | category | flops | bytes accessed | tf_op | source)
XLA Modules:
  0.0 142.7 jit_solution(15415209138335594058)
XLA Ops:
  0.6 0.6 pad_add_fusion.at_ref
  1.3 2.2 %shard_map.95 = f32[8,104,128]{2,1,0:T(8,128)} custom-call(s32[3]{0:T(128)} %pad_add_fusion.at_ref, f32[3,16,128]{2,1,0:T(8,128)} %bitcast.23, s32[4,16]{1,0:T(4,128)} %routes_ref.1, s32[4,2,64]{2,1,0:T(2,128)} %bitcast.25, s32[16,128]{1,0:T(8,128)} %nodes_ref.3, f32[12,8,128]{2,1,0:T(8,128)} %bitcast.18, f32[12,8,128]{2,1,0:T(8,128)} %bitcast.21, ...), custom_call_target="tpu_custom_call" | custom-call | tf_op jit(solution)/shard_map/pallas_call | solution.py:745
  3.4 26.8 %all_to_all.10.all_ref.first_ref = f32[8,104,128]{2,1,0:T(8,128)} all-to-all(f32[8,104,128]{2,1,0:T(8,128)} %shard_map.95), channel_id=1, replica_groups=mesh['gx'=8,'gy'=4,'gz'=8] {'gz'}, dimensions={0} | all-to-all | bytes 851968 | tf_op jit(solution)/shard_map/all_to_all | solution.py:717
  30.2 3.8 %shard_map.96 = (s32[12,512]{1,0:T(8,128)}, f32[4,4,8,128]{3,2,1,0:T(8,128)}) custom-call(s32[3]{0:T(128)} %pad_add_fusion.at_ref, f32[8,104,128]{2,1,0:T(8,128)} %all_to_all.10.all_ref.first_ref), custom_call_target="tpu_custom_call" | custom-call | tf_op jit(solution)/shard_map/pallas_call | solution.py:749
  34.0 9.4 %shard_map.97 = (f32[4,13,16,256]{3,2,1,0:T(8,128)}, f32[3,13,16,256]{3,2,1,0:T(8,128)}, f32[13,16,256]{2,1,0:T(8,128)}, f32[10,16,128]{2,1,0:T(8,128)}, f32[5,16,128]{2,1,0:T(8,128)}) custom-call(s32[3]{0:T(128)} %pad_add_fusion.at_ref, s32[12,512]{1,0:T(8,128)} %get-tuple-element.20.list_ref, f32[4,4,8,128]{3,2,1,0:T(8,128)} %get-tuple-element.21.task_ref, ...), custom_call_target="tpu_custom_call" | custom-call | tf_op jit(solution)/shard_map/pallas_call | solution.py:750
  43.4 1.9 %collective-permute-start = (f32[10,16,128]{2,1,0:T(8,128)}, f32[10,16,128]{2,1,0:T(8,128)S(1)}, u32[]{:S(2)}, u32[]{:S(2)}) collective-permute-start(f32[10,16,128]{2,1,0:T(8,128)} %get-tuple-element.25), channel_id=1, source_target_pairs={{0,32},{32,64},{64,96},{96,128},{128,160},{160,192},{192,224},{1,3... | collective-permute-start | bytes 245768 | tf_op jit(solution)/shard_map/ppermute | solution.py:723
  45.3 3.6 %collective-permute-start.1 = (f32[5,16,128]{2,1,0:T(8,128)}, f32[5,16,128]{2,1,0:T(8,128)S(1)}, u32[]{:S(2)}, u32[]{:S(2)}) collective-permute-start(f32[5,16,128]{2,1,0:T(8,128)} %get-tuple-element.26), channel_id=1, source_target_pairs={{32,0},{64,32},{96,64},{128,96},{160,128},{192,160},{224,192},{33,... | collective-permute-start | bytes 122888 | tf_op jit(solution)/shard_map/ppermute | solution.py:723
  49.0 2.0 %collective-permute-done.1.downs_ref.xd_ref = f32[5,16,128]{2,1,0:T(8,128)S(1)} collective-permute-done((f32[5,16,128]{2,1,0:T(8,128)}, f32[5,16,128]{2,1,0:T(8,128)S(1)}, u32[]{:S(2)}, u32[]{:S(2)}) %collective-permute-start.1) | collective-permute-done | bytes 40992 | tf_op jit(solution)/shard_map/ppermute | solution.py:723
  50.9 0.0 copy-start.4
  50.9 0.0 collective-permute-done.ups_ref.xu_ref
  50.9 0.0 copy-start.2
  50.9 0.6 copy-done.4
  51.5 0.0 copy-done.2
  51.6 2.1 %shard_map.98 = (f32[10,16,128]{2,1,0:T(8,128)}, f32[5,16,128]{2,1,0:T(8,128)}) custom-call(f32[4,13,16,256]{3,2,1,0:T(8,128)} %get-tuple-element.22.fm_ref, f32[13,16,256]{2,1,0:T(8,128)} %get-tuple-element.24.m1_ref, f32[10,16,128]{2,1,0:T(8,128)} %copy-done.2, f32[5,16,128]{2,1,0:T(8,128)} %copy-done.4), custom_call_target="tpu_custom_call" | custom-call | tf_op jit(solution)/shard_map/pallas_call | solution.py:764
  53.7 1.9 %collective-permute-start.2 = (f32[10,16,128]{2,1,0:T(8,128)}, f32[10,16,128]{2,1,0:T(8,128)S(1)}, u32[]{:S(2)}, u32[]{:S(2)}) collective-permute-start(f32[10,16,128]{2,1,0:T(8,128)} %get-tuple-element.27), channel_id=1, source_target_pairs={{0,8},{8,16},{16,24},{1,9},{9,17},{17,25},{2,10},{10,18},{18,26},{... | collective-permute-start | bytes 245768 | tf_op jit(solution)/shard_map/ppermute | solution.py:723
  55.6 3.9 %collective-permute-start.3 = (f32[5,16,128]{2,1,0:T(8,128)}, f32[5,16,128]{2,1,0:T(8,128)S(1)}, u32[]{:S(2)}, u32[]{:S(2)}) collective-permute-start(f32[5,16,128]{2,1,0:T(8,128)} %get-tuple-element.28), channel_id=1, source_target_pairs={{8,0},{16,8},{24,16},{9,1},{17,9},{25,17},{10,2},{18,10},{26,18},{... | collective-permute-start | bytes 122888 | tf_op jit(solution)/shard_map/ppermute | solution.py:723
  59.6 6.7 %shard_map.99.c1_ref = f32[3,12,8,128]{3,2,1,0:T(8,128)} custom-call(s32[3]{0:T(128)} %pad_add_fusion.at_ref, s32[12,512]{1,0:T(8,128)} %get-tuple-element.20.list_ref, f32[8,104,128]{2,1,0:T(8,128)} %all_to_all.10.all_ref.first_ref), custom_call_target="tpu_custom_call" | custom-call | tf_op jit(solution)/shard_map/pallas_call | solution.py:758
  66.3 0.0 collective-permute-done.3.yd_ref
  66.3 0.0 copy-start.7
  66.3 0.0 collective-permute-done.2.yu_ref
  66.3 0.0 copy-start.6
  66.3 0.6 copy-done.7
  66.9 0.0 copy-done.6
  67.0 6.4 %shard_map.100 = (f32[8,128,128]{2,1,0:T(8,128)}, f32[10,13,16,256]{3,2,1,0:T(8,128)}) custom-call(f32[4,13,16,256]{3,2,1,0:T(8,128)} %get-tuple-element.22.fm_ref, f32[3,13,16,256]{3,2,1,0:T(8,128)} %get-tuple-element.23.c0_ref, f32[13,16,256]{2,1,0:T(8,128)} %get-tuple-element.24.m1_ref, f32[10,16,128]{2,1,0:T(8,128)} %copy-done.2, ...), custom_call_target="tpu_custom_call" | custom-call | tf_op jit(solution)/shard_map/pallas_call | solution.py:768
  73.4 23.2 %all_to_all.11.all_ref = f32[8,128,128]{2,1,0:T(8,128)} all-to-all(f32[8,128,128]{2,1,0:T(8,128)} %get-tuple-element.29), channel_id=1, replica_groups=mesh['gx'=8,'gy'=4,'gz'=8] {'gz'}, dimensions={0} | all-to-all | bytes 1048576 | tf_op jit(solution)/shard_map/all_to_all | solution.py:717
  96.6 16.4 %shard_map.101 = (f32[12,13,16,256]{3,2,1,0:T(8,128)}, f32[14,16,128]{2,1,0:T(8,128)}, f32[25,16,128]{2,1,0:T(8,128)}) custom-call(s32[3]{0:T(128)} %pad_add_fusion.at_ref, s32[12,512]{1,0:T(8,128)} %get-tuple-element.20.list_ref, f32[4,4,8,128]{3,2,1,0:T(8,128)} %get-tuple-element.21.task_ref, f32[8,104,128]{2,1,0:T(8,128)} %all_to_all.10.all_ref.first_ref, ...), custom_call_target="tpu_custom_call" | custom-call | tf_op jit(solution)/shard_map/pallas_call | solution.py:775
  113.0 2.0 %collective-permute-start.5 = (f32[25,16,128]{2,1,0:T(8,128)}, f32[25,16,128]{2,1,0:T(8,128)S(1)}, u32[]{:S(2)}, u32[]{:S(2)}) collective-permute-start(f32[25,16,128]{2,1,0:T(8,128)} %get-tuple-element.33), channel_id=1, source_target_pairs={{32,0},{64,32},{96,64},{128,96},{160,128},{192,160},{224,192},{33,... | collective-permute-start | bytes 614408 | tf_op jit(solution)/shard_map/ppermute | solution.py:723
  114.9 2.6 %collective-permute-start.4 = (f32[14,16,128]{2,1,0:T(8,128)}, f32[14,16,128]{2,1,0:T(8,128)S(1)}, u32[]{:S(2)}, u32[]{:S(2)}) collective-permute-start(f32[14,16,128]{2,1,0:T(8,128)} %get-tuple-element.32), channel_id=1, source_target_pairs={{0,32},{32,64},{64,96},{96,128},{128,160},{160,192},{192,224},{1,3... | collective-permute-start | bytes 344072 | tf_op jit(solution)/shard_map/ppermute | solution.py:723
  117.6 3.7 %collective-permute-done.4.ups_ref.xu_ref = f32[14,16,128]{2,1,0:T(8,128)S(1)} collective-permute-done((f32[14,16,128]{2,1,0:T(8,128)}, f32[14,16,128]{2,1,0:T(8,128)S(1)}, u32[]{:S(2)}, u32[]{:S(2)}) %collective-permute-start.4) | collective-permute-done | bytes 114720 | tf_op jit(solution)/shard_map/ppermute | solution.py:723
  121.2 0.0 copy-start.1
  121.3 0.0 collective-permute-done.5.downs_ref.xd_ref
  121.3 0.0 copy-start
  121.3 0.6 copy-done.1
  121.9 0.1 copy-done
  122.0 2.8 %shard_map.102 = (f32[14,16,128]{2,1,0:T(8,128)}, f32[25,16,128]{2,1,0:T(8,128)}) custom-call(s32[3]{0:T(128)} %pad_add_fusion.at_ref, f32[12,13,16,256]{3,2,1,0:T(8,128)} %get-tuple-element.31.own_ref, f32[14,16,128]{2,1,0:T(8,128)} %copy-done.1, f32[25,16,128]{2,1,0:T(8,128)} %copy-done), custom_call_target="tpu_custom_call" | custom-call | tf_op jit(solution)/shard_map/pallas_call | solution.py:782
  124.8 3.0 %collective-permute-start.7 = (f32[25,16,128]{2,1,0:T(8,128)}, f32[25,16,128]{2,1,0:T(8,128)S(1)}, u32[]{:S(2)}, u32[]{:S(2)}) collective-permute-start(f32[25,16,128]{2,1,0:T(8,128)} %get-tuple-element.35), channel_id=1, source_target_pairs={{8,0},{16,8},{24,16},{9,1},{17,9},{25,17},{10,2},{18,10},{26,18},{... | collective-permute-start | bytes 614408 | tf_op jit(solution)/shard_map/ppermute | solution.py:723
  127.8 2.8 %collective-permute-start.6 = (f32[14,16,128]{2,1,0:T(8,128)}, f32[14,16,128]{2,1,0:T(8,128)S(1)}, u32[]{:S(2)}, u32[]{:S(2)}) collective-permute-start(f32[14,16,128]{2,1,0:T(8,128)} %get-tuple-element.34), channel_id=1, source_target_pairs={{0,8},{8,16},{16,24},{1,9},{9,17},{17,25},{2,10},{10,18},{18,26},{... | collective-permute-start | bytes 344072 | tf_op jit(solution)/shard_map/ppermute | solution.py:723
  130.6 4.1 %collective-permute-done.6.yu_ref = f32[14,16,128]{2,1,0:T(8,128)S(1)} collective-permute-done((f32[14,16,128]{2,1,0:T(8,128)}, f32[14,16,128]{2,1,0:T(8,128)S(1)}, u32[]{:S(2)}, u32[]{:S(2)}) %collective-permute-start.6) | collective-permute-done | bytes 114720 | tf_op jit(solution)/shard_map/ppermute | solution.py:723
  134.8 0.0 copy-start.5
  134.8 0.0 collective-permute-done.7.yd_ref
  134.8 0.6 copy-done.5
  135.4 0.0 copy-start.3
  135.4 0.7 copy-done.3
  136.1 6.6 %shard_map.103 = (f32[3,12,8,128]{3,2,1,0:T(8,128)}, f32[6,12,8,128]{3,2,1,0:T(8,128)}) custom-call(s32[3]{0:T(128)} %pad_add_fusion.at_ref, f32[12,13,16,256]{3,2,1,0:T(8,128)} %get-tuple-element.31.own_ref, f32[14,16,128]{2,1,0:T(8,128)} %copy-done.1, f32[25,16,128]{2,1,0:T(8,128)} %copy-done, f32[14,16,128]{2,1,0:T(8,128)} %copy-done.5, ...), custom_call_target="tpu_custom_call" | custom-call | tf_op jit(solution)/shard_map/pallas_call | solution.py:788
Async XLA Ops:
  43.4 7.5 %collective-permute-start = (f32[10,16,128]{2,1,0:T(8,128)}, f32[10,16,128]{2,1,0:T(8,128)S(1)}, u32[]{:S(2)}, u32[]{:S(2)}) collective-permute-start(f32[10,16,128]{2,1,0:T(8,128)} %get-tuple-element.25), channel_id=1, source_target_pairs={{0,32},{32,64},{64,96},{96,128},{128,160},{160,192},{192,224},{1,3... | collective-permute-start | bytes 245768 | tf_op jit(solution)/shard_map/ppermute | solution.py:723
  45.3 5.6 %collective-permute-start.1 = (f32[5,16,128]{2,1,0:T(8,128)}, f32[5,16,128]{2,1,0:T(8,128)S(1)}, u32[]{:S(2)}, u32[]{:S(2)}) collective-permute-start(f32[5,16,128]{2,1,0:T(8,128)} %get-tuple-element.26), channel_id=1, source_target_pairs={{32,0},{64,32},{96,64},{128,96},{160,128},{192,160},{224,192},{33,... | collective-permute-start | bytes 122888 | tf_op jit(solution)/shard_map/ppermute | solution.py:723
  50.9 0.6 copy-start.4
  50.9 0.7 copy-start.2
  53.7 12.6 %collective-permute-start.2 = (f32[10,16,128]{2,1,0:T(8,128)}, f32[10,16,128]{2,1,0:T(8,128)S(1)}, u32[]{:S(2)}, u32[]{:S(2)}) collective-permute-start(f32[10,16,128]{2,1,0:T(8,128)} %get-tuple-element.27), channel_id=1, source_target_pairs={{0,8},{8,16},{16,24},{1,9},{9,17},{17,25},{2,10},{10,18},{18,26},{... | collective-permute-start | bytes 245768 | tf_op jit(solution)/shard_map/ppermute | solution.py:723
  55.6 10.7 %collective-permute-start.3 = (f32[5,16,128]{2,1,0:T(8,128)}, f32[5,16,128]{2,1,0:T(8,128)S(1)}, u32[]{:S(2)}, u32[]{:S(2)}) collective-permute-start(f32[5,16,128]{2,1,0:T(8,128)} %get-tuple-element.28), channel_id=1, source_target_pairs={{8,0},{16,8},{24,16},{9,1},{17,9},{25,17},{10,2},{18,10},{26,18},{... | collective-permute-start | bytes 122888 | tf_op jit(solution)/shard_map/ppermute | solution.py:723
  66.3 0.6 copy-start.7
  66.3 0.7 copy-start.6
  113.0 8.3 %collective-permute-start.5 = (f32[25,16,128]{2,1,0:T(8,128)}, f32[25,16,128]{2,1,0:T(8,128)S(1)}, u32[]{:S(2)}, u32[]{:S(2)}) collective-permute-start(f32[25,16,128]{2,1,0:T(8,128)} %get-tuple-element.33), channel_id=1, source_target_pairs={{32,0},{64,32},{96,64},{128,96},{160,128},{192,160},{224,192},{33,... | collective-permute-start | bytes 614408 | tf_op jit(solution)/shard_map/ppermute | solution.py:723
  114.9 6.3 %collective-permute-start.4 = (f32[14,16,128]{2,1,0:T(8,128)}, f32[14,16,128]{2,1,0:T(8,128)S(1)}, u32[]{:S(2)}, u32[]{:S(2)}) collective-permute-start(f32[14,16,128]{2,1,0:T(8,128)} %get-tuple-element.32), channel_id=1, source_target_pairs={{0,32},{32,64},{64,96},{96,128},{128,160},{160,192},{192,224},{1,3... | collective-permute-start | bytes 344072 | tf_op jit(solution)/shard_map/ppermute | solution.py:723
  121.2 0.6 copy-start.1
  121.3 0.8 copy-start
  124.8 10.0 %collective-permute-start.7 = (f32[25,16,128]{2,1,0:T(8,128)}, f32[25,16,128]{2,1,0:T(8,128)S(1)}, u32[]{:S(2)}, u32[]{:S(2)}) collective-permute-start(f32[25,16,128]{2,1,0:T(8,128)} %get-tuple-element.35), channel_id=1, source_target_pairs={{8,0},{16,8},{24,16},{9,1},{17,9},{25,17},{10,2},{18,10},{26,18},{... | collective-permute-start | bytes 614408 | tf_op jit(solution)/shard_map/ppermute | solution.py:723
  127.8 7.0 %collective-permute-start.6 = (f32[14,16,128]{2,1,0:T(8,128)}, f32[14,16,128]{2,1,0:T(8,128)S(1)}, u32[]{:S(2)}, u32[]{:S(2)}) collective-permute-start(f32[14,16,128]{2,1,0:T(8,128)} %get-tuple-element.34), channel_id=1, source_target_pairs={{0,8},{8,16},{16,24},{1,9},{9,17},{17,25},{2,10},{10,18},{18,26},{... | collective-permute-start | bytes 344072 | tf_op jit(solution)/shard_map/ppermute | solution.py:723
  134.8 0.6 copy-start.5
  135.4 0.7 copy-start.3

commit v4 on v3

--- a/solution.py
+++ b/solution.py
@@ -11,9 +11,11 @@
 BF16 = jnp.bfloat16
 SCALE = math.sqrt(math.log2(math.e) / 0.08)
 DT = 0.2
-PARAMS = pltpu.CompilerParams(vmem_limit_bytes=56 * 2**20)
+PARAMS = pltpu.CompilerParams(vmem_limit_bytes=28 * 2**20)
 VMEM = pl.BlockSpec(memory_space=pltpu.VMEM)
 SMEM = pl.BlockSpec(memory_space=pltpu.SMEM)
+HELD = pl.BlockSpec(memory_space=pltpu.VMEM)
+FAR = pl.BlockSpec(memory_space=pltpu.HBM)
 KEYS, PAIRS, NODES, PLANES = 48, 52, 56, 72
 ROWS_1 = 104
 LATE, PLANES_2 = 48, 96
@@ -108,15 +110,21 @@
     return jnp.dot(x.astype(BF16), to, preferred_element_type=F32)
 
 
-def prep_kernel(
-    at_ref, coords_ref, routes_ref, pairs_ref, nodes_ref, stiff_ref, dens_ref, load_ref, alive_ref,
-    out_ref, square_ref,
-):
+def prep_kernel(at_ref, *refs):
+    far, (out_ref, field_ref, square_ref), near, sems = refs[:8], refs[8:11], refs[11:19], refs[19]
+    copies = [pltpu.make_async_copy(a, b, sems.at[n]) for n, (a, b) in enumerate(zip(far, near))]
+    for copy in copies:
+        copy.start()
+    for copy in copies:
+        copy.wait()
+    coords_ref, routes_ref, pairs_ref, nodes_ref, stiff_ref, dens_ref, load_ref, alive_ref = near
     me = at_ref[2]
-    fields = [load_ref[0], load_ref[1], load_ref[2], dens_ref[...]]
+    for c in range(3):
+        field_ref[c] = load_ref[c]
+    field_ref[3] = dens_ref[...]
     for step in (1, 2, 3):
-        fields.append(stiff_ref[...] * alive_ref[step].astype(F32))
-    rows = planes_to_rows(pack([fill16(f) for f in fields], 4), square_ref)
+        field_ref[3 + step] = stiff_ref[...] * alive_ref[step].astype(F32)
+    rows = planes_to_rows(pack([fill16(field_ref[n]) for n in range(7)], 4), square_ref)
     nodes = nodes_ref[...].astype(F32)
     routes = routes_ref[...].astype(F32)
     rank = jnp.zeros((4, 16), F32)
@@ -414,15 +422,14 @@
 
 
 def first_contact_kernel(
-    at_ref, list_ref, task_ref, all_ref, load_ref, dens_ref, stiff_ref, alive_ref,
+    at_ref, list_ref, task_ref, all_ref, field_ref,
     fm_ref, c0_ref, m1_ref, up_ref, down_ref,
     turned_ref, force_ref, sum_ref, lhs_ref, lanes_ref, square_ref, *rim,
 ):
     me = at_ref[2]
     planes = neighbour_planes(all_ref, PLANES, 4, me, square_ref, 12)
-    fields = [load_ref[0], load_ref[1], load_ref[2], dens_ref[...]]
-    sums = [node_sum(both(fill16(f), unpack(planes, n, 4))) for n, f in enumerate(fields)]
-    m1 = both(fill16(stiff_ref[...] * alive_ref[1].astype(F32)), unpack(planes, 4, 4))
+    sums = [node_sum(both(fill16(field_ref[n]), unpack(planes, n, 4))) for n in range(4)]
+    m1 = both(fill16(field_ref[4]), unpack(planes, 4, 4))
     zero = jnp.zeros((1, 16, 256), F32)
     m1 = jnp.concatenate([m1, zero], axis=0)
     m1_ref[...] = m1
@@ -533,7 +540,7 @@
 
 
 def second_step_kernel(
-    fm_ref, c0_ref, m1_ref, xu_ref, xd_ref, yu_ref, yd_ref, c1_ref, coords_ref, nodes_ref,
+    at_ref, fm_ref, c0_ref, m1_ref, xu_ref, xd_ref, yu_ref, yd_ref, c1_ref, all_ref,
     out_ref, state_ref, rows_ref, lanes_ref, square_ref,
 ):
     fields, m1 = x_extended_1(fm_ref, m1_ref, xu_ref, xd_ref, range(13))
@@ -568,9 +575,10 @@
         state_ref[3 + c] = back[1]
         state_ref[6 + c] = back[2]
     state_ref[9] = shift_rows(jnp.where(good, inv, 0.0), -1)
+    me = at_ref[2]
     for s in range(16):
         at = slice(128 * s, 128 * s + 128)
-        r, l = row_and_lane(nodes_ref[s : s + 1, :].astype(F32))
+        r, l = row_and_lane(all_ref[me, NODES + s : NODES + s + 1, :])
         hot = one_hot(r, 96).astype(BF16)
         rows_ref[0:96, at] = hot
         rows_ref[96:192, at] = hot
@@ -583,7 +591,7 @@
         for c in range(3):
             block = jnp.concatenate(
                 [values[c][:, 128 * s : 128 * s + 128] for s in range(16)], axis=0
-            ) + coords_ref[c]
+            ) + all_ref[me, 16 * c : 16 * c + 16, :]
             for dest in range(8):
                 out_ref[dest, first + 16 * c : first + 16 * c + 16, :] = block
     rows = planes_to_rows(pack([x[:, :, :128] for x in disp2s + vel2s], 5), square_ref)
@@ -609,7 +617,7 @@
 
 
 def late_contact_kernel(
-    at_ref, list_ref, task_ref, first_ref, all_ref, state_ref, stiff_ref, alive_ref,
+    at_ref, list_ref, task_ref, first_ref, all_ref, state_ref, field_ref,
     own_ref, up_ref, down_ref,
     turned_ref, force_ref, sum_ref, lhs_ref, lanes_ref, square_ref, *rims,
 ):
@@ -629,7 +637,7 @@
         own_ref[3 + c] = with_rim(state_ref[3 + c], 3 + c) + state_ref[6 + c]
         own_ref[6 + c] = state_ref[6 + c]
     for n, step in ((10, 2), (11, 3)):
-        m = both(fill16(stiff_ref[...] * alive_ref[step].astype(F32)), unpack(mplanes, 3 + step, 4))
+        m = both(fill16(field_ref[3 + step]), unpack(mplanes, 3 + step, 4))
         own_ref[n] = jnp.concatenate([m, zero], axis=0)
     for step, first_row, n in ((2, 0, 3), (3, LATE, 6)):
         pair_loop(list_ref, step, first_row, me, all_ref, turned_ref, force_ref, sum_ref)
@@ -702,15 +710,26 @@
         vel_ref[c] = shift_rows(0.125 * s[:, :, :128], -2)[:, :8, :]
 
 
-def call(kernel, outs, specs, scratch=()):
-    return pl.pallas_call(
-        kernel,
-        out_shape=[jax.ShapeDtypeStruct(s, d) for s, d in outs],
-        in_specs=specs,
-        out_specs=[VMEM] * len(outs),
-        scratch_shapes=list(scratch),
-        compiler_params=PARAMS,
-    )
+def call(kernel, outs, specs, scratch=(), held=()):
+    def run(*args):
+        spaces = [pltpu.VMEM if spec is HELD else pltpu.HBM if spec is FAR else None for spec in specs]
+        args = [
+            a if space is None else pltpu.with_memory_space_constraint(a, space)
+            for a, space in zip(args, spaces)
+        ]
+        return pl.pallas_call(
+            kernel,
+            out_shape=[
+                pltpu.VMEM(s, d) if n in held else jax.ShapeDtypeStruct(s, d)
+                for n, (s, d) in enumerate(outs)
+            ],
+            in_specs=specs,
+            out_specs=[VMEM] * len(outs),
+            scratch_shapes=list(scratch),
+            compiler_params=PARAMS,
+        )(*args)
+
+    return run
 
 
 def share(blocks):
@@ -742,53 +761,62 @@
     load, alive = jnp.swapaxes(load, 1, 2), jnp.swapaxes(alive, 1, 2)
     coords = jnp.swapaxes(surf_coords, 0, 1)
     pairs = jnp.swapaxes(pairs[:, 0], 1, 2)
-    (payload,) = call(prep_kernel, [((8, ROWS_1, 128), F32)], [SMEM] + [VMEM] * 8, [SQUARE])(
-        at, coords, routes, pairs, surf_nodes, stiffness, density, load, alive
-    )
+    params = (coords, routes, pairs, surf_nodes, stiffness, density, load, alive)
+    payload, fields = call(
+        prep_kernel,
+        [((8, ROWS_1, 128), F32), ((7, 12, 8, 128), F32)],
+        [SMEM] + [FAR] * 8,
+        [SQUARE] + [pltpu.VMEM(p.shape, p.dtype) for p in params] + [pltpu.SemaphoreType.DMA((8,))],
+        (1,),
+    )(at, *params)
     everyone = share(payload)
-    lists, tasks = call(plan_kernel, [((12, 512), jnp.int32), ((4, 4, 8, 128), F32)], [SMEM, VMEM])(at, everyone)
+    lists, tasks = call(plan_kernel, [((12, 512), jnp.int32), ((4, 4, 8, 128), F32)], [SMEM, HELD], (), (1,))(at, everyone)
     fm, c0, m1, up, down = call(
         first_contact_kernel,
         [((4, 13, 16, 256), F32), ((3, 13, 16, 256), F32), ((13, 16, 256), F32), ((10, 16, 128), F32),
          ((5, 16, 128), F32)],
-        [SMEM, SMEM] + [VMEM] * 6,
+        [SMEM, SMEM, HELD, HELD, HELD],
         [TURNED, TURNED, SUMS, LHS, LANES, SQUARE] + RIM,
-    )(at, lists, tasks, everyone, load, density, stiffness, alive)
+        (0, 1, 2),
+    )(at, lists, tasks, everyone, fields)
     xu, xd = neighbours(up, down, "gx")
     (c1,) = call(
         step_contact_kernel,
         [((3, 12, 8, 128), F32)],
-        [SMEM, SMEM, VMEM],
+        [SMEM, SMEM, HELD],
         [TURNED, TURNED, SUMS, LHS, LANES],
+        (0,),
     )(at, lists, everyone)
-    up, down = call(y_send_1_kernel, [((10, 16, 128), F32), ((5, 16, 128), F32)], [VMEM] * 4)(
+    up, down = call(y_send_1_kernel, [((10, 16, 128), F32), ((5, 16, 128), F32)], [HELD] * 4)(
         fm, m1, xu, xd
     )
     yu, yd = neighbours(up, down, "gy")
     payload, state = call(
         second_step_kernel,
         [((8, ROWS_2, 128), F32), ((10, 13, 16, 256), F32)],
-        [VMEM] * 10,
+        [SMEM] + [HELD] * 9,
         [pltpu.VMEM((192, 2048), BF16), LANES, SQUARE],
-    )(fm, c0, m1, xu, xd, yu, yd, c1, coords, surf_nodes)
+        (1,),
+    )(at, fm, c0, m1, xu, xd, yu, yd, c1, everyone)
     late = share(payload)
     own, up, down = call(
         late_contact_kernel,
         [((12, 13, 16, 256), F32), ((UPS + 1, 16, 128), F32), ((DOWNS + 2, 16, 128), F32)],
-        [SMEM, SMEM] + [VMEM] * 6,
+        [SMEM, SMEM] + [HELD] * 5,
         [TURNED, TURNED, SUMS, LHS, LANES, SQUARE] + RIM,
-    )(at, lists, tasks, everyone, late, state, stiffness, alive)
+        (0,),
+    )(at, lists, tasks, everyone, late, state, fields)
     xu, xd = neighbours(up, down, "gx")
     up, down = call(
         y_send_2_kernel,
         [((UPS + 1, 16, 128), F32), ((DOWNS + 2, 16, 128), F32)],
-        [SMEM] + [VMEM] * 3,
+        [SMEM] + [HELD] * 3,
     )(at, own, xu, xd)
     yu, yd = neighbours(up, down, "gy")
     vel, stress = call(
         last_kernel,
         [((3, 12, 8, 128), F32), ((6, 12, 8, 128), F32)],
-        [SMEM] + [VMEM] * 5,
+        [SMEM] + [HELD] * 5,
     )(at, own, xu, xd, yu, yd)
     return jnp.swapaxes(vel, 1, 2), jnp.swapaxes(stress, 1, 2)
 

time: 145 us -> 125 us (0.86); the launches traced: 143 us -> 125 us
  Pallas kernels: 56.3 us -> 41.9 us
  local copies, waits for them, and re-layouts: 3.36 us -> 0 us
    pallas_call x9, Pallas kernels: 56.3 us -> 41.9 us  [run(): pl.pallas_call(kernel, out_shape=[pltpu.VMEM(s, d) if n in held else jax....]
    unnamed x16 -> x0, local copies, waits for them, and re-layouts: 3.36 us -> none
  transfers between devices with their start and end apart: 8 -> 8, of which waited for: 3 -> 3; matrix products, arithmetic and copies ran while one was open for 0% -> 0% of each run, Pallas kernels for 5% -> 4%
where the time goes in v4:
time: 125 us
  blocking collectives  50.1 us (40%)
  Pallas kernels  41.9 us (34%)
  starting transfers between devices  21.7 us (17%)
  waiting for transfers between devices  10.1 us (8%)
    all_to_all x2, blocking collectives, share(): return lax.all_to_all(blocks, 'gz', split_axis=0, concat_axis=0, tiled=True)  50.1 us
    pallas_call x9, Pallas kernels, run(): pl.pallas_call(kernel, out_shape=[pltpu.VMEM(s, d) if n in held else jax....  41.9 us
    ppermute x4, starting transfers between devices, neighbours(): lax.ppermute(down, axis, [(j, i) for i, j in ahead])  13.5 us
    ppermute x4, waiting for transfers between devices, neighbours(): lax.ppermute(up, axis, ahead)  8.45 us
    ppermute x4, starting transfers between devices, neighbours(): lax.ppermute(up, axis, ahead)  8.17 us
  transfers between devices with their start and end apart: 8, of which 3 were waited for; matrix products, arithmetic and copies ran while one was open for 0% of the time, Pallas kernels for 4%

profile of v4, /device:TPU:80, one launch (start us, length us, event | category | flops | bytes accessed | tf_op | source)
XLA Modules:
  0.0 124.6 jit_solution(3209183508306177366)
XLA Ops:
  0.6 0.1 pad_add_fusion.at_ref
  0.7 2.0 %shard_map.95 = (f32[8,104,128]{2,1,0:T(8,128)S(1)}, f32[7,12,8,128]{3,2,1,0:T(8,128)S(1)}) custom-call(s32[3]{0:T(128)S(1)} %pad_add_fusion.at_ref, f32[3,16,128]{2,1,0:T(8,128)} %bitcast.17, s32[4,16]{1,0:T(4,128)} %refs_1_.1, s32[4,2,64]{2,1,0:T(2,128)} %bitcast.18, s32[16,128]{1,0:T(8,128)} %refs_3_.1, f32[12,8,128]{2,1,0:T(8,128)} %bitcast.15, ...), custom_call_target="tpu_custom_call" | custom-call | tf_op jit(solution)/shard_map/pallas_call | solution.py:720
  2.8 26.5 %all_to_all.10.all_ref.first_ref = f32[8,104,128]{2,1,0:T(8,128)S(1)} all-to-all(f32[8,104,128]{2,1,0:T(8,128)S(1)} %get-tuple-element.22), channel_id=1, replica_groups=mesh['gx'=8,'gy'=4,'gz'=8] {'gz'}, dimensions={0} | all-to-all | bytes 851968 | tf_op jit(solution)/shard_map/all_to_all | solution.py:736
  29.3 2.6 %shard_map.96 = (s32[12,512]{1,0:T(8,128)S(1)}, f32[4,4,8,128]{3,2,1,0:T(8,128)S(1)}) custom-call(s32[3]{0:T(128)S(1)} %pad_add_fusion.at_ref, f32[8,104,128]{2,1,0:T(8,128)S(1)} %all_to_all.10.all_ref.first_ref), custom_call_target="tpu_custom_call" | custom-call | tf_op jit(solution)/shard_map/pallas_call | solution.py:720
  31.9 7.2 %shard_map.97 = (f32[4,13,16,256]{3,2,1,0:T(8,128)S(1)}, f32[3,13,16,256]{3,2,1,0:T(8,128)S(1)}, f32[13,16,256]{2,1,0:T(8,128)S(1)}, f32[10,16,128]{2,1,0:T(8,128)S(1)}, f32[5,16,128]{2,1,0:T(8,128)S(1)}) custom-call(s32[3]{0:T(128)S(1)} %pad_add_fusion.at_ref, s32[12,512]{1,0:T(8,128)S(1)} %get-tuple-element.23.list_ref, ...), custom_call_target="tpu_custom_call" | custom-call | tf_op jit(solution)/shard_map/pallas_call | solution.py:720
  39.1 1.9 %collective-permute-start = (f32[10,16,128]{2,1,0:T(8,128)S(1)}, f32[10,16,128]{2,1,0:T(8,128)S(1)}, u32[]{:S(2)}, u32[]{:S(2)}) collective-permute-start(f32[10,16,128]{2,1,0:T(8,128)S(1)} %get-tuple-element.29), channel_id=1, source_target_pairs={{0,32},{32,64},{64,96},{96,128},{128,160},{160,192},{192,224},{1,3... | collective-permute-start | bytes 245768 | tf_op jit(solution)/shard_map/ppermute | solution.py:742
  41.1 3.6 %collective-permute-start.1 = (f32[5,16,128]{2,1,0:T(8,128)S(1)}, f32[5,16,128]{2,1,0:T(8,128)S(1)}, u32[]{:S(2)}, u32[]{:S(2)}) collective-permute-start(f32[5,16,128]{2,1,0:T(8,128)S(1)} %get-tuple-element.30), channel_id=1, source_target_pairs={{32,0},{64,32},{96,64},{128,96},{160,128},{192,160},{224,192},{33,... | collective-permute-start | bytes 122888 | tf_op jit(solution)/shard_map/ppermute | solution.py:742
  44.7 1.7 %collective-permute-done.1.downs_ref.xd_ref = f32[5,16,128]{2,1,0:T(8,128)S(1)} collective-permute-done((f32[5,16,128]{2,1,0:T(8,128)S(1)}, f32[5,16,128]{2,1,0:T(8,128)S(1)}, u32[]{:S(2)}, u32[]{:S(2)}) %collective-permute-start.1) | collective-permute-done | bytes 40992 | tf_op jit(solution)/shard_map/ppermute | solution.py:742
  46.4 0.0 collective-permute-done.ups_ref.xu_ref
  46.4 0.2 shard_map.98
  46.6 1.9 %collective-permute-start.2 = (f32[10,16,128]{2,1,0:T(8,128)S(1)}, f32[10,16,128]{2,1,0:T(8,128)S(1)}, u32[]{:S(2)}, u32[]{:S(2)}) collective-permute-start(f32[10,16,128]{2,1,0:T(8,128)S(1)} %get-tuple-element.31), channel_id=1, source_target_pairs={{0,8},{8,16},{16,24},{1,9},{9,17},{17,25},{2,10},{10,18},{18,26},{... | collective-permute-start | bytes 245768 | tf_op jit(solution)/shard_map/ppermute | solution.py:742
  48.5 3.9 %collective-permute-start.3 = (f32[5,16,128]{2,1,0:T(8,128)S(1)}, f32[5,16,128]{2,1,0:T(8,128)S(1)}, u32[]{:S(2)}, u32[]{:S(2)}) collective-permute-start(f32[5,16,128]{2,1,0:T(8,128)S(1)} %get-tuple-element.32), channel_id=1, source_target_pairs={{8,0},{16,8},{24,16},{9,1},{17,9},{25,17},{10,2},{18,10},{26,18},{... | collective-permute-start | bytes 122888 | tf_op jit(solution)/shard_map/ppermute | solution.py:742
  52.4 5.5 %shard_map.99.c1_ref = f32[3,12,8,128]{3,2,1,0:T(8,128)S(1)} custom-call(s32[3]{0:T(128)S(1)} %pad_add_fusion.at_ref, s32[12,512]{1,0:T(8,128)S(1)} %get-tuple-element.23.list_ref, f32[8,104,128]{2,1,0:T(8,128)S(1)} %all_to_all.10.all_ref.first_ref), custom_call_target="tpu_custom_call" | custom-call | tf_op jit(solution)/shard_map/pallas_call | solution.py:720
  58.0 0.0 collective-permute-done.3.yd_ref
  58.0 0.0 collective-permute-done.2.yu_ref
  58.0 4.1 %shard_map.100 = (f32[8,128,128]{2,1,0:T(8,128)S(1)}, f32[10,13,16,256]{3,2,1,0:T(8,128)S(1)}) custom-call(s32[3]{0:T(128)S(1)} %pad_add_fusion.at_ref, f32[4,13,16,256]{3,2,1,0:T(8,128)S(1)} %get-tuple-element.26.fm_ref, f32[3,13,16,256]{3,2,1,0:T(8,128)S(1)} %get-tuple-element.27.c0_ref, f32[13,16,256]{2,1,0:T(8,128)S(1)} %get-tuple-element.28.m1_ref, ...), custom_call_target="tpu_custom_call" | custom-call | tf_op jit(solution)/shard_map/pallas_call | solution.py:720
  62.1 23.6 %all_to_all.11.all_ref = f32[8,128,128]{2,1,0:T(8,128)S(1)} all-to-all(f32[8,128,128]{2,1,0:T(8,128)S(1)} %get-tuple-element.33), channel_id=1, replica_groups=mesh['gx'=8,'gy'=4,'gz'=8] {'gz'}, dimensions={0} | all-to-all | bytes 1048576 | tf_op jit(solution)/shard_map/all_to_all | solution.py:736
  85.7 13.9 %shard_map.101 = (f32[12,13,16,256]{3,2,1,0:T(8,128)S(1)}, f32[14,16,128]{2,1,0:T(8,128)S(1)}, f32[25,16,128]{2,1,0:T(8,128)S(1)}) custom-call(s32[3]{0:T(128)S(1)} %pad_add_fusion.at_ref, s32[12,512]{1,0:T(8,128)S(1)} %get-tuple-element.23.list_ref, f32[4,4,8,128]{3,2,1,0:T(8,128)S(1)} %get-tuple-element.24.task_ref, ...), custom_call_target="tpu_custom_call" | custom-call | tf_op jit(solution)/shard_map/pallas_call | solution.py:720
  99.6 1.9 %collective-permute-start.5 = (f32[25,16,128]{2,1,0:T(8,128)S(1)}, f32[25,16,128]{2,1,0:T(8,128)S(1)}, u32[]{:S(2)}, u32[]{:S(2)}) collective-permute-start(f32[25,16,128]{2,1,0:T(8,128)S(1)} %get-tuple-element.37), channel_id=1, source_target_pairs={{32,0},{64,32},{96,64},{128,96},{160,128},{192,160},{224,192},{33,... | collective-permute-start | bytes 614408 | tf_op jit(solution)/shard_map/ppermute | solution.py:742
  101.5 2.4 %collective-permute-start.4 = (f32[14,16,128]{2,1,0:T(8,128)S(1)}, f32[14,16,128]{2,1,0:T(8,128)S(1)}, u32[]{:S(2)}, u32[]{:S(2)}) collective-permute-start(f32[14,16,128]{2,1,0:T(8,128)S(1)} %get-tuple-element.36), channel_id=1, source_target_pairs={{0,32},{32,64},{64,96},{96,128},{128,160},{160,192},{192,224},{1,3... | collective-permute-start | bytes 344072 | tf_op jit(solution)/shard_map/ppermute | solution.py:742
  103.9 3.7 %collective-permute-done.4.ups_ref.xu_ref = f32[14,16,128]{2,1,0:T(8,128)S(1)} collective-permute-done((f32[14,16,128]{2,1,0:T(8,128)S(1)}, f32[14,16,128]{2,1,0:T(8,128)S(1)}, u32[]{:S(2)}, u32[]{:S(2)}) %collective-permute-start.4) | collective-permute-done | bytes 114720 | tf_op jit(solution)/shard_map/ppermute | solution.py:742
  107.6 0.0 collective-permute-done.5.downs_ref.xd_ref
  107.6 0.8 shard_map.102
  108.4 4.0 %collective-permute-start.7 = (f32[25,16,128]{2,1,0:T(8,128)S(1)}, f32[25,16,128]{2,1,0:T(8,128)S(1)}, u32[]{:S(2)}, u32[]{:S(2)}) collective-permute-start(f32[25,16,128]{2,1,0:T(8,128)S(1)} %get-tuple-element.39), channel_id=1, source_target_pairs={{8,0},{16,8},{24,16},{9,1},{17,9},{25,17},{10,2},{18,10},{26,18},{... | collective-permute-start | bytes 614408 | tf_op jit(solution)/shard_map/ppermute | solution.py:742
  112.4 1.9 %collective-permute-start.6 = (f32[14,16,128]{2,1,0:T(8,128)S(1)}, f32[14,16,128]{2,1,0:T(8,128)S(1)}, u32[]{:S(2)}, u32[]{:S(2)}) collective-permute-start(f32[14,16,128]{2,1,0:T(8,128)S(1)} %get-tuple-element.38), channel_id=1, source_target_pairs={{0,8},{8,16},{16,24},{1,9},{9,17},{17,25},{2,10},{10,18},{18,26},{... | collective-permute-start | bytes 344072 | tf_op jit(solution)/shard_map/ppermute | solution.py:742
  114.4 4.8 %collective-permute-done.6.yu_ref = f32[14,16,128]{2,1,0:T(8,128)S(1)} collective-permute-done((f32[14,16,128]{2,1,0:T(8,128)S(1)}, f32[14,16,128]{2,1,0:T(8,128)S(1)}, u32[]{:S(2)}, u32[]{:S(2)}) %collective-permute-start.6) | collective-permute-done | bytes 114720 | tf_op jit(solution)/shard_map/ppermute | solution.py:742
  119.1 0.0 collective-permute-done.7.yd_ref
  119.1 5.4 %shard_map.103 = (f32[3,12,8,128]{3,2,1,0:T(8,128)}, f32[6,12,8,128]{3,2,1,0:T(8,128)}) custom-call(s32[3]{0:T(128)S(1)} %pad_add_fusion.at_ref, f32[12,13,16,256]{3,2,1,0:T(8,128)S(1)} %get-tuple-element.35.own_ref, f32[14,16,128]{2,1,0:T(8,128)S(1)} %collective-permute-done.4.ups_ref.xu_ref, f32[25,16,128]{2,1,0:T(8,128)S(1)} %collective-permute-done.5.downs_ref.xd_ref, ...), custom_call_target="tpu_custom_call" | custom-call | tf_op jit(solution)/shard_map/pallas_call | solution.py:720
Async XLA Ops:
  39.1 7.2 %collective-permute-start = (f32[10,16,128]{2,1,0:T(8,128)S(1)}, f32[10,16,128]{2,1,0:T(8,128)S(1)}, u32[]{:S(2)}, u32[]{:S(2)}) collective-permute-start(f32[10,16,128]{2,1,0:T(8,128)S(1)} %get-tuple-element.29), channel_id=1, source_target_pairs={{0,32},{32,64},{64,96},{96,128},{128,160},{160,192},{192,224},{1,3... | collective-permute-start | bytes 245768 | tf_op jit(solution)/shard_map/ppermute | solution.py:742
  41.1 5.3 %collective-permute-start.1 = (f32[5,16,128]{2,1,0:T(8,128)S(1)}, f32[5,16,128]{2,1,0:T(8,128)S(1)}, u32[]{:S(2)}, u32[]{:S(2)}) collective-permute-start(f32[5,16,128]{2,1,0:T(8,128)S(1)} %get-tuple-element.30), channel_id=1, source_target_pairs={{32,0},{64,32},{96,64},{128,96},{160,128},{192,160},{224,192},{33,... | collective-permute-start | bytes 122888 | tf_op jit(solution)/shard_map/ppermute | solution.py:742
  46.6 11.4 %collective-permute-start.2 = (f32[10,16,128]{2,1,0:T(8,128)S(1)}, f32[10,16,128]{2,1,0:T(8,128)S(1)}, u32[]{:S(2)}, u32[]{:S(2)}) collective-permute-start(f32[10,16,128]{2,1,0:T(8,128)S(1)} %get-tuple-element.31), channel_id=1, source_target_pairs={{0,8},{8,16},{16,24},{1,9},{9,17},{17,25},{2,10},{10,18},{18,26},{... | collective-permute-start | bytes 245768 | tf_op jit(solution)/shard_map/ppermute | solution.py:742
  48.5 9.5 %collective-permute-start.3 = (f32[5,16,128]{2,1,0:T(8,128)S(1)}, f32[5,16,128]{2,1,0:T(8,128)S(1)}, u32[]{:S(2)}, u32[]{:S(2)}) collective-permute-start(f32[5,16,128]{2,1,0:T(8,128)S(1)} %get-tuple-element.32), channel_id=1, source_target_pairs={{8,0},{16,8},{24,16},{9,1},{17,9},{25,17},{10,2},{18,10},{26,18},{... | collective-permute-start | bytes 122888 | tf_op jit(solution)/shard_map/ppermute | solution.py:742
  99.6 8.0 %collective-permute-start.5 = (f32[25,16,128]{2,1,0:T(8,128)S(1)}, f32[25,16,128]{2,1,0:T(8,128)S(1)}, u32[]{:S(2)}, u32[]{:S(2)}) collective-permute-start(f32[25,16,128]{2,1,0:T(8,128)S(1)} %get-tuple-element.37), channel_id=1, source_target_pairs={{32,0},{64,32},{96,64},{128,96},{160,128},{192,160},{224,192},{33,... | collective-permute-start | bytes 614408 | tf_op jit(solution)/shard_map/ppermute | solution.py:742
  101.5 6.1 %collective-permute-start.4 = (f32[14,16,128]{2,1,0:T(8,128)S(1)}, f32[14,16,128]{2,1,0:T(8,128)S(1)}, u32[]{:S(2)}, u32[]{:S(2)}) collective-permute-start(f32[14,16,128]{2,1,0:T(8,128)S(1)} %get-tuple-element.36), channel_id=1, source_target_pairs={{0,32},{32,64},{64,96},{96,128},{128,160},{160,192},{192,224},{1,3... | collective-permute-start | bytes 344072 | tf_op jit(solution)/shard_map/ppermute | solution.py:742
  108.4 10.7 %collective-permute-start.7 = (f32[25,16,128]{2,1,0:T(8,128)S(1)}, f32[25,16,128]{2,1,0:T(8,128)S(1)}, u32[]{:S(2)}, u32[]{:S(2)}) collective-permute-start(f32[25,16,128]{2,1,0:T(8,128)S(1)} %get-tuple-element.39), channel_id=1, source_target_pairs={{8,0},{16,8},{24,16},{9,1},{17,9},{25,17},{10,2},{18,10},{26,18},{... | collective-permute-start | bytes 614408 | tf_op jit(solution)/shard_map/ppermute | solution.py:742
  112.4 6.7 %collective-permute-start.6 = (f32[14,16,128]{2,1,0:T(8,128)S(1)}, f32[14,16,128]{2,1,0:T(8,128)S(1)}, u32[]{:S(2)}, u32[]{:S(2)}) collective-permute-start(f32[14,16,128]{2,1,0:T(8,128)S(1)} %get-tuple-element.38), channel_id=1, source_target_pairs={{0,8},{8,16},{16,24},{1,9},{9,17},{17,25},{2,10},{10,18},{18,26},{... | collective-permute-start | bytes 344072 | tf_op jit(solution)/shard_map/ppermute | solution.py:742

commit v5 on v4

--- a/solution.py
+++ b/solution.py
@@ -11,7 +11,7 @@
 BF16 = jnp.bfloat16
 SCALE = math.sqrt(math.log2(math.e) / 0.08)
 DT = 0.2
-PARAMS = pltpu.CompilerParams(vmem_limit_bytes=28 * 2**20)
+PARAMS = pltpu.CompilerParams(vmem_limit_bytes=20 * 2**20)
 VMEM = pl.BlockSpec(memory_space=pltpu.VMEM)
 SMEM = pl.BlockSpec(memory_space=pltpu.SMEM)
 HELD = pl.BlockSpec(memory_space=pltpu.VMEM)
@@ -111,7 +111,8 @@
 
 
 def prep_kernel(at_ref, *refs):
-    far, (out_ref, field_ref, square_ref), near, sems = refs[:8], refs[8:11], refs[11:19], refs[19]
+    far, (out_ref, field_ref, square_ref) = refs[:8], refs[8:11]
+    near, sems = refs[11:19], refs[19]
     copies = [pltpu.make_async_copy(a, b, sems.at[n]) for n, (a, b) in enumerate(zip(far, near))]
     for copy in copies:
         copy.start()
@@ -143,7 +144,8 @@
         out_ref[dest, PLANES:ROWS_1, :] = rows
 
 
-def plan_kernel(at_ref, all_ref, list_ref, task_ref):
+def plan_kernel(at_ref, all_ref, *refs, steps):
+    list_ref, task_ref = refs[-2:]
     me = at_ref[2]
     lane = iota((1, 128), 1)
     block_of = iota((128, 128), 0).astype(F32)
@@ -171,7 +173,7 @@
     def prefix(x):
         return jnp.dot(jnp.broadcast_to(x, (8, 128)).astype(BF16), upper, preferred_element_type=F32)[0:1]
 
-    for step in range(4):
+    for step in steps:
         keys = all_ref[0, KEYS + step : KEYS + 1 + step, :]
         for src in range(1, 8):
             keys = keys + all_ref[src, KEYS + step : KEYS + 1 + step, :]
@@ -237,8 +239,7 @@
 UNROLL = 8
 
 
-def pair_loop(list_ref, step, first_row, me, all_ref, turned_ref, force_ref, sum_ref):
-    force_ref[...] = jnp.zeros_like(force_ref)
+def pair_loop(list_ref, step, first_row, me, all_ref, turned_ref, force_ref, part=(0, 1)):
     for c in range(3):
         turned_ref[16, :, c] = jnp.zeros((4, 8, 128), F32)
         for s in range(16):
@@ -276,7 +277,12 @@
                     force_ref[slot, a, c] += out[a][c]
         return carry
 
-    lax.fori_loop(0, (list_ref[4 + step, 0] + (UNROLL - 1)) // UNROLL, body, 0)
+    groups = (list_ref[4 + step, 0] + (UNROLL - 1)) // UNROLL
+    at, of = part
+    lax.fori_loop(groups * at // of, groups * (at + 1) // of, body, 0)
+
+
+def block_sums(force_ref, sum_ref):
     for c in range(3):
         total = force_ref[0:16, 0, c]
         for a in range(1, 4):
@@ -295,19 +301,29 @@
     return jnp.where(iota((rows, 128), 0).astype(F32) == at, 1.0, 0.0)
 
 
-def scatter_own(sum_ref, all_ref, me, lhs_ref, lanes_ref):
+def hot_rows_lanes(ids):
+    row, lane = row_and_lane(ids)
+    return one_hot(row, 96).astype(BF16), one_hot(lane, 128)
+
+
+def first_plan_kernel(at_ref, all_ref, list_ref, task_ref, rows_ref, lanes_ref):
+    plan_kernel(at_ref, all_ref, list_ref, task_ref, steps=(0, 1))
     for s in range(16):
         at = slice(128 * s, 128 * s + 128)
-        row, lane = row_and_lane(all_ref[me, NODES + s : NODES + s + 1, :])
-        hot = one_hot(row, 96)
-        lanes_ref[:, at] = one_hot(lane, 128).astype(BF16)
+        rows_ref[:, at], lanes = hot_rows_lanes(all_ref[at_ref[2], NODES + s : NODES + s + 1, :])
+        lanes_ref[at, :] = jnp.transpose(lanes).astype(BF16)
+
+
+def scatter_own(force_ref, sum_ref, rows_ref, lanes_ref, lhs_ref):
+    block_sums(force_ref, sum_ref)
+    for s in range(16):
+        at = slice(128 * s, 128 * s + 128)
+        hot = rows_ref[:, at]
         for c in range(3):
             hi, lo = split2(sum_ref[c, s : s + 1, :])
-            lhs_ref[96 * c : 96 * c + 96, at] = (hot * hi.astype(F32)).astype(BF16)
-            lhs_ref[288 + 96 * c : 384 + 96 * c, at] = (hot * lo.astype(F32)).astype(BF16)
-    out = lax.dot_general(
-        lhs_ref[...], lanes_ref[...], (((1,), (1,)), ((), ())), preferred_element_type=F32
-    )
+            lhs_ref[96 * c : 96 * c + 96, at] = hot * hi
+            lhs_ref[288 + 96 * c : 384 + 96 * c, at] = hot * lo
+    out = jnp.dot(lhs_ref[...], lanes_ref[...], preferred_element_type=F32)
     return (out[:288] + out[288:]).reshape(3, 12, 8, 128)
 
 
@@ -422,9 +438,9 @@
 
 
 def first_contact_kernel(
-    at_ref, list_ref, task_ref, all_ref, field_ref,
+    at_ref, list_ref, task_ref, all_ref, field_ref, rows_ref, lanes_ref,
     fm_ref, c0_ref, m1_ref, up_ref, down_ref,
-    turned_ref, force_ref, sum_ref, lhs_ref, lanes_ref, square_ref, *rim,
+    turned_ref, force_ref, sum_ref, lhs_ref, square_ref, *rim,
 ):
     me = at_ref[2]
     planes = neighbour_planes(all_ref, PLANES, 4, me, square_ref, 12)
@@ -436,8 +452,9 @@
     fm_ref[3] = sums[3]
     for c in range(3):
         fm_ref[c] = sums[c]
-    pair_loop(list_ref, 0, 0, me, all_ref, turned_ref, force_ref, sum_ref)
-    own = scatter_own(sum_ref, all_ref, me, lhs_ref, lanes_ref)
+    force_ref[...] = jnp.zeros_like(force_ref)
+    pair_loop(list_ref, 0, 0, me, all_ref, turned_ref, force_ref)
+    own = scatter_own(force_ref, sum_ref, rows_ref, lanes_ref, lhs_ref)
     rim = contact_rim(list_ref, task_ref, 0, 0, me, all_ref, all_ref, rim, square_ref)
     for c in range(3):
         full = jnp.concatenate([both(fill16(own[c]), unpack(rim, c)), zero], axis=0)
@@ -449,11 +466,11 @@
 
 
 def step_contact_kernel(
-    at_ref, list_ref, all_ref, out_ref, turned_ref, force_ref, sum_ref, lhs_ref, lanes_ref
+    at_ref, list_ref, all_ref, rows_ref, lanes_ref, out_ref, turned_ref, force_ref, sum_ref, lhs_ref
 ):
-    me = at_ref[2]
-    pair_loop(list_ref, 1, 0, me, all_ref, turned_ref, force_ref, sum_ref)
-    out_ref[...] = scatter_own(sum_ref, all_ref, me, lhs_ref, lanes_ref)
+    force_ref[...] = jnp.zeros_like(force_ref)
+    pair_loop(list_ref, 1, 0, at_ref[2], all_ref, turned_ref, force_ref)
+    out_ref[...] = scatter_own(force_ref, sum_ref, rows_ref, lanes_ref, lhs_ref)
 
 
 def shift_rows(x, by):
@@ -490,7 +507,7 @@
     return out, extend(take(m1_ref[...]), get_plane(ups_ref, 8, 9), None, None)
 
 
-def y_send_1_kernel(fm_ref, m1_ref, ups_ref, downs_ref, up_ref, down_ref):
+def y_send_1_kernel(fm_ref, m1_ref, ups_ref, downs_ref, task_ref, up_ref, down_ref):
     fields, m1 = x_extended_1(fm_ref, m1_ref, ups_ref, downs_ref, (0, 11, 12))
     send_planes([f[1] for f in fields] + [f[2] for f in fields] + [m1[1]], up_ref)
     send_planes([f[0] for f in fields], down_ref)
@@ -532,16 +549,18 @@
     hot = rows_ref[...]
     values = []
     for c in range(3):
-        hi, lo = split2(disp[c])
-        field = jnp.concatenate([hi, lo], axis=0)
-        picked = lax.dot_general(field, hot, (((0,), (0,)), ((), ())), preferred_element_type=F32)
-        values.append(jnp.sum(picked * lanes_ref[...].astype(F32), axis=0, keepdims=True))
+        picked = [
+            lax.dot_general(part, hot, (((0,), (0,)), ((), ())), preferred_element_type=F32)
+            for part in split2(disp[c])
+        ]
+        picked = picked[0] + picked[1]
+        values.append(jnp.sum(picked * lanes_ref[...], axis=0, keepdims=True))
     return values
 
 
 def second_step_kernel(
-    at_ref, fm_ref, c0_ref, m1_ref, xu_ref, xd_ref, yu_ref, yd_ref, c1_ref, all_ref,
-    out_ref, state_ref, rows_ref, lanes_ref, square_ref,
+    at_ref, fm_ref, c0_ref, m1_ref, xu_ref, xd_ref, yu_ref, yd_ref, c1_ref, all_ref, rows_ref,
+    out_ref, state_ref, square_ref, lanes_ref,
 ):
     fields, m1 = x_extended_1(fm_ref, m1_ref, xu_ref, xd_ref, range(13))
     zero = jnp.zeros((1, 16, 256), F32)
@@ -577,12 +596,7 @@
     state_ref[9] = shift_rows(jnp.where(good, inv, 0.0), -1)
     me = at_ref[2]
     for s in range(16):
-        at = slice(128 * s, 128 * s + 128)
-        r, l = row_and_lane(all_ref[me, NODES + s : NODES + s + 1, :])
-        hot = one_hot(r, 96).astype(BF16)
-        rows_ref[0:96, at] = hot
-        rows_ref[96:192, at] = hot
-        lanes_ref[:, at] = one_hot(l, 128).astype(BF16)
+        lanes_ref[:, 128 * s : 128 * s + 128] = hot_rows_lanes(all_ref[me, NODES + s : NODES + s + 1, :])[1]
     for first, disp in (
         (0, [shift_rows(d[1:13], -1)[:, :8, :128] for d in disp1]),
         (LATE, [d[0:12, :8, :128] for d in disp2s]),
@@ -617,9 +631,9 @@
 
 
 def late_contact_kernel(
-    at_ref, list_ref, task_ref, first_ref, all_ref, state_ref, field_ref,
+    at_ref, list_ref, task_ref, first_ref, all_ref, state_ref, field_ref, rows_ref, lanes_ref,
     own_ref, up_ref, down_ref,
-    turned_ref, force_ref, sum_ref, lhs_ref, lanes_ref, square_ref, *rims,
+    turned_ref, force_ref, sum_ref, lhs_ref, square_ref, *rims,
 ):
     me = at_ref[2]
     zplanes = neighbour_planes(all_ref, PLANES_2, 5, me, square_ref, 13)
@@ -640,8 +654,9 @@
         m = both(fill16(field_ref[3 + step]), unpack(mplanes, 3 + step, 4))
         own_ref[n] = jnp.concatenate([m, zero], axis=0)
     for step, first_row, n in ((2, 0, 3), (3, LATE, 6)):
-        pair_loop(list_ref, step, first_row, me, all_ref, turned_ref, force_ref, sum_ref)
-        own = scatter_own(sum_ref, first_ref, me, lhs_ref, lanes_ref)
+        force_ref[...] = jnp.zeros_like(force_ref)
+        pair_loop(list_ref, step, first_row, me, all_ref, turned_ref, force_ref)
+        own = scatter_own(force_ref, sum_ref, rows_ref, lanes_ref, lhs_ref)
         rim = contact_rim(list_ref, task_ref, step, first_row, me, all_ref, first_ref, rims, square_ref)
         for c in range(3):
             full = both(fill16(own[c]), unpack(rim, c))
@@ -751,7 +766,6 @@
     pltpu.VMEM((16, 128), F32),
 ]
 LHS = pltpu.VMEM((576, 2048), BF16)
-LANES = pltpu.VMEM((128, 2048), BF16)
 SQUARE = pltpu.VMEM((128, 128), F32)
 
 
@@ -770,42 +784,52 @@
         (1,),
     )(at, *params)
     everyone = share(payload)
-    lists, tasks = call(plan_kernel, [((12, 512), jnp.int32), ((4, 4, 8, 128), F32)], [SMEM, HELD], (), (1,))(at, everyone)
+    plan_out = [((12, 512), jnp.int32), ((4, 4, 8, 128), F32)]
+    lists, tasks, *hot = call(
+        first_plan_kernel,
+        plan_out + [((96, 2048), BF16), ((2048, 128), BF16)],
+        [SMEM, HELD],
+        (),
+        (1, 2, 3),
+    )(at, everyone)
     fm, c0, m1, up, down = call(
         first_contact_kernel,
         [((4, 13, 16, 256), F32), ((3, 13, 16, 256), F32), ((13, 16, 256), F32), ((10, 16, 128), F32),
          ((5, 16, 128), F32)],
-        [SMEM, SMEM, HELD, HELD, HELD],
-        [TURNED, TURNED, SUMS, LHS, LANES, SQUARE] + RIM,
+        [SMEM, SMEM] + [HELD] * 5,
+        [TURNED, TURNED, SUMS, LHS, SQUARE] + RIM,
         (0, 1, 2),
-    )(at, lists, tasks, everyone, fields)
+    )(at, lists, tasks, everyone, fields, *hot)
     xu, xd = neighbours(up, down, "gx")
+    late_lists, late_tasks = call(
+        functools.partial(plan_kernel, steps=(2, 3)), plan_out, [SMEM, HELD, HELD], (), (1,)
+    )(at, everyone, m1)
+    up, down = call(y_send_1_kernel, [((10, 16, 128), F32), ((5, 16, 128), F32)], [HELD] * 5)(
+        fm, m1, xu, xd, late_tasks
+    )
+    yu, yd = neighbours(up, down, "gy")
     (c1,) = call(
         step_contact_kernel,
         [((3, 12, 8, 128), F32)],
-        [SMEM, SMEM, HELD],
-        [TURNED, TURNED, SUMS, LHS, LANES],
+        [SMEM, SMEM] + [HELD] * 3,
+        [TURNED, TURNED, SUMS, LHS],
         (0,),
-    )(at, lists, everyone)
-    up, down = call(y_send_1_kernel, [((10, 16, 128), F32), ((5, 16, 128), F32)], [HELD] * 4)(
-        fm, m1, xu, xd
-    )
-    yu, yd = neighbours(up, down, "gy")
+    )(at, lists, everyone, *hot)
     payload, state = call(
         second_step_kernel,
         [((8, ROWS_2, 128), F32), ((10, 13, 16, 256), F32)],
-        [SMEM] + [HELD] * 9,
-        [pltpu.VMEM((192, 2048), BF16), LANES, SQUARE],
+        [SMEM] + [HELD] * 10,
+        [SQUARE, pltpu.VMEM((128, 2048), F32)],
         (1,),
-    )(at, fm, c0, m1, xu, xd, yu, yd, c1, everyone)
+    )(at, fm, c0, m1, xu, xd, yu, yd, c1, everyone, hot[0])
     late = share(payload)
     own, up, down = call(
         late_contact_kernel,
         [((12, 13, 16, 256), F32), ((UPS + 1, 16, 128), F32), ((DOWNS + 2, 16, 128), F32)],
-        [SMEM, SMEM] + [HELD] * 5,
-        [TURNED, TURNED, SUMS, LHS, LANES, SQUARE] + RIM,
+        [SMEM, SMEM] + [HELD] * 7,
+        [TURNED, TURNED, SUMS, LHS, SQUARE] + RIM,
         (0,),
-    )(at, lists, tasks, everyone, late, state, fields)
+    )(at, late_lists, late_tasks, everyone, late, state, fields, *hot)
     xu, xd = neighbours(up, down, "gx")
     up, down = call(
         y_send_2_kernel,

time: 125 us -> 123 us (0.984)
  waiting for transfers between devices: 10.1 us -> 7.21 us
    ppermute x4, waiting for transfers between devices: 1.66 us -> 0.07 us  [neighbours(): lax.ppermute(down, axis, [(j, i) for i, j in ahead])]
    ppermute x4, starting transfers between devices: 13.5 us -> 12 us  [neighbours(): lax.ppermute(down, axis, [(j, i) for i, j in ahead])]
    ppermute x4, starting transfers between devices: 8.17 us -> 9.57 us  [neighbours(): lax.ppermute(up, axis, ahead)]
    ppermute x4, waiting for transfers between devices: 8.45 us -> 7.14 us  [neighbours(): lax.ppermute(up, axis, ahead)]
    pallas_call x9 -> x10, Pallas kernels: 41.9 us -> 42.5 us  [run(): pl.pallas_call(kernel, out_shape=[pltpu.VMEM(s, d) if n in held else jax....]
  transfers between devices with their start and end apart: 8 -> 8, of which waited for: 3 -> 3; matrix products, arithmetic and copies ran while one was open for 0% -> 0% of each run, Pallas kernels for 4% -> 7%
where the time goes in v5:
time: 123 us; the launch traced here: 122 us
  blocking collectives  49.8 us (40%)
  Pallas kernels  42.5 us (35%)
  starting transfers between devices  21.6 us (18%)
  waiting for transfers between devices  7.21 us (6%)
    all_to_all x2, blocking collectives, share(): return lax.all_to_all(blocks, 'gz', split_axis=0, concat_axis=0, tiled=True)  49.8 us
    pallas_call x10, Pallas kernels, run(): pl.pallas_call(kernel, out_shape=[pltpu.VMEM(s, d) if n in held else jax....  42.5 us
    ppermute x4, starting transfers between devices, neighbours(): lax.ppermute(down, axis, [(j, i) for i, j in ahead])  12 us
    ppermute x4, starting transfers between devices, neighbours(): lax.ppermute(up, axis, ahead)  9.57 us
    ppermute x4, waiting for transfers between devices, neighbours(): lax.ppermute(up, axis, ahead)  7.14 us
  transfers between devices with their start and end apart: 8, of which 3 were waited for; matrix products, arithmetic and copies ran while one was open for 0% of the time, Pallas kernels for 7%

profile of v5, /device:TPU:80, one launch (start us, length us, event | category | flops | bytes accessed | tf_op | source)
XLA Modules:
  0.0 122.0 jit_solution(14035913815964198528)
XLA Ops:
  0.6 0.1 pad_add_fusion.at_ref
  0.7 2.0 %shard_map.95 = (f32[8,104,128]{2,1,0:T(8,128)S(1)}, f32[7,12,8,128]{3,2,1,0:T(8,128)S(1)}) custom-call(s32[3]{0:T(128)S(1)} %pad_add_fusion.at_ref, f32[3,16,128]{2,1,0:T(8,128)} %bitcast.17, s32[4,16]{1,0:T(4,128)} %refs_1_.1, s32[4,2,64]{2,1,0:T(2,128)} %bitcast.18, s32[16,128]{1,0:T(8,128)} %refs_3_.1, f32[12,8,128]{2,1,0:T(8,128)} %bitcast.15, ...), custom_call_target="tpu_custom_call" | custom-call | tf_op jit(solution)/shard_map/pallas_call | solution.py:735
  2.8 26.5 %all_to_all.10.all_ref.first_ref = f32[8,104,128]{2,1,0:T(8,128)S(1)} all-to-all(f32[8,104,128]{2,1,0:T(8,128)S(1)} %get-tuple-element.26), channel_id=1, replica_groups=mesh['gx'=8,'gy'=4,'gz'=8] {'gz'}, dimensions={0} | all-to-all | bytes 851968 | tf_op jit(solution)/shard_map/all_to_all | solution.py:751
  29.3 1.9 %shard_map.96 = (s32[12,512]{1,0:T(8,128)S(1)}, f32[4,4,8,128]{3,2,1,0:T(8,128)S(1)}, bf16[96,2048]{1,0:T(8,128)(2,1)S(1)}, bf16[2048,128]{1,0:T(8,128)(2,1)S(1)}) custom-call(s32[3]{0:T(128)S(1)} %pad_add_fusion.at_ref, f32[8,104,128]{2,1,0:T(8,128)S(1)} %all_to_all.10.all_ref.first_ref), custom_call_target="tpu_custom_call" | custom-call | tf_op jit(solution)/shard_map/pallas_call | solution.py:735
  31.2 6.6 %shard_map.97 = (f32[4,13,16,256]{3,2,1,0:T(8,128)S(1)}, f32[3,13,16,256]{3,2,1,0:T(8,128)S(1)}, f32[13,16,256]{2,1,0:T(8,128)S(1)}, f32[10,16,128]{2,1,0:T(8,128)S(1)}, f32[5,16,128]{2,1,0:T(8,128)S(1)}) custom-call(s32[3]{0:T(128)S(1)} %pad_add_fusion.at_ref, s32[12,512]{1,0:T(8,128)S(1)} %get-tuple-element.27.list_ref, ...), custom_call_target="tpu_custom_call" | custom-call | tf_op jit(solution)/shard_map/pallas_call | solution.py:735
  37.8 1.9 %collective-permute-start = (f32[10,16,128]{2,1,0:T(8,128)S(1)}, f32[10,16,128]{2,1,0:T(8,128)S(1)}, u32[]{:S(2)}, u32[]{:S(2)}) collective-permute-start(f32[10,16,128]{2,1,0:T(8,128)S(1)} %get-tuple-element.37), channel_id=1, source_target_pairs={{0,32},{32,64},{64,96},{96,128},{128,160},{160,192},{192,224},{1,3... | collective-permute-start | bytes 245768 | tf_op jit(solution)/shard_map/ppermute | solution.py:757
  39.7 3.6 %collective-permute-start.1 = (f32[5,16,128]{2,1,0:T(8,128)S(1)}, f32[5,16,128]{2,1,0:T(8,128)S(1)}, u32[]{:S(2)}, u32[]{:S(2)}) collective-permute-start(f32[5,16,128]{2,1,0:T(8,128)S(1)} %get-tuple-element.38), channel_id=1, source_target_pairs={{32,0},{64,32},{96,64},{128,96},{160,128},{192,160},{224,192},{33,... | collective-permute-start | bytes 122888 | tf_op jit(solution)/shard_map/ppermute | solution.py:757
  43.4 1.6 %shard_map.98 = (s32[12,512]{1,0:T(8,128)S(1)}, f32[4,4,8,128]{3,2,1,0:T(8,128)S(1)}) custom-call(s32[3]{0:T(128)S(1)} %pad_add_fusion.at_ref, f32[8,104,128]{2,1,0:T(8,128)S(1)} %all_to_all.10.all_ref.first_ref, f32[13,16,256]{2,1,0:T(8,128)S(1)} %get-tuple-element.32.refs_0_.m1_ref), custom_call_target="tpu_custom_call" | custom-call | tf_op jit(solution)/shard_map/pallas_call | solution.py:735
  45.0 0.1 collective-permute-done.1.downs_ref.xd_ref
  45.0 0.0 collective-permute-done.ups_ref.xu_ref
  45.0 0.2 shard_map.99
  45.2 1.9 %collective-permute-start.2 = (f32[10,16,128]{2,1,0:T(8,128)S(1)}, f32[10,16,128]{2,1,0:T(8,128)S(1)}, u32[]{:S(2)}, u32[]{:S(2)}) collective-permute-start(f32[10,16,128]{2,1,0:T(8,128)S(1)} %get-tuple-element.39), channel_id=1, source_target_pairs={{0,8},{8,16},{16,24},{1,9},{9,17},{17,25},{2,10},{10,18},{18,26},{... | collective-permute-start | bytes 245768 | tf_op jit(solution)/shard_map/ppermute | solution.py:757
  47.2 3.9 %collective-permute-start.3 = (f32[5,16,128]{2,1,0:T(8,128)S(1)}, f32[5,16,128]{2,1,0:T(8,128)S(1)}, u32[]{:S(2)}, u32[]{:S(2)}) collective-permute-start(f32[5,16,128]{2,1,0:T(8,128)S(1)} %get-tuple-element.40), channel_id=1, source_target_pairs={{8,0},{16,8},{24,16},{9,1},{17,9},{25,17},{10,2},{18,10},{26,18},{... | collective-permute-start | bytes 122888 | tf_op jit(solution)/shard_map/ppermute | solution.py:757
  51.1 6.7 %shard_map.100.c1_ref = f32[3,12,8,128]{3,2,1,0:T(8,128)S(1)} custom-call(s32[3]{0:T(128)S(1)} %pad_add_fusion.at_ref, s32[12,512]{1,0:T(8,128)S(1)} %get-tuple-element.27.list_ref, f32[8,104,128]{2,1,0:T(8,128)S(1)} %all_to_all.10.all_ref.first_ref, bf16[96,2048]{1,0:T(8,128)(2,1)S(1)} %get-tuple-element.30.rows_ref, ...), custom_call_target="tpu_custom_call" | custom-call | tf_op jit(solution)/shard_map/pallas_call | solution.py:735
  57.8 0.0 collective-permute-done.3.yd_ref
  57.8 0.0 collective-permute-done.2.yu_ref
  57.8 3.8 %shard_map.101 = (f32[8,128,128]{2,1,0:T(8,128)S(1)}, f32[10,13,16,256]{3,2,1,0:T(8,128)S(1)}) custom-call(s32[3]{0:T(128)S(1)} %pad_add_fusion.at_ref, f32[4,13,16,256]{3,2,1,0:T(8,128)S(1)} %get-tuple-element.35.fm_ref, f32[3,13,16,256]{3,2,1,0:T(8,128)S(1)} %get-tuple-element.36.c0_ref, f32[13,16,256]{2,1,0:T(8,128)S(1)} %get-tuple-element.32.refs_0_.m1_ref, ...), custom_call_target="tpu_custom_call" | custom-call | tf_op jit(solution)/shard_map/pallas_call | solution.py:735
  61.6 23.3 %all_to_all.11.all_ref = f32[8,128,128]{2,1,0:T(8,128)S(1)} all-to-all(f32[8,128,128]{2,1,0:T(8,128)S(1)} %get-tuple-element.41), channel_id=1, replica_groups=mesh['gx'=8,'gy'=4,'gz'=8] {'gz'}, dimensions={0} | all-to-all | bytes 1048576 | tf_op jit(solution)/shard_map/all_to_all | solution.py:751
  85.0 13.4 %shard_map.102 = (f32[12,13,16,256]{3,2,1,0:T(8,128)S(1)}, f32[14,16,128]{2,1,0:T(8,128)S(1)}, f32[25,16,128]{2,1,0:T(8,128)S(1)}) custom-call(s32[3]{0:T(128)S(1)} %pad_add_fusion.at_ref, s32[12,512]{1,0:T(8,128)S(1)} %get-tuple-element.33.list_ref, f32[4,4,8,128]{3,2,1,0:T(8,128)S(1)} %get-tuple-element.34.task_ref, ...), custom_call_target="tpu_custom_call" | custom-call | tf_op jit(solution)/shard_map/pallas_call | solution.py:735
  98.4 1.9 %collective-permute-start.5 = (f32[25,16,128]{2,1,0:T(8,128)S(1)}, f32[25,16,128]{2,1,0:T(8,128)S(1)}, u32[]{:S(2)}, u32[]{:S(2)}) collective-permute-start(f32[25,16,128]{2,1,0:T(8,128)S(1)} %get-tuple-element.45), channel_id=1, source_target_pairs={{32,0},{64,32},{96,64},{128,96},{160,128},{192,160},{224,192},{33,... | collective-permute-start | bytes 614408 | tf_op jit(solution)/shard_map/ppermute | solution.py:757
  100.3 2.4 %collective-permute-start.4 = (f32[14,16,128]{2,1,0:T(8,128)S(1)}, f32[14,16,128]{2,1,0:T(8,128)S(1)}, u32[]{:S(2)}, u32[]{:S(2)}) collective-permute-start(f32[14,16,128]{2,1,0:T(8,128)S(1)} %get-tuple-element.44), channel_id=1, source_target_pairs={{0,32},{32,64},{64,96},{96,128},{128,160},{160,192},{192,224},{1,3... | collective-permute-start | bytes 344072 | tf_op jit(solution)/shard_map/ppermute | solution.py:757
  102.8 3.7 %collective-permute-done.4.ups_ref.xu_ref = f32[14,16,128]{2,1,0:T(8,128)S(1)} collective-permute-done((f32[14,16,128]{2,1,0:T(8,128)S(1)}, f32[14,16,128]{2,1,0:T(8,128)S(1)}, u32[]{:S(2)}, u32[]{:S(2)}) %collective-permute-start.4) | collective-permute-done | bytes 114720 | tf_op jit(solution)/shard_map/ppermute | solution.py:757
  106.5 0.0 collective-permute-done.5.downs_ref.xd_ref
  106.5 0.8 shard_map.103
  107.2 2.5 %collective-permute-start.7 = (f32[25,16,128]{2,1,0:T(8,128)S(1)}, f32[25,16,128]{2,1,0:T(8,128)S(1)}, u32[]{:S(2)}, u32[]{:S(2)}) collective-permute-start(f32[25,16,128]{2,1,0:T(8,128)S(1)} %get-tuple-element.47), channel_id=1, source_target_pairs={{8,0},{16,8},{24,16},{9,1},{17,9},{25,17},{10,2},{18,10},{26,18},{... | collective-permute-start | bytes 614408 | tf_op jit(solution)/shard_map/ppermute | solution.py:757
  109.8 3.3 %collective-permute-start.6 = (f32[14,16,128]{2,1,0:T(8,128)S(1)}, f32[14,16,128]{2,1,0:T(8,128)S(1)}, u32[]{:S(2)}, u32[]{:S(2)}) collective-permute-start(f32[14,16,128]{2,1,0:T(8,128)S(1)} %get-tuple-element.46), channel_id=1, source_target_pairs={{0,8},{8,16},{16,24},{1,9},{9,17},{17,25},{2,10},{10,18},{18,26},{... | collective-permute-start | bytes 344072 | tf_op jit(solution)/shard_map/ppermute | solution.py:757
  113.1 3.4 %collective-permute-done.6.yu_ref = f32[14,16,128]{2,1,0:T(8,128)S(1)} collective-permute-done((f32[14,16,128]{2,1,0:T(8,128)S(1)}, f32[14,16,128]{2,1,0:T(8,128)S(1)}, u32[]{:S(2)}, u32[]{:S(2)}) %collective-permute-start.6) | collective-permute-done | bytes 114720 | tf_op jit(solution)/shard_map/ppermute | solution.py:757
  116.5 0.0 collective-permute-done.7.yd_ref
  116.6 5.4 %shard_map.104 = (f32[3,12,8,128]{3,2,1,0:T(8,128)}, f32[6,12,8,128]{3,2,1,0:T(8,128)}) custom-call(s32[3]{0:T(128)S(1)} %pad_add_fusion.at_ref, f32[12,13,16,256]{3,2,1,0:T(8,128)S(1)} %get-tuple-element.43.own_ref, f32[14,16,128]{2,1,0:T(8,128)S(1)} %collective-permute-done.4.ups_ref.xu_ref, f32[25,16,128]{2,1,0:T(8,128)S(1)} %collective-permute-done.5.downs_ref.xd_ref, ...), custom_call_target="tpu_custom_call" | custom-call | tf_op jit(solution)/shard_map/pallas_call | solution.py:735
Async XLA Ops:
  37.8 7.2 %collective-permute-start = (f32[10,16,128]{2,1,0:T(8,128)S(1)}, f32[10,16,128]{2,1,0:T(8,128)S(1)}, u32[]{:S(2)}, u32[]{:S(2)}) collective-permute-start(f32[10,16,128]{2,1,0:T(8,128)S(1)} %get-tuple-element.37), channel_id=1, source_target_pairs={{0,32},{32,64},{64,96},{96,128},{128,160},{160,192},{192,224},{1,3... | collective-permute-start | bytes 245768 | tf_op jit(solution)/shard_map/ppermute | solution.py:757
  39.7 5.3 %collective-permute-start.1 = (f32[5,16,128]{2,1,0:T(8,128)S(1)}, f32[5,16,128]{2,1,0:T(8,128)S(1)}, u32[]{:S(2)}, u32[]{:S(2)}) collective-permute-start(f32[5,16,128]{2,1,0:T(8,128)S(1)} %get-tuple-element.38), channel_id=1, source_target_pairs={{32,0},{64,32},{96,64},{128,96},{160,128},{192,160},{224,192},{33,... | collective-permute-start | bytes 122888 | tf_op jit(solution)/shard_map/ppermute | solution.py:757
  45.2 12.6 %collective-permute-start.2 = (f32[10,16,128]{2,1,0:T(8,128)S(1)}, f32[10,16,128]{2,1,0:T(8,128)S(1)}, u32[]{:S(2)}, u32[]{:S(2)}) collective-permute-start(f32[10,16,128]{2,1,0:T(8,128)S(1)} %get-tuple-element.39), channel_id=1, source_target_pairs={{0,8},{8,16},{16,24},{1,9},{9,17},{17,25},{2,10},{10,18},{18,26},{... | collective-permute-start | bytes 245768 | tf_op jit(solution)/shard_map/ppermute | solution.py:757
  47.2 10.7 %collective-permute-start.3 = (f32[5,16,128]{2,1,0:T(8,128)S(1)}, f32[5,16,128]{2,1,0:T(8,128)S(1)}, u32[]{:S(2)}, u32[]{:S(2)}) collective-permute-start(f32[5,16,128]{2,1,0:T(8,128)S(1)} %get-tuple-element.40), channel_id=1, source_target_pairs={{8,0},{16,8},{24,16},{9,1},{17,9},{25,17},{10,2},{18,10},{26,18},{... | collective-permute-start | bytes 122888 | tf_op jit(solution)/shard_map/ppermute | solution.py:757
  98.4 8.0 %collective-permute-start.5 = (f32[25,16,128]{2,1,0:T(8,128)S(1)}, f32[25,16,128]{2,1,0:T(8,128)S(1)}, u32[]{:S(2)}, u32[]{:S(2)}) collective-permute-start(f32[25,16,128]{2,1,0:T(8,128)S(1)} %get-tuple-element.45), channel_id=1, source_target_pairs={{32,0},{64,32},{96,64},{128,96},{160,128},{192,160},{224,192},{33,... | collective-permute-start | bytes 614408 | tf_op jit(solution)/shard_map/ppermute | solution.py:757
  100.3 6.1 %collective-permute-start.4 = (f32[14,16,128]{2,1,0:T(8,128)S(1)}, f32[14,16,128]{2,1,0:T(8,128)S(1)}, u32[]{:S(2)}, u32[]{:S(2)}) collective-permute-start(f32[14,16,128]{2,1,0:T(8,128)S(1)} %get-tuple-element.44), channel_id=1, source_target_pairs={{0,32},{32,64},{64,96},{96,128},{128,160},{160,192},{192,224},{1,3... | collective-permute-start | bytes 344072 | tf_op jit(solution)/shard_map/ppermute | solution.py:757
  107.2 9.3 %collective-permute-start.7 = (f32[25,16,128]{2,1,0:T(8,128)S(1)}, f32[25,16,128]{2,1,0:T(8,128)S(1)}, u32[]{:S(2)}, u32[]{:S(2)}) collective-permute-start(f32[25,16,128]{2,1,0:T(8,128)S(1)} %get-tuple-element.47), channel_id=1, source_target_pairs={{8,0},{16,8},{24,16},{9,1},{17,9},{25,17},{10,2},{18,10},{26,18},{... | collective-permute-start | bytes 614408 | tf_op jit(solution)/shard_map/ppermute | solution.py:757
  109.8 6.8 %collective-permute-start.6 = (f32[14,16,128]{2,1,0:T(8,128)S(1)}, f32[14,16,128]{2,1,0:T(8,128)S(1)}, u32[]{:S(2)}, u32[]{:S(2)}) collective-permute-start(f32[14,16,128]{2,1,0:T(8,128)S(1)} %get-tuple-element.46), channel_id=1, source_target_pairs={{0,8},{8,16},{16,24},{1,9},{9,17},{17,25},{2,10},{10,18},{18,26},{... | collective-permute-start | bytes 344072 | tf_op jit(solution)/shard_map/ppermute | solution.py:757

commit v6 on v5

--- a/solution.py
+++ b/solution.py
@@ -233,10 +233,10 @@
             if part == 0:
                 write()
             else:
-                pl.when(count + 8.0 > 128.0 * part)(write)
-
-
-UNROLL = 8
+                pl.when(count + 16.0 > 128.0 * part)(write)
+
+
+UNROLL = 16
 
 
 def pair_loop(list_ref, step, first_row, me, all_ref, turned_ref, force_ref, part=(0, 1)):
@@ -433,25 +433,44 @@
     return both(ref[n], unpack(ref[count + n // 16], n % 16))
 
 
-def row_plane(x, i):
-    return fill16(x[:, i, :])
+class Halves:
+    def __init__(self, main, rim):
+        self.refs = (main, rim)
+
+    def __getitem__(self, at):
+        return both(*[ref[at] for ref in self.refs])
+
+    def __setitem__(self, at, value):
+        self.refs[0][at] = value[..., :128]
+        self.refs[1][at] = value[..., 128:]
+
+    def row(self, n, i):
+        lines = pl.ds(208 * n + i, 13, stride=16)
+        flat = [ref.reshape(ref.shape[0] * 208, 128) for ref in self.refs]
+        return fill16(both(*[ref[lines, :] for ref in flat]))
+
+    def set_row(self, n, i, plane):
+        lines = pl.ds(208 * n + i, 13, stride=16)
+        for t, ref in enumerate(self.refs):
+            ref.reshape(ref.shape[0] * 208, 128)[lines, :] = plane[:13, 128 * t : 128 * t + 128]
 
 
 def first_contact_kernel(
     at_ref, list_ref, task_ref, all_ref, field_ref, rows_ref, lanes_ref,
-    fm_ref, c0_ref, m1_ref, up_ref, down_ref,
+    fm_main_ref, fm_rim_ref, c0_ref, m1_ref, up_ref, down_ref,
     turned_ref, force_ref, sum_ref, lhs_ref, square_ref, *rim,
 ):
     me = at_ref[2]
+    fm = Halves(fm_main_ref, fm_rim_ref)
     planes = neighbour_planes(all_ref, PLANES, 4, me, square_ref, 12)
     sums = [node_sum(both(fill16(field_ref[n]), unpack(planes, n, 4))) for n in range(4)]
     m1 = both(fill16(field_ref[4]), unpack(planes, 4, 4))
     zero = jnp.zeros((1, 16, 256), F32)
     m1 = jnp.concatenate([m1, zero], axis=0)
     m1_ref[...] = m1
-    fm_ref[3] = sums[3]
+    fm[3] = sums[3]
     for c in range(3):
-        fm_ref[c] = sums[c]
+        fm[c] = sums[c]
     force_ref[...] = jnp.zeros_like(force_ref)
     pair_loop(list_ref, 0, 0, me, all_ref, turned_ref, force_ref)
     own = scatter_own(force_ref, sum_ref, rows_ref, lanes_ref, lhs_ref)
@@ -459,10 +478,10 @@
     for c in range(3):
         full = jnp.concatenate([both(fill16(own[c]), unpack(rim, c)), zero], axis=0)
         c0_ref[c] = full
-        fm_ref[c] = fm_ref[c] + full
-    ups = [row_plane(fm_ref[n], 7) for n in range(4)] + [row_plane(fm_ref[n], 8) for n in range(4)]
-    send_planes(ups + [row_plane(m1, 7)], up_ref)
-    send_planes([row_plane(fm_ref[n], 0) for n in range(4)], down_ref)
+        fm[c] = fm[c] + full
+    ups = [fm.row(n, 7) for n in range(4)] + [fm.row(n, 8) for n in range(4)]
+    send_planes(ups + [fill16(m1[:, 7, :])], up_ref)
+    send_planes([fm.row(n, 0) for n in range(4)], down_ref)
 
 
 def step_contact_kernel(
@@ -477,7 +496,7 @@
     return pltpu.roll(x, by % x.shape[1], 1)
 
 
-def x_extended_1(fm_ref, m1_ref, ups_ref, downs_ref, pick):
+def x_extended_1(fm, m1_ref, ups_ref, downs_ref, pick):
     lines = sorted(pick)
     row = iota((len(lines), 16, 256), 1)
 
@@ -497,7 +516,7 @@
 
     out = [
         extend(
-            take(fm_ref[n]),
+            take(fm[n]),
             get_plane(ups_ref, n, 9),
             get_plane(ups_ref, 4 + n, 9),
             get_plane(downs_ref, n, 4),
@@ -507,8 +526,8 @@
     return out, extend(take(m1_ref[...]), get_plane(ups_ref, 8, 9), None, None)
 
 
-def y_send_1_kernel(fm_ref, m1_ref, ups_ref, downs_ref, task_ref, up_ref, down_ref):
-    fields, m1 = x_extended_1(fm_ref, m1_ref, ups_ref, downs_ref, (0, 11, 12))
+def y_send_1_kernel(fm_main_ref, fm_rim_ref, m1_ref, ups_ref, downs_ref, task_ref, up_ref, down_ref):
+    fields, m1 = x_extended_1(Halves(fm_main_ref, fm_rim_ref), m1_ref, ups_ref, downs_ref, (0, 11, 12))
     send_planes([f[1] for f in fields] + [f[2] for f in fields] + [m1[1]], up_ref)
     send_planes([f[0] for f in fields], down_ref)
 
@@ -559,10 +578,10 @@
 
 
 def second_step_kernel(
-    at_ref, fm_ref, c0_ref, m1_ref, xu_ref, xd_ref, yu_ref, yd_ref, c1_ref, all_ref, rows_ref,
+    at_ref, fm_main_ref, fm_rim_ref, c0_ref, m1_ref, xu_ref, xd_ref, yu_ref, yd_ref, c1_ref, all_ref, rows_ref,
     out_ref, state_ref, square_ref, lanes_ref,
 ):
-    fields, m1 = x_extended_1(fm_ref, m1_ref, xu_ref, xd_ref, range(13))
+    fields, m1 = x_extended_1(Halves(fm_main_ref, fm_rim_ref), m1_ref, xu_ref, xd_ref, range(13))
     zero = jnp.zeros((1, 16, 256), F32)
     for n in range(4):
         low, add = get_plane(yu_ref, n, 9), get_plane(yu_ref, 4 + n, 9)
@@ -632,40 +651,41 @@
 
 def late_contact_kernel(
     at_ref, list_ref, task_ref, first_ref, all_ref, state_ref, field_ref, rows_ref, lanes_ref,
-    own_ref, up_ref, down_ref,
+    main_ref, rim_ref, up_ref, down_ref,
     turned_ref, force_ref, sum_ref, lhs_ref, square_ref, *rims,
 ):
     me = at_ref[2]
+    own = Halves(main_ref, rim_ref)
     zplanes = neighbour_planes(all_ref, PLANES_2, 5, me, square_ref, 13)
     mplanes = neighbour_planes(first_ref, PLANES, 4, me, square_ref, 12)
     top = (iota((13, 16, 128), 2) == 0) & (me == 7)
     zero = jnp.zeros((1, 16, 256), F32)
 
-    def with_rim(own, n):
-        return both(own[:, :, :128], jnp.where(top, own[:, :, 128:], unpack(zplanes, n, 5)))
+    def with_rim(x, n):
+        return both(x[:, :, :128], jnp.where(top, x[:, :, 128:], unpack(zplanes, n, 5)))
 
     inv = state_ref[9]
-    own_ref[9] = inv
+    own[9] = inv
     for c in range(3):
-        own_ref[c] = with_rim(state_ref[c], c)
-        own_ref[3 + c] = with_rim(state_ref[3 + c], 3 + c) + state_ref[6 + c]
-        own_ref[6 + c] = state_ref[6 + c]
+        own[c] = with_rim(state_ref[c], c)
+        own[3 + c] = with_rim(state_ref[3 + c], 3 + c) + state_ref[6 + c]
+        own[6 + c] = state_ref[6 + c]
     for n, step in ((10, 2), (11, 3)):
         m = both(fill16(field_ref[3 + step]), unpack(mplanes, 3 + step, 4))
-        own_ref[n] = jnp.concatenate([m, zero], axis=0)
+        own[n] = jnp.concatenate([m, zero], axis=0)
     for step, first_row, n in ((2, 0, 3), (3, LATE, 6)):
         force_ref[...] = jnp.zeros_like(force_ref)
         pair_loop(list_ref, step, first_row, me, all_ref, turned_ref, force_ref)
-        own = scatter_own(force_ref, sum_ref, rows_ref, lanes_ref, lhs_ref)
+        got = scatter_own(force_ref, sum_ref, rows_ref, lanes_ref, lhs_ref)
         rim = contact_rim(list_ref, task_ref, step, first_row, me, all_ref, first_ref, rims, square_ref)
         for c in range(3):
-            full = both(fill16(own[c]), unpack(rim, c))
-            own_ref[n + c, 0:12] = own_ref[n + c, 0:12] + own_ref[9, 0:12] * full
-    send_planes([row_plane(own_ref[n], 6 + p) for n, p in UP_LIST], up_ref)
-    send_planes([row_plane(own_ref[n], p) for n, p in DOWN_LIST], down_ref)
-
-
-def x_extended_2(own_ref, ups_ref, downs_ref, at_last, lines):
+            full = both(fill16(got[c]), unpack(rim, c))
+            own[n + c, 0:12] = own[n + c, 0:12] + own[9, 0:12] * full
+    send_planes([own.row(n, 6 + p) for n, p in UP_LIST], up_ref)
+    send_planes([own.row(n, p) for n, p in DOWN_LIST], down_ref)
+
+
+def x_extended_2(own, ups_ref, downs_ref, at_last, lines):
     row = iota((len(lines), 16, 256), 1)
     keep = (row < 8) | ((row == 8) & at_last)
 
@@ -674,7 +694,7 @@
 
     out = []
     for n in range(12):
-        x = jnp.stack([own_ref[n, j] for j in lines])
+        x = jnp.stack([own[n, j] for j in lines])
         x = shift_rows(jnp.where(keep, x, 0.0), 2)
         for ref, listed, first, count in ((ups_ref, UP_LIST, 0, 2), (downs_ref, DOWN_LIST, 10, 3)):
             for p in range(count):
@@ -689,14 +709,29 @@
     return out
 
 
-def y_send_2_kernel(at_ref, own_ref, ups_ref, downs_ref, up_ref, down_ref):
-    fields = x_extended_2(own_ref, ups_ref, downs_ref, at_ref[0] == 7, (0, 1, 2, 10, 11))
+def y_send_2_kernel(at_ref, main_ref, rim_ref, ups_ref, downs_ref, up_ref, down_ref):
+    fields = x_extended_2(Halves(main_ref, rim_ref), ups_ref, downs_ref, at_ref[0] == 7, (0, 1, 2, 10, 11))
     send_planes([fields[n][3 + p] for n, p in UP_LIST], up_ref)
     send_planes([fields[n][p] for n, p in DOWN_LIST], down_ref)
 
 
-def last_kernel(at_ref, own_ref, xu_ref, xd_ref, yu_ref, yd_ref, vel_ref, stress_ref):
-    fields = x_extended_2(own_ref, xu_ref, xd_ref, at_ref[0] == 7, range(13))
+def last_kernel(
+    at_ref, main_ref, rim_ref, xu_ref, xd_ref, yu_ref, yd_ref, vel_ref, stress_ref, wide_main_ref, wide_rim_ref
+):
+    own, grown = Halves(main_ref, rim_ref), Halves(wide_main_ref, wide_rim_ref)
+    at_last = at_ref[0] == 7
+    row = iota((13, 16, 256), 1)
+    for n in range(12):
+        grown[n] = shift_rows(jnp.where((row < 8) | ((row == 8) & at_last), own[n], 0.0), 2)
+        for ref, listed, first, count in ((xu_ref, UP_LIST, 0, 2), (xd_ref, DOWN_LIST, 10, 3)):
+            for p in range(count):
+                got = plane_of(ref, listed, n, p)
+                if got is None:
+                    continue
+                if first + p == 10:
+                    got = jnp.where(at_last, own.row(n, 8), got)
+                grown.set_row(n, first + p, got)
+    fields = [grown[n] for n in range(12)]
     y_last = at_ref[1] == 3
     none = jnp.zeros((16, 256), F32)
     wide = []
@@ -792,20 +827,20 @@
         (),
         (1, 2, 3),
     )(at, everyone)
-    fm, c0, m1, up, down = call(
+    fm, fm_rim, c0, m1, up, down = call(
         first_contact_kernel,
-        [((4, 13, 16, 256), F32), ((3, 13, 16, 256), F32), ((13, 16, 256), F32), ((10, 16, 128), F32),
+        [((5, 13, 16, 128), F32)] * 2 + [((3, 13, 16, 256), F32), ((13, 16, 256), F32), ((10, 16, 128), F32),
          ((5, 16, 128), F32)],
         [SMEM, SMEM] + [HELD] * 5,
         [TURNED, TURNED, SUMS, LHS, SQUARE] + RIM,
-        (0, 1, 2),
+        (0, 1, 2, 3),
     )(at, lists, tasks, everyone, fields, *hot)
     xu, xd = neighbours(up, down, "gx")
     late_lists, late_tasks = call(
         functools.partial(plan_kernel, steps=(2, 3)), plan_out, [SMEM, HELD, HELD], (), (1,)
     )(at, everyone, m1)
-    up, down = call(y_send_1_kernel, [((10, 16, 128), F32), ((5, 16, 128), F32)], [HELD] * 5)(
-        fm, m1, xu, xd, late_tasks
+    up, down = call(y_send_1_kernel, [((10, 16, 128), F32), ((5, 16, 128), F32)], [HELD] * 6)(
+        fm, fm_rim, m1, xu, xd, late_tasks
     )
     yu, yd = neighbours(up, down, "gy")
     (c1,) = call(
@@ -818,30 +853,31 @@
     payload, state = call(
         second_step_kernel,
         [((8, ROWS_2, 128), F32), ((10, 13, 16, 256), F32)],
-        [SMEM] + [HELD] * 10,
+        [SMEM] + [HELD] * 11,
         [SQUARE, pltpu.VMEM((128, 2048), F32)],
         (1,),
-    )(at, fm, c0, m1, xu, xd, yu, yd, c1, everyone, hot[0])
+    )(at, fm, fm_rim, c0, m1, xu, xd, yu, yd, c1, everyone, hot[0])
     late = share(payload)
-    own, up, down = call(
+    own, own_rim, up, down = call(
         late_contact_kernel,
-        [((12, 13, 16, 256), F32), ((UPS + 1, 16, 128), F32), ((DOWNS + 2, 16, 128), F32)],
+        [((13, 13, 16, 128), F32)] * 2 + [((UPS + 1, 16, 128), F32), ((DOWNS + 2, 16, 128), F32)],
         [SMEM, SMEM] + [HELD] * 7,
         [TURNED, TURNED, SUMS, LHS, SQUARE] + RIM,
-        (0,),
+        (0, 1),
     )(at, late_lists, late_tasks, everyone, late, state, fields, *hot)
     xu, xd = neighbours(up, down, "gx")
     up, down = call(
         y_send_2_kernel,
         [((UPS + 1, 16, 128), F32), ((DOWNS + 2, 16, 128), F32)],
-        [SMEM] + [HELD] * 3,
-    )(at, own, xu, xd)
+        [SMEM] + [HELD] * 4,
+    )(at, own, own_rim, xu, xd)
     yu, yd = neighbours(up, down, "gy")
     vel, stress = call(
         last_kernel,
         [((3, 12, 8, 128), F32), ((6, 12, 8, 128), F32)],
-        [SMEM] + [HELD] * 5,
-    )(at, own, xu, xd, yu, yd)
+        [SMEM] + [HELD] * 6,
+        [pltpu.VMEM((13, 13, 16, 128), F32)] * 2,
+    )(at, own, own_rim, xu, xd, yu, yd)
     return jnp.swapaxes(vel, 1, 2), jnp.swapaxes(stress, 1, 2)
 
 

time: 123 us -> 122 us (level)
  Pallas kernels: 42.5 us -> 41.2 us
    pallas_call x10, Pallas kernels: 42.5 us -> 41.2 us  [run(): pl.pallas_call(kernel, out_shape=[pltpu.VMEM(s, d) if n in held else jax....]
  transfers between devices with their start and end apart: 8 -> 8, of which waited for: 3 -> 3; matrix products, arithmetic and copies ran while one was open for 0% -> 0% of each run, Pallas kernels for 7% -> 6%
where the time goes in v6:
time: 122 us; the launch traced here: 121 us
  blocking collectives  49.9 us (41%)
  Pallas kernels  41.2 us (34%)
  starting transfers between devices  21.8 us (18%)
  waiting for transfers between devices  7.01 us (6%)
    all_to_all x2, blocking collectives, share(): return lax.all_to_all(blocks, 'gz', split_axis=0, concat_axis=0, tiled=True)  49.9 us
    pallas_call x10, Pallas kernels, run(): pl.pallas_call(kernel, out_shape=[pltpu.VMEM(s, d) if n in held else jax....  41.2 us
    ppermute x4, starting transfers between devices, neighbours(): lax.ppermute(down, axis, [(j, i) for i, j in ahead])  12.1 us
    ppermute x4, starting transfers between devices, neighbours(): lax.ppermute(up, axis, ahead)  9.69 us
    ppermute x4, waiting for transfers between devices, neighbours(): lax.ppermute(up, axis, ahead)  6.94 us
  transfers between devices with their start and end apart: 8, of which 3 were waited for; matrix products, arithmetic and copies ran while one was open for 0% of the time, Pallas kernels for 6%

profile of v6, /device:TPU:80, one launch (start us, length us, event | category | flops | bytes accessed | tf_op | source)
XLA Modules:
  0.0 120.7 jit_solution(10365942667704355359)
XLA Ops:
  0.6 0.1 pad_add_fusion.at_ref
  0.7 2.0 %shard_map.95 = (f32[8,104,128]{2,1,0:T(8,128)S(1)}, f32[7,12,8,128]{3,2,1,0:T(8,128)S(1)}) custom-call(s32[3]{0:T(128)S(1)} %pad_add_fusion.at_ref, f32[3,16,128]{2,1,0:T(8,128)} %bitcast.17, s32[4,16]{1,0:T(4,128)} %refs_1_.1, s32[4,2,64]{2,1,0:T(2,128)} %bitcast.18, s32[16,128]{1,0:T(8,128)} %refs_3_.1, f32[12,8,128]{2,1,0:T(8,128)} %bitcast.15, ...), custom_call_target="tpu_custom_call" | custom-call | tf_op jit(solution)/shard_map/pallas_call | solution.py:770
  2.8 26.5 %all_to_all.10.all_ref.first_ref = f32[8,104,128]{2,1,0:T(8,128)S(1)} all-to-all(f32[8,104,128]{2,1,0:T(8,128)S(1)} %get-tuple-element.28), channel_id=1, replica_groups=mesh['gx'=8,'gy'=4,'gz'=8] {'gz'}, dimensions={0} | all-to-all | bytes 851968 | tf_op jit(solution)/shard_map/all_to_all | solution.py:786
  29.3 1.9 %shard_map.96 = (s32[12,512]{1,0:T(8,128)S(1)}, f32[4,4,8,128]{3,2,1,0:T(8,128)S(1)}, bf16[96,2048]{1,0:T(8,128)(2,1)S(1)}, bf16[2048,128]{1,0:T(8,128)(2,1)S(1)}) custom-call(s32[3]{0:T(128)S(1)} %pad_add_fusion.at_ref, f32[8,104,128]{2,1,0:T(8,128)S(1)} %all_to_all.10.all_ref.first_ref), custom_call_target="tpu_custom_call" | custom-call | tf_op jit(solution)/shard_map/pallas_call | solution.py:770
  31.2 7.3 %shard_map.97 = (f32[5,13,16,128]{3,2,1,0:T(8,128)S(1)}, f32[5,13,16,128]{3,2,1,0:T(8,128)S(1)}, f32[3,13,16,256]{3,2,1,0:T(8,128)S(1)}, f32[13,16,256]{2,1,0:T(...) custom-call(s32[3]{0:T(128)S(1)} %pad_add_fusion.at_ref, s32[12,512]{1,0:T(8,128)S(1)} %get-tuple-element.29.list_ref, ...), custom_call_target="tpu_custom_call" | custom-call | tf_op jit(solution)/shard_map/pallas_call | solution.py:770
  38.5 1.9 %collective-permute-start = (f32[10,16,128]{2,1,0:T(8,128)S(1)}, f32[10,16,128]{2,1,0:T(8,128)S(1)}, u32[]{:S(2)}, u32[]{:S(2)}) collective-permute-start(f32[10,16,128]{2,1,0:T(8,128)S(1)} %get-tuple-element.40), channel_id=1, source_target_pairs={{0,32},{32,64},{64,96},{96,128},{128,160},{160,192},{192,224},{1,3... | collective-permute-start | bytes 245768 | tf_op jit(solution)/shard_map/ppermute | solution.py:792
  40.4 3.6 %collective-permute-start.1 = (f32[5,16,128]{2,1,0:T(8,128)S(1)}, f32[5,16,128]{2,1,0:T(8,128)S(1)}, u32[]{:S(2)}, u32[]{:S(2)}) collective-permute-start(f32[5,16,128]{2,1,0:T(8,128)S(1)} %get-tuple-element.41), channel_id=1, source_target_pairs={{32,0},{64,32},{96,64},{128,96},{160,128},{192,160},{224,192},{33,... | collective-permute-start | bytes 122888 | tf_op jit(solution)/shard_map/ppermute | solution.py:792
  44.1 1.6 %shard_map.98 = (s32[12,512]{1,0:T(8,128)S(1)}, f32[4,4,8,128]{3,2,1,0:T(8,128)S(1)}) custom-call(s32[3]{0:T(128)S(1)} %pad_add_fusion.at_ref, f32[8,104,128]{2,1,0:T(8,128)S(1)} %all_to_all.10.all_ref.first_ref, f32[13,16,256]{2,1,0:T(8,128)S(1)} %get-tuple-element.34.refs_0_.m1_ref), custom_call_target="tpu_custom_call" | custom-call | tf_op jit(solution)/shard_map/pallas_call | solution.py:770
  45.6 0.1 collective-permute-done.1.downs_ref.xd_ref
  45.7 0.0 collective-permute-done.ups_ref.xu_ref
  45.7 0.2 shard_map.99
  45.9 1.9 %collective-permute-start.2 = (f32[10,16,128]{2,1,0:T(8,128)S(1)}, f32[10,16,128]{2,1,0:T(8,128)S(1)}, u32[]{:S(2)}, u32[]{:S(2)}) collective-permute-start(f32[10,16,128]{2,1,0:T(8,128)S(1)} %get-tuple-element.42), channel_id=1, source_target_pairs={{0,8},{8,16},{16,24},{1,9},{9,17},{17,25},{2,10},{10,18},{18,26},{... | collective-permute-start | bytes 245768 | tf_op jit(solution)/shard_map/ppermute | solution.py:792
  47.8 3.9 %collective-permute-start.3 = (f32[5,16,128]{2,1,0:T(8,128)S(1)}, f32[5,16,128]{2,1,0:T(8,128)S(1)}, u32[]{:S(2)}, u32[]{:S(2)}) collective-permute-start(f32[5,16,128]{2,1,0:T(8,128)S(1)} %get-tuple-element.43), channel_id=1, source_target_pairs={{8,0},{16,8},{24,16},{9,1},{17,9},{25,17},{10,2},{18,10},{26,18},{... | collective-permute-start | bytes 122888 | tf_op jit(solution)/shard_map/ppermute | solution.py:792
  51.8 5.2 %shard_map.100.c1_ref = f32[3,12,8,128]{3,2,1,0:T(8,128)S(1)} custom-call(s32[3]{0:T(128)S(1)} %pad_add_fusion.at_ref, s32[12,512]{1,0:T(8,128)S(1)} %get-tuple-element.29.list_ref, f32[8,104,128]{2,1,0:T(8,128)S(1)} %all_to_all.10.all_ref.first_ref, bf16[96,2048]{1,0:T(8,128)(2,1)S(1)} %get-tuple-element.32.rows_ref, ...), custom_call_target="tpu_custom_call" | custom-call | tf_op jit(solution)/shard_map/pallas_call | solution.py:770
  56.9 0.0 collective-permute-done.3.yd_ref
  56.9 0.0 collective-permute-done.2.yu_ref
  56.9 3.8 %shard_map.101 = (f32[8,128,128]{2,1,0:T(8,128)S(1)}, f32[10,13,16,256]{3,2,1,0:T(8,128)S(1)}) custom-call(s32[3]{0:T(128)S(1)} %pad_add_fusion.at_ref, f32[5,13,16,128]{3,2,1,0:T(8,128)S(1)} %get-tuple-element.37.fm_main_ref, f32[5,13,16,128]{3,2,1,0:T(8,128)S(1)} %get-tuple-element.38.fm_rim_ref, f32[3,13,16,256]{3,2,1,0:T(8,128)S(1)} %get-tuple-element.39.c0_ref, ...), custom_call_target="tpu_custom_call" | custom-call | tf_op jit(solution)/shard_map/pallas_call | solution.py:770
  60.7 23.4 %all_to_all.11.all_ref = f32[8,128,128]{2,1,0:T(8,128)S(1)} all-to-all(f32[8,128,128]{2,1,0:T(8,128)S(1)} %get-tuple-element.44), channel_id=1, replica_groups=mesh['gx'=8,'gy'=4,'gz'=8] {'gz'}, dimensions={0} | all-to-all | bytes 1048576 | tf_op jit(solution)/shard_map/all_to_all | solution.py:786
  84.1 13.2 %shard_map.102 = (f32[13,13,16,128]{3,2,1,0:T(8,128)S(1)}, f32[13,13,16,128]{3,2,1,0:T(8,128)S(1)}, f32[14,16,128]{2,1,0:T(8,128)S(1)}, f32[25,16,128]{2,1,0:T(8,128)S(1)}) custom-call(s32[3]{0:T(128)S(1)} %pad_add_fusion.at_ref, s32[12,512]{1,0:T(8,128)S(1)} %get-tuple-element.35.list_ref, f32[4,4,8,128]{3,2,1,0:T(8,128)S(1)} %get-tuple-element.36.task_ref, ...), custom_call_target="tpu_custom_call" | custom-call | tf_op jit(solution)/shard_map/pallas_call | solution.py:770
  97.3 2.6 %collective-permute-start.5 = (f32[25,16,128]{2,1,0:T(8,128)S(1)}, f32[25,16,128]{2,1,0:T(8,128)S(1)}, u32[]{:S(2)}, u32[]{:S(2)}) collective-permute-start(f32[25,16,128]{2,1,0:T(8,128)S(1)} %get-tuple-element.49), channel_id=1, source_target_pairs={{32,0},{64,32},{96,64},{128,96},{160,128},{192,160},{224,192},{33,... | collective-permute-start | bytes 614408 | tf_op jit(solution)/shard_map/ppermute | solution.py:792
  99.9 1.9 %collective-permute-start.4 = (f32[14,16,128]{2,1,0:T(8,128)S(1)}, f32[14,16,128]{2,1,0:T(8,128)S(1)}, u32[]{:S(2)}, u32[]{:S(2)}) collective-permute-start(f32[14,16,128]{2,1,0:T(8,128)S(1)} %get-tuple-element.48), channel_id=1, source_target_pairs={{0,32},{32,64},{64,96},{96,128},{128,160},{160,192},{192,224},{1,3... | collective-permute-start | bytes 344072 | tf_op jit(solution)/shard_map/ppermute | solution.py:792
  101.8 4.2 %collective-permute-done.4.ups_ref.xu_ref = f32[14,16,128]{2,1,0:T(8,128)S(1)} collective-permute-done((f32[14,16,128]{2,1,0:T(8,128)S(1)}, f32[14,16,128]{2,1,0:T(8,128)S(1)}, u32[]{:S(2)}, u32[]{:S(2)}) %collective-permute-start.4) | collective-permute-done | bytes 114720 | tf_op jit(solution)/shard_map/ppermute | solution.py:792
  106.0 0.0 collective-permute-done.5.downs_ref.xd_ref
  106.0 0.8 shard_map.103
  106.8 1.9 %collective-permute-start.7 = (f32[25,16,128]{2,1,0:T(8,128)S(1)}, f32[25,16,128]{2,1,0:T(8,128)S(1)}, u32[]{:S(2)}, u32[]{:S(2)}) collective-permute-start(f32[25,16,128]{2,1,0:T(8,128)S(1)} %get-tuple-element.51), channel_id=1, source_target_pairs={{8,0},{16,8},{24,16},{9,1},{17,9},{25,17},{10,2},{18,10},{26,18},{... | collective-permute-start | bytes 614408 | tf_op jit(solution)/shard_map/ppermute | solution.py:792
  108.7 3.9 %collective-permute-start.6 = (f32[14,16,128]{2,1,0:T(8,128)S(1)}, f32[14,16,128]{2,1,0:T(8,128)S(1)}, u32[]{:S(2)}, u32[]{:S(2)}) collective-permute-start(f32[14,16,128]{2,1,0:T(8,128)S(1)} %get-tuple-element.50), channel_id=1, source_target_pairs={{0,8},{8,16},{16,24},{1,9},{9,17},{17,25},{2,10},{10,18},{18,26},{... | collective-permute-start | bytes 344072 | tf_op jit(solution)/shard_map/ppermute | solution.py:792
  112.7 2.7 %collective-permute-done.6.yu_ref = f32[14,16,128]{2,1,0:T(8,128)S(1)} collective-permute-done((f32[14,16,128]{2,1,0:T(8,128)S(1)}, f32[14,16,128]{2,1,0:T(8,128)S(1)}, u32[]{:S(2)}, u32[]{:S(2)}) %collective-permute-start.6) | collective-permute-done | bytes 114720 | tf_op jit(solution)/shard_map/ppermute | solution.py:792
  115.4 0.0 collective-permute-done.7.yd_ref
  115.4 5.3 %shard_map.104 = (f32[3,12,8,128]{3,2,1,0:T(8,128)}, f32[6,12,8,128]{3,2,1,0:T(8,128)}) custom-call(s32[3]{0:T(128)S(1)} %pad_add_fusion.at_ref, f32[13,13,16,128]{3,2,1,0:T(8,128)S(1)} %get-tuple-element.46.main_ref, f32[13,13,16,128]{3,2,1,0:T(8,128)S(1)} %get-tuple-element.47.rim_ref, f32[14,16,128]{2,1,0:T(8,128)S(1)} %collective-permute-done.4.ups_ref.xu_ref, ...), custom_call_target="tpu_custom_call" | custom-call | tf_op jit(solution)/shard_map/pallas_call | solution.py:770
Async XLA Ops:
  38.5 7.2 %collective-permute-start = (f32[10,16,128]{2,1,0:T(8,128)S(1)}, f32[10,16,128]{2,1,0:T(8,128)S(1)}, u32[]{:S(2)}, u32[]{:S(2)}) collective-permute-start(f32[10,16,128]{2,1,0:T(8,128)S(1)} %get-tuple-element.40), channel_id=1, source_target_pairs={{0,32},{32,64},{64,96},{96,128},{128,160},{160,192},{192,224},{1,3... | collective-permute-start | bytes 245768 | tf_op jit(solution)/shard_map/ppermute | solution.py:792
  40.4 5.3 %collective-permute-start.1 = (f32[5,16,128]{2,1,0:T(8,128)S(1)}, f32[5,16,128]{2,1,0:T(8,128)S(1)}, u32[]{:S(2)}, u32[]{:S(2)}) collective-permute-start(f32[5,16,128]{2,1,0:T(8,128)S(1)} %get-tuple-element.41), channel_id=1, source_target_pairs={{32,0},{64,32},{96,64},{128,96},{160,128},{192,160},{224,192},{33,... | collective-permute-start | bytes 122888 | tf_op jit(solution)/shard_map/ppermute | solution.py:792
  45.9 11.0 %collective-permute-start.2 = (f32[10,16,128]{2,1,0:T(8,128)S(1)}, f32[10,16,128]{2,1,0:T(8,128)S(1)}, u32[]{:S(2)}, u32[]{:S(2)}) collective-permute-start(f32[10,16,128]{2,1,0:T(8,128)S(1)} %get-tuple-element.42), channel_id=1, source_target_pairs={{0,8},{8,16},{16,24},{1,9},{9,17},{17,25},{2,10},{10,18},{18,26},{... | collective-permute-start | bytes 245768 | tf_op jit(solution)/shard_map/ppermute | solution.py:792
  47.8 9.1 %collective-permute-start.3 = (f32[5,16,128]{2,1,0:T(8,128)S(1)}, f32[5,16,128]{2,1,0:T(8,128)S(1)}, u32[]{:S(2)}, u32[]{:S(2)}) collective-permute-start(f32[5,16,128]{2,1,0:T(8,128)S(1)} %get-tuple-element.43), channel_id=1, source_target_pairs={{8,0},{16,8},{24,16},{9,1},{17,9},{25,17},{10,2},{18,10},{26,18},{... | collective-permute-start | bytes 122888 | tf_op jit(solution)/shard_map/ppermute | solution.py:792
  97.3 8.7 %collective-permute-start.5 = (f32[25,16,128]{2,1,0:T(8,128)S(1)}, f32[25,16,128]{2,1,0:T(8,128)S(1)}, u32[]{:S(2)}, u32[]{:S(2)}) collective-permute-start(f32[25,16,128]{2,1,0:T(8,128)S(1)} %get-tuple-element.49), channel_id=1, source_target_pairs={{32,0},{64,32},{96,64},{128,96},{160,128},{192,160},{224,192},{33,... | collective-permute-start | bytes 614408 | tf_op jit(solution)/shard_map/ppermute | solution.py:792
  99.9 6.1 %collective-permute-start.4 = (f32[14,16,128]{2,1,0:T(8,128)S(1)}, f32[14,16,128]{2,1,0:T(8,128)S(1)}, u32[]{:S(2)}, u32[]{:S(2)}) collective-permute-start(f32[14,16,128]{2,1,0:T(8,128)S(1)} %get-tuple-element.48), channel_id=1, source_target_pairs={{0,32},{32,64},{64,96},{96,128},{128,160},{160,192},{192,224},{1,3... | collective-permute-start | bytes 344072 | tf_op jit(solution)/shard_map/ppermute | solution.py:792
  106.8 8.6 %collective-permute-start.7 = (f32[25,16,128]{2,1,0:T(8,128)S(1)}, f32[25,16,128]{2,1,0:T(8,128)S(1)}, u32[]{:S(2)}, u32[]{:S(2)}) collective-permute-start(f32[25,16,128]{2,1,0:T(8,128)S(1)} %get-tuple-element.51), channel_id=1, source_target_pairs={{8,0},{16,8},{24,16},{9,1},{17,9},{25,17},{10,2},{18,10},{26,18},{... | collective-permute-start | bytes 614408 | tf_op jit(solution)/shard_map/ppermute | solution.py:792
  108.7 6.7 %collective-permute-start.6 = (f32[14,16,128]{2,1,0:T(8,128)S(1)}, f32[14,16,128]{2,1,0:T(8,128)S(1)}, u32[]{:S(2)}, u32[]{:S(2)}) collective-permute-start(f32[14,16,128]{2,1,0:T(8,128)S(1)} %get-tuple-element.50), channel_id=1, source_target_pairs={{0,8},{8,16},{16,24},{1,9},{9,17},{17,25},{2,10},{10,18},{18,26},{... | collective-permute-start | bytes 344072 | tf_op jit(solution)/shard_map/ppermute | solution.py:792

commit v7 on v6

--- a/solution.py
+++ b/solution.py
@@ -327,11 +327,11 @@
     return (out[:288] + out[288:]).reshape(3, 12, 8, 128)
 
 
-def split3(x):
+def split3(x, axis=0):
     hi, rest = x.astype(BF16), x
     rest = rest - hi.astype(F32)
     mid = rest.astype(BF16)
-    return jnp.concatenate([hi, mid, (rest - mid.astype(F32)).astype(BF16)], axis=0)
+    return jnp.concatenate([hi, mid, (rest - mid.astype(F32)).astype(BF16)], axis=axis)
 
 
 def contact_rim(list_ref, task_ref, step, first_row, me, pos_ref, ids_ref, rim, square_ref):
@@ -340,7 +340,7 @@
     for c in range(3):
         at = first_row + 16 * c
         block = jnp.concatenate([pos_ref[src, at : at + 16, :] for src in range(8)], axis=0)
-        all_ref[c] = split3(block * SCALE)
+        all_ref[c] = split3(jnp.transpose(block * SCALE), 1)
         block = jnp.concatenate([pos_ref[low, at : at + 16, :], pos_ref[up, at : at + 16, :]], axis=0)
         near_ref[c] = split3(block * SCALE)
     ids = jnp.concatenate(
@@ -386,7 +386,7 @@
         xi, xj = [], []
         for c in range(3):
             xi.append(jnp.sum(jnp.where(match, pick(near_ref[c], hot_p3), 0.0), axis=0, keepdims=True))
-            xj.append(pick(all_ref[c], hot_r3))
+            xj.append(jnp.dot(all_ref[c], hot_r3, preferred_element_type=F32))
         diff = [xi[c] - xj[c] for c in range(3)]
         dist = diff[0] * diff[0] + diff[1] * diff[1] + diff[2] * diff[2]
         w = jnp.exp2(-dist)
@@ -795,7 +795,7 @@
 TURNED = pltpu.VMEM((17, 4, 3, 8, 128), F32)
 SUMS = pltpu.VMEM((3, 16, 128), F32)
 RIM = [
-    pltpu.VMEM((3, 384, 128), BF16),
+    pltpu.VMEM((3, 128, 384), BF16),
     pltpu.VMEM((3, 96, 128), BF16),
     pltpu.VMEM((3, 32, 128), BF16),
     pltpu.VMEM((16, 128), F32),

time: 122 us -> 123 us (level)
  waiting for transfers between devices: 7.01 us -> 9.02 us
    ppermute x4, starting transfers between devices: 12.1 us -> 15.2 us  [neighbours(): lax.ppermute(down, axis, [(j, i) for i, j in ahead])]
    ppermute x4, starting transfers between devices: 9.69 us -> 7.68 us  [neighbours(): lax.ppermute(up, axis, ahead)]
    ppermute x4, waiting for transfers between devices: 6.94 us -> 8.95 us  [neighbours(): lax.ppermute(up, axis, ahead)]
where the time goes in v7:
time: 123 us
  blocking collectives  49.4 us (40%)
  Pallas kernels  40.4 us (33%)
  starting transfers between devices  22.9 us (19%)
  waiting for transfers between devices  9.02 us (7%)
    all_to_all x2, blocking collectives, share(): return lax.all_to_all(blocks, 'gz', split_axis=0, concat_axis=0, tiled=True)  49.4 us
    pallas_call x10, Pallas kernels, run(): pl.pallas_call(kernel, out_shape=[pltpu.VMEM(s, d) if n in held else jax....  40.4 us
    ppermute x4, starting transfers between devices, neighbours(): lax.ppermute(down, axis, [(j, i) for i, j in ahead])  15.2 us
    ppermute x4, waiting for transfers between devices, neighbours(): lax.ppermute(up, axis, ahead)  8.95 us
    ppermute x4, starting transfers between devices, neighbours(): lax.ppermute(up, axis, ahead)  7.68 us
  transfers between devices with their start and end apart: 8, of which 3 were waited for; matrix products, arithmetic and copies ran while one was open for 0% of the time, Pallas kernels for 6%

profile of v7, /device:TPU:80, one launch (start us, length us, event | category | flops | bytes accessed | tf_op | source)
XLA Modules:
  0.0 122.6 jit_solution(5905603917232360748)
XLA Ops:
  0.6 0.1 pad_add_fusion.at_ref
  0.7 2.0 %shard_map.95 = (f32[8,104,128]{2,1,0:T(8,128)S(1)}, f32[7,12,8,128]{3,2,1,0:T(8,128)S(1)}) custom-call(s32[3]{0:T(128)S(1)} %pad_add_fusion.at_ref, f32[3,16,128]{2,1,0:T(8,128)} %bitcast.17, s32[4,16]{1,0:T(4,128)} %refs_1_.1, s32[4,2,64]{2,1,0:T(2,128)} %bitcast.18, s32[16,128]{1,0:T(8,128)} %refs_3_.1, f32[12,8,128]{2,1,0:T(8,128)} %bitcast.15, ...), custom_call_target="tpu_custom_call" | custom-call | tf_op jit(solution)/shard_map/pallas_call | solution.py:770
  2.8 26.5 %all_to_all.10.all_ref.first_ref = f32[8,104,128]{2,1,0:T(8,128)S(1)} all-to-all(f32[8,104,128]{2,1,0:T(8,128)S(1)} %get-tuple-element.28), channel_id=1, replica_groups=mesh['gx'=8,'gy'=4,'gz'=8] {'gz'}, dimensions={0} | all-to-all | bytes 851968 | tf_op jit(solution)/shard_map/all_to_all | solution.py:786
  29.3 1.9 %shard_map.96 = (s32[12,512]{1,0:T(8,128)S(1)}, f32[4,4,8,128]{3,2,1,0:T(8,128)S(1)}, bf16[96,2048]{1,0:T(8,128)(2,1)S(1)}, bf16[2048,128]{1,0:T(8,128)(2,1)S(1)}) custom-call(s32[3]{0:T(128)S(1)} %pad_add_fusion.at_ref, f32[8,104,128]{2,1,0:T(8,128)S(1)} %all_to_all.10.all_ref.first_ref), custom_call_target="tpu_custom_call" | custom-call | tf_op jit(solution)/shard_map/pallas_call | solution.py:770
  31.2 7.3 %shard_map.97 = (f32[5,13,16,128]{3,2,1,0:T(8,128)S(1)}, f32[5,13,16,128]{3,2,1,0:T(8,128)S(1)}, f32[3,13,16,256]{3,2,1,0:T(8,128)S(1)}, f32[13,16,256]{2,1,0:T(...) custom-call(s32[3]{0:T(128)S(1)} %pad_add_fusion.at_ref, s32[12,512]{1,0:T(8,128)S(1)} %get-tuple-element.29.list_ref, ...), custom_call_target="tpu_custom_call" | custom-call | tf_op jit(solution)/shard_map/pallas_call | solution.py:770
  38.5 1.9 %collective-permute-start = (f32[10,16,128]{2,1,0:T(8,128)S(1)}, f32[10,16,128]{2,1,0:T(8,128)S(1)}, u32[]{:S(2)}, u32[]{:S(2)}) collective-permute-start(f32[10,16,128]{2,1,0:T(8,128)S(1)} %get-tuple-element.40), channel_id=1, source_target_pairs={{0,32},{32,64},{64,96},{96,128},{128,160},{160,192},{192,224},{1,3... | collective-permute-start | bytes 245768 | tf_op jit(solution)/shard_map/ppermute | solution.py:792
  40.4 3.6 %collective-permute-start.1 = (f32[5,16,128]{2,1,0:T(8,128)S(1)}, f32[5,16,128]{2,1,0:T(8,128)S(1)}, u32[]{:S(2)}, u32[]{:S(2)}) collective-permute-start(f32[5,16,128]{2,1,0:T(8,128)S(1)} %get-tuple-element.41), channel_id=1, source_target_pairs={{32,0},{64,32},{96,64},{128,96},{160,128},{192,160},{224,192},{33,... | collective-permute-start | bytes 122888 | tf_op jit(solution)/shard_map/ppermute | solution.py:792
  44.1 1.6 %shard_map.98 = (s32[12,512]{1,0:T(8,128)S(1)}, f32[4,4,8,128]{3,2,1,0:T(8,128)S(1)}) custom-call(s32[3]{0:T(128)S(1)} %pad_add_fusion.at_ref, f32[8,104,128]{2,1,0:T(8,128)S(1)} %all_to_all.10.all_ref.first_ref, f32[13,16,256]{2,1,0:T(8,128)S(1)} %get-tuple-element.34.refs_0_.m1_ref), custom_call_target="tpu_custom_call" | custom-call | tf_op jit(solution)/shard_map/pallas_call | solution.py:770
  45.6 0.1 collective-permute-done.1.downs_ref.xd_ref
  45.7 0.0 collective-permute-done.ups_ref.xu_ref
  45.7 0.2 shard_map.99
  45.9 1.9 %collective-permute-start.2 = (f32[10,16,128]{2,1,0:T(8,128)S(1)}, f32[10,16,128]{2,1,0:T(8,128)S(1)}, u32[]{:S(2)}, u32[]{:S(2)}) collective-permute-start(f32[10,16,128]{2,1,0:T(8,128)S(1)} %get-tuple-element.42), channel_id=1, source_target_pairs={{0,8},{8,16},{16,24},{1,9},{9,17},{17,25},{2,10},{10,18},{18,26},{... | collective-permute-start | bytes 245768 | tf_op jit(solution)/shard_map/ppermute | solution.py:792
  47.8 3.9 %collective-permute-start.3 = (f32[5,16,128]{2,1,0:T(8,128)S(1)}, f32[5,16,128]{2,1,0:T(8,128)S(1)}, u32[]{:S(2)}, u32[]{:S(2)}) collective-permute-start(f32[5,16,128]{2,1,0:T(8,128)S(1)} %get-tuple-element.43), channel_id=1, source_target_pairs={{8,0},{16,8},{24,16},{9,1},{17,9},{25,17},{10,2},{18,10},{26,18},{... | collective-permute-start | bytes 122888 | tf_op jit(solution)/shard_map/ppermute | solution.py:792
  51.8 5.8 %shard_map.100.c1_ref = f32[3,12,8,128]{3,2,1,0:T(8,128)S(1)} custom-call(s32[3]{0:T(128)S(1)} %pad_add_fusion.at_ref, s32[12,512]{1,0:T(8,128)S(1)} %get-tuple-element.29.list_ref, f32[8,104,128]{2,1,0:T(8,128)S(1)} %all_to_all.10.all_ref.first_ref, bf16[96,2048]{1,0:T(8,128)(2,1)S(1)} %get-tuple-element.32.rows_ref, ...), custom_call_target="tpu_custom_call" | custom-call | tf_op jit(solution)/shard_map/pallas_call | solution.py:770
  57.6 0.0 collective-permute-done.3.yd_ref
  57.6 0.0 collective-permute-done.2.yu_ref
  57.6 3.8 %shard_map.101 = (f32[8,128,128]{2,1,0:T(8,128)S(1)}, f32[10,13,16,256]{3,2,1,0:T(8,128)S(1)}) custom-call(s32[3]{0:T(128)S(1)} %pad_add_fusion.at_ref, f32[5,13,16,128]{3,2,1,0:T(8,128)S(1)} %get-tuple-element.37.fm_main_ref, f32[5,13,16,128]{3,2,1,0:T(8,128)S(1)} %get-tuple-element.38.fm_rim_ref, f32[3,13,16,256]{3,2,1,0:T(8,128)S(1)} %get-tuple-element.39.c0_ref, ...), custom_call_target="tpu_custom_call" | custom-call | tf_op jit(solution)/shard_map/pallas_call | solution.py:770
  61.4 22.9 %all_to_all.11.all_ref = f32[8,128,128]{2,1,0:T(8,128)S(1)} all-to-all(f32[8,128,128]{2,1,0:T(8,128)S(1)} %get-tuple-element.44), channel_id=1, replica_groups=mesh['gx'=8,'gy'=4,'gz'=8] {'gz'}, dimensions={0} | all-to-all | bytes 1048576 | tf_op jit(solution)/shard_map/all_to_all | solution.py:786
  84.3 11.8 %shard_map.102 = (f32[13,13,16,128]{3,2,1,0:T(8,128)S(1)}, f32[13,13,16,128]{3,2,1,0:T(8,128)S(1)}, f32[14,16,128]{2,1,0:T(8,128)S(1)}, f32[25,16,128]{2,1,0:T(8,128)S(1)}) custom-call(s32[3]{0:T(128)S(1)} %pad_add_fusion.at_ref, s32[12,512]{1,0:T(8,128)S(1)} %get-tuple-element.35.list_ref, f32[4,4,8,128]{3,2,1,0:T(8,128)S(1)} %get-tuple-element.36.task_ref, ...), custom_call_target="tpu_custom_call" | custom-call | tf_op jit(solution)/shard_map/pallas_call | solution.py:770
  96.0 3.1 %collective-permute-start.5 = (f32[25,16,128]{2,1,0:T(8,128)S(1)}, f32[25,16,128]{2,1,0:T(8,128)S(1)}, u32[]{:S(2)}, u32[]{:S(2)}) collective-permute-start(f32[25,16,128]{2,1,0:T(8,128)S(1)} %get-tuple-element.49), channel_id=1, source_target_pairs={{32,0},{64,32},{96,64},{128,96},{160,128},{192,160},{224,192},{33,... | collective-permute-start | bytes 614408 | tf_op jit(solution)/shard_map/ppermute | solution.py:792
  99.1 1.9 %collective-permute-start.4 = (f32[14,16,128]{2,1,0:T(8,128)S(1)}, f32[14,16,128]{2,1,0:T(8,128)S(1)}, u32[]{:S(2)}, u32[]{:S(2)}) collective-permute-start(f32[14,16,128]{2,1,0:T(8,128)S(1)} %get-tuple-element.48), channel_id=1, source_target_pairs={{0,32},{32,64},{64,96},{96,128},{128,160},{160,192},{192,224},{1,3... | collective-permute-start | bytes 344072 | tf_op jit(solution)/shard_map/ppermute | solution.py:792
  101.1 4.2 %collective-permute-done.4.ups_ref.xu_ref = f32[14,16,128]{2,1,0:T(8,128)S(1)} collective-permute-done((f32[14,16,128]{2,1,0:T(8,128)S(1)}, f32[14,16,128]{2,1,0:T(8,128)S(1)}, u32[]{:S(2)}, u32[]{:S(2)}) %collective-permute-start.4) | collective-permute-done | bytes 114720 | tf_op jit(solution)/shard_map/ppermute | solution.py:792
  105.3 0.0 collective-permute-done.5.downs_ref.xd_ref
  105.3 0.8 shard_map.103
  106.0 4.6 %collective-permute-start.7 = (f32[25,16,128]{2,1,0:T(8,128)S(1)}, f32[25,16,128]{2,1,0:T(8,128)S(1)}, u32[]{:S(2)}, u32[]{:S(2)}) collective-permute-start(f32[25,16,128]{2,1,0:T(8,128)S(1)} %get-tuple-element.51), channel_id=1, source_target_pairs={{8,0},{16,8},{24,16},{9,1},{17,9},{25,17},{10,2},{18,10},{26,18},{... | collective-permute-start | bytes 614408 | tf_op jit(solution)/shard_map/ppermute | solution.py:792
  110.6 1.9 %collective-permute-start.6 = (f32[14,16,128]{2,1,0:T(8,128)S(1)}, f32[14,16,128]{2,1,0:T(8,128)S(1)}, u32[]{:S(2)}, u32[]{:S(2)}) collective-permute-start(f32[14,16,128]{2,1,0:T(8,128)S(1)} %get-tuple-element.50), channel_id=1, source_target_pairs={{0,8},{8,16},{16,24},{1,9},{9,17},{17,25},{2,10},{10,18},{18,26},{... | collective-permute-start | bytes 344072 | tf_op jit(solution)/shard_map/ppermute | solution.py:792
  112.5 4.8 %collective-permute-done.6.yu_ref = f32[14,16,128]{2,1,0:T(8,128)S(1)} collective-permute-done((f32[14,16,128]{2,1,0:T(8,128)S(1)}, f32[14,16,128]{2,1,0:T(8,128)S(1)}, u32[]{:S(2)}, u32[]{:S(2)}) %collective-permute-start.6) | collective-permute-done | bytes 114720 | tf_op jit(solution)/shard_map/ppermute | solution.py:792
  117.3 0.0 collective-permute-done.7.yd_ref
  117.3 5.3 %shard_map.104 = (f32[3,12,8,128]{3,2,1,0:T(8,128)}, f32[6,12,8,128]{3,2,1,0:T(8,128)}) custom-call(s32[3]{0:T(128)S(1)} %pad_add_fusion.at_ref, f32[13,13,16,128]{3,2,1,0:T(8,128)S(1)} %get-tuple-element.46.main_ref, f32[13,13,16,128]{3,2,1,0:T(8,128)S(1)} %get-tuple-element.47.rim_ref, f32[14,16,128]{2,1,0:T(8,128)S(1)} %collective-permute-done.4.ups_ref.xu_ref, ...), custom_call_target="tpu_custom_call" | custom-call | tf_op jit(solution)/shard_map/pallas_call | solution.py:770
Async XLA Ops:
  38.5 7.2 %collective-permute-start = (f32[10,16,128]{2,1,0:T(8,128)S(1)}, f32[10,16,128]{2,1,0:T(8,128)S(1)}, u32[]{:S(2)}, u32[]{:S(2)}) collective-permute-start(f32[10,16,128]{2,1,0:T(8,128)S(1)} %get-tuple-element.40), channel_id=1, source_target_pairs={{0,32},{32,64},{64,96},{96,128},{128,160},{160,192},{192,224},{1,3... | collective-permute-start | bytes 245768 | tf_op jit(solution)/shard_map/ppermute | solution.py:792
  40.4 5.3 %collective-permute-start.1 = (f32[5,16,128]{2,1,0:T(8,128)S(1)}, f32[5,16,128]{2,1,0:T(8,128)S(1)}, u32[]{:S(2)}, u32[]{:S(2)}) collective-permute-start(f32[5,16,128]{2,1,0:T(8,128)S(1)} %get-tuple-element.41), channel_id=1, source_target_pairs={{32,0},{64,32},{96,64},{128,96},{160,128},{192,160},{224,192},{33,... | collective-permute-start | bytes 122888 | tf_op jit(solution)/shard_map/ppermute | solution.py:792
  45.9 11.7 %collective-permute-start.2 = (f32[10,16,128]{2,1,0:T(8,128)S(1)}, f32[10,16,128]{2,1,0:T(8,128)S(1)}, u32[]{:S(2)}, u32[]{:S(2)}) collective-permute-start(f32[10,16,128]{2,1,0:T(8,128)S(1)} %get-tuple-element.42), channel_id=1, source_target_pairs={{0,8},{8,16},{16,24},{1,9},{9,17},{17,25},{2,10},{10,18},{18,26},{... | collective-permute-start | bytes 245768 | tf_op jit(solution)/shard_map/ppermute | solution.py:792
  47.8 9.8 %collective-permute-start.3 = (f32[5,16,128]{2,1,0:T(8,128)S(1)}, f32[5,16,128]{2,1,0:T(8,128)S(1)}, u32[]{:S(2)}, u32[]{:S(2)}) collective-permute-start(f32[5,16,128]{2,1,0:T(8,128)S(1)} %get-tuple-element.43), channel_id=1, source_target_pairs={{8,0},{16,8},{24,16},{9,1},{17,9},{25,17},{10,2},{18,10},{26,18},{... | collective-permute-start | bytes 122888 | tf_op jit(solution)/shard_map/ppermute | solution.py:792
  96.0 9.2 %collective-permute-start.5 = (f32[25,16,128]{2,1,0:T(8,128)S(1)}, f32[25,16,128]{2,1,0:T(8,128)S(1)}, u32[]{:S(2)}, u32[]{:S(2)}) collective-permute-start(f32[25,16,128]{2,1,0:T(8,128)S(1)} %get-tuple-element.49), channel_id=1, source_target_pairs={{32,0},{64,32},{96,64},{128,96},{160,128},{192,160},{224,192},{33,... | collective-permute-start | bytes 614408 | tf_op jit(solution)/shard_map/ppermute | solution.py:792
  99.1 6.1 %collective-permute-start.4 = (f32[14,16,128]{2,1,0:T(8,128)S(1)}, f32[14,16,128]{2,1,0:T(8,128)S(1)}, u32[]{:S(2)}, u32[]{:S(2)}) collective-permute-start(f32[14,16,128]{2,1,0:T(8,128)S(1)} %get-tuple-element.48), channel_id=1, source_target_pairs={{0,32},{32,64},{64,96},{96,128},{128,160},{160,192},{192,224},{1,3... | collective-permute-start | bytes 344072 | tf_op jit(solution)/shard_map/ppermute | solution.py:792
  106.0 11.2 %collective-permute-start.7 = (f32[25,16,128]{2,1,0:T(8,128)S(1)}, f32[25,16,128]{2,1,0:T(8,128)S(1)}, u32[]{:S(2)}, u32[]{:S(2)}) collective-permute-start(f32[25,16,128]{2,1,0:T(8,128)S(1)} %get-tuple-element.51), channel_id=1, source_target_pairs={{8,0},{16,8},{24,16},{9,1},{17,9},{25,17},{10,2},{18,10},{26,18},{... | collective-permute-start | bytes 614408 | tf_op jit(solution)/shard_map/ppermute | solution.py:792
  110.6 6.7 %collective-permute-start.6 = (f32[14,16,128]{2,1,0:T(8,128)S(1)}, f32[14,16,128]{2,1,0:T(8,128)S(1)}, u32[]{:S(2)}, u32[]{:S(2)}) collective-permute-start(f32[14,16,128]{2,1,0:T(8,128)S(1)} %get-tuple-element.50), channel_id=1, source_target_pairs={{0,8},{8,16},{16,24},{1,9},{9,17},{17,25},{2,10},{10,18},{18,26},{... | collective-permute-start | bytes 344072 | tf_op jit(solution)/shard_map/ppermute | solution.py:792
